TPU v7x, 32 devices: a whole 2x2x4 slice. The times are simulated.
32 devices in a mesh: groups: 2 (over y), hist: 4 (over z), head: 2 (over x), rep: 2 (over core).
Axes of the slice: x: 2, y: 2, z: 4, core: 2. Of those that a mesh axis runs over, the one named last changes fastest.
Arguments:
- item_feats: bfloat16 [4096, 4096], P(('groups', 'hist', 'rep')), parts along dimension 0, may hold values from -6 to 6
- adapter: bfloat16 [4096, 512], P('hist', 'head'), may hold values from -0.09375 to 0.09375
- hist_emb: bfloat16 [8192, 512], P(('groups', 'hist')), parts along dimension 0, may hold values from -6 to 6
- key_weight: bfloat16 [512, 512], P(None, 'head'), may hold values from -0.25 to 0.25
- value_weight: bfloat16 [512, 512], P(None, 'head'), may hold values from -0.25 to 0.25
- routes: int32 [4096, 1], P(('groups', 'hist', 'rep')), parts along dimension 0, may hold values from 0 to 3; in each aligned block of 256 rows (0 to 255, 256 to 511, ...) at most 128 rows name the same one
- cand_index: int32 [1024], P(('groups', 'hist', 'rep')), parts along dimension 0, may hold values from 0 to 255
- item_user: int32 [4096], P(('groups', 'hist', 'rep')), parts along dimension 0, may hold values from 0 to 255
- hist_user: int32 [8192], P(('groups', 'hist')), parts along dimension 0, may hold values from 0 to 255
Outputs:
- scored: bfloat16 [1024, 512], P(('groups', 'hist', 'rep'), 'head'), parts along dimension 0
There are 2 independent parts, one for each index of `groups`. A program takes and returns all parts, laid end to end along the dimension named above; an argument that names none is the same for every part. Nothing has to cross between parts.
Inputs may be any that keep to these rules, and one draw needn't show every extreme that they name: `routes`: in the rows of one device no owner is named more than 128 times; some owner is named exactly 128 times.
All inputs are finite; a program needn't handle non-finite values.
Results may differ from a plain program's by a relative error of at most 0.0081.
Values may be sent and summed in bfloat16 or wider, within the bound.
No kernel may reach another device: no remote copies, remote signals or barrier semaphores. Data moves between devices by JAX's collectives and lax.ppermute only.
A program may use at most 64 MiB of HBM per device.

v0:
```python
import functools
import math

import jax
import jax.numpy as jnp
from jax import lax
from jax.experimental import pallas as pl
from jax.experimental.pallas import tpu as pltpu
from jax.sharding import PartitionSpec as P


HS = 64
USERS = 256
VM = pl.BlockSpec(memory_space=pltpu.VMEM)
HBM = pl.BlockSpec(memory_space=pltpu.HBM)
F32 = jnp.float32
BF16 = jnp.bfloat16


def attend(query_block, user_block, key_rows, value_rows, key_users):
    row_count = query_block.shape[0]
    col_count = query_block.shape[1]
    heads_here = col_count // HS
    att_scale = float(HS) ** (-0.5)
    query_three = query_block.reshape(row_count, heads_here, HS)
    key_three = key_rows.reshape(-1, heads_here, HS)
    value_three = value_rows.reshape(-1, heads_here, HS)
    scores = (
        jnp.einsum("rhd,khd->hrk", query_three, key_three, preferred_element_type=jnp.float32)
        * att_scale
    )
    matching = user_block[:, None] == key_users[None, :]
    weights = jnp.where(matching[None], jax.nn.silu(scores), 0.0).astype(jnp.bfloat16)
    mixture = jnp.einsum("hrk,khd->rhd", weights, value_three, preferred_element_type=jnp.float32)
    counted = jnp.sum(matching.astype(jnp.float32), axis=1)
    inverse = 1.0 / jnp.maximum(counted, 1.0)
    return mixture.reshape(row_count, col_count) * inverse[:, None]


def dense_partial(queries, users, key_rows, value_rows, key_users):
    total_rows = queries.shape[0]
    col_count = queries.shape[1]
    block_size = math.gcd(total_rows, 512)
    blocked_queries = queries.reshape(total_rows // block_size, block_size, col_count)
    blocked_users = users.reshape(total_rows // block_size, block_size)

    def one_block(operands):
        return attend(operands[0], operands[1], key_rows, value_rows, key_users)

    return lax.map(one_block, (blocked_queries, blocked_users)).reshape(total_rows, col_count)


def generic_body(
    item_feats,
    adapter,
    hist_emb,
    key_weight,
    value_weight,
    routes,
    cand_index,
    item_user,
    hist_user,
):
    owners = lax.axis_size("hist")
    item_count = item_feats.shape[0]
    col_count = adapter.shape[1]
    embedded = jnp.dot(
        item_feats,
        lax.all_gather(adapter, "hist", axis=0, tiled=True),
        preferred_element_type=jnp.float32,
    ).astype(jnp.bfloat16)
    capacity = 2 * item_count // owners
    owner_of = routes[:, 0]
    owner_hot = (owner_of[:, None] == jnp.arange(owners, dtype=jnp.int32)[None, :]).astype(
        jnp.int32
    )
    earlier = jnp.cumsum(owner_hot, axis=0) - owner_hot
    slot_of = jnp.sum(earlier * owner_hot, axis=1)
    position = owner_of * capacity + slot_of
    placing = (jnp.arange(owners * capacity, dtype=jnp.int32)[:, None] == position[None, :]).astype(
        jnp.bfloat16
    )
    outgoing = jnp.dot(placing, embedded, preferred_element_type=jnp.float32).astype(jnp.bfloat16)
    outgoing = outgoing.reshape(owners, capacity, col_count)
    shifted_user = (item_user + 1).astype(jnp.bfloat16)
    outgoing_user = (
        jnp.dot(placing, shifted_user, preferred_element_type=jnp.float32) - 1.0
    ).astype(jnp.bfloat16)
    outgoing_user = outgoing_user.reshape(owners, capacity)
    incoming, incoming_user = (
        lax.all_to_all(outgoing, "hist", split_axis=0, concat_axis=0, tiled=True),
        lax.all_to_all(outgoing_user, "hist", split_axis=0, concat_axis=0, tiled=True),
    )
    routed, routed_user = (
        lax.all_gather(incoming, "rep", axis=0, tiled=True),
        lax.all_gather(incoming_user, "rep", axis=0, tiled=True),
    )
    routed = routed.reshape(-1, col_count)
    routed_user = routed_user.reshape(-1)
    key_local = jnp.dot(hist_emb, key_weight, preferred_element_type=jnp.float32).astype(
        jnp.bfloat16
    )
    value_local = jnp.dot(hist_emb, value_weight, preferred_element_type=jnp.float32).astype(
        jnp.bfloat16
    )
    key_rows = jnp.concatenate([key_local, routed], axis=0)
    value_rows = jnp.concatenate([value_local, routed], axis=0)
    key_users = jnp.concatenate([hist_user.astype(jnp.bfloat16), routed_user], axis=0)
    own_queries = embedded[cand_index]
    own_users = item_user[cand_index].astype(jnp.bfloat16)
    gathered, gathered_users = (
        lax.all_gather(own_queries, "hist", axis=0, tiled=True),
        lax.all_gather(own_users, "hist", axis=0, tiled=True),
    )
    partial_value = dense_partial(gathered, gathered_users, key_rows, value_rows, key_users)
    attended = lax.psum_scatter(partial_value, "hist", scatter_dimension=0, tiled=True)
    gating = jax.nn.silu(own_queries.astype(jnp.float32))
    return (gating * attended).astype(jnp.bfloat16)


def call(kernel, outs, args, flops=0, bytes_accessed=1 << 18, vmem=16, specs=None, scratch=()):
    return pl.pallas_call(
        kernel,
        out_shape=outs,
        in_specs=specs or [VM] * len(args),
        out_specs=jax.tree.map(lambda _: VM, outs),
        scratch_shapes=scratch,
        compiler_params=pltpu.CompilerParams(vmem_limit_bytes=vmem << 20),
        cost_estimate=pl.CostEstimate(flops=flops, bytes_accessed=bytes_accessed, transcendentals=0),
    )(*args)


def shape(dims, dtype):
    return jax.ShapeDtypeStruct(dims, dtype)


def iota(dims, axis):
    return lax.broadcasted_iota(jnp.int32, dims, axis)


def dot(a, b, contract=((1,), (0,))):
    return lax.dot_general(a, b, (contract, ((), ())), preferred_element_type=F32)


def col_start(width):
    return pl.multiple_of(lax.axis_index("rep") * width, width)


def share_kernel(adapter, block, out, sems):
    rows, cols = out.shape
    row = pl.multiple_of(lax.axis_index("groups") * rows, rows)
    columns = pl.ds(col_start(cols), cols)
    copies = [
        pltpu.make_async_copy(adapter.at[pl.ds(row, rows), columns], out, sems.at[0]),
        pltpu.make_async_copy(adapter.at[:, columns], block, sems.at[1]),
    ]
    for copy in copies:
        copy.start()
    for copy in copies:
        copy.wait()


def users_kernel(mine, other, pay, hot, pick):
    items = pick.shape[1] // 2
    owners = pay.shape[0] - 8
    both_user = jnp.concatenate([mine[:, :items], other[:, :items]], axis=1)
    both_owner = jnp.concatenate([mine[:, items : 2 * items], other[:, items : 2 * items]], axis=1)
    lanes = pick.shape[0]
    half = lanes // 2
    lane = iota((1, lanes), 1)
    cand = jnp.where(
        lane < half,
        mine[:, 2 * items : 2 * items + lanes],
        pltpu.roll(jnp.broadcast_to(other[:, 2 * items : 2 * items + lanes], (8, lanes)), half, 1)[:1] + items,
    )
    hist_user = mine[:, 2 * items + lanes :]
    events = hist_user.shape[1]
    here = lax.axis_index("hist")
    item_hot = (iota((USERS, 2 * items), 0) == both_user).astype(F32).astype(BF16)
    event_hot = (iota((USERS, events), 0) == hist_user).astype(F32).astype(BF16)
    hot[:, :events] = event_hot
    hot[:, events:] = item_hot
    rows = pay.shape[0]
    owns_item = (iota((rows, 2 * items), 0) == both_owner).astype(F32).astype(BF16)
    owns_event = (iota((rows, events), 0) == here).astype(F32).astype(BF16)
    counts = dot(owns_item, item_hot, ((1,), (1,))) + dot(owns_event, event_hot, ((1,), (1,)))
    chosen = (iota((2 * items, lanes), 0) == cand).astype(F32)
    users = dot(jnp.broadcast_to(both_user, (8, 2 * items)).astype(F32).astype(BF16), chosen.astype(BF16))
    padded = jnp.concatenate([users, jnp.zeros((8, USERS - lanes), F32)], axis=1)
    pay[...] = counts
    pay[owners:, :] = padded
    pick[...] = jnp.transpose(chosen).astype(BF16)


def scale_kernel(n, items, mine, other, hot, *refs):
    pays, out = refs[:n], refs[n]
    rows = pays[0].shape[0]
    owners = rows - 8
    lanes = out.shape[1]
    hist_user = mine[:, 2 * items + lanes :]
    events = hist_user.shape[1]
    total = pays[0][...]
    for pay in pays[1:]:
        total = total + pay[...]
    high = jnp.floor(total * (1.0 / 256.0))
    low = total - 256.0 * high
    counts = 256.0 * dot(high.astype(BF16), hot[...]) + dot(low.astype(BF16), hot[...])
    both_owner = jnp.concatenate([mine[:, items : 2 * items], other[:, items : 2 * items]], axis=1)
    here = jnp.zeros((1, events), jnp.int32) + lax.axis_index("hist")
    owner = jnp.concatenate([here, both_owner], axis=1)
    count = jnp.sum(jnp.where(iota(counts.shape, 0) == owner, counts, 0.0), axis=0, keepdims=True)
    inverse = 1.0 / jnp.maximum(count, 1.0)
    user = jnp.concatenate([hist_user, mine[:, :items], other[:, :items]], axis=1).astype(F32)
    diagonal = iota((lanes, lanes), 0) == iota((lanes, lanes), 1)
    for k in range(n):
        row = pays[k][owners : owners + 1, :lanes]
        column = jnp.sum(jnp.where(diagonal, row, 0.0), axis=1, keepdims=True)
        out[k] = jnp.where(column == user, inverse, 0.0)


def project_kernel(hist_emb, key_weight, value_weight, key_t, value, emb, keys, values, sems):
    width = value.shape[1]
    columns = pl.ds(col_start(width), width)
    copies = [
        pltpu.make_async_copy(key_weight.at[:, columns], keys, sems.at[0]),
        pltpu.make_async_copy(value_weight.at[:, columns], values, sems.at[1]),
        pltpu.make_async_copy(hist_emb, emb, sems.at[2]),
    ]
    for copy in copies:
        copy.start()
    for copy in copies:
        copy.wait()
    value[...] = dot(emb[...], values[...]).astype(BF16)
    key_t[...] = jnp.transpose(dot(emb[...], keys[...]).astype(BF16))


def embed_own_kernel(mine, other, block, total):
    items = mine.shape[0]
    depth = block.shape[0]
    at = pl.ds(pl.multiple_of(lax.axis_index("hist") * depth, depth), depth)
    total[:items] = dot(mine[:, at], block[...])
    total[items:] = dot(other[:, at], block[...])


def add_blocks(n, k, mine, other, base, blocks):
    depth = blocks[0].shape[0]
    groups = len(blocks)
    source = lax.rem(lax.axis_index("hist") + n - k, n)
    top, bottom = base
    for step, block in enumerate(blocks):
        group = lax.rem(lax.axis_index("groups") + groups - step, groups)
        at = pl.ds(pl.multiple_of((source * groups + group) * depth, depth), depth)
        top = top + dot(mine[:, at], block[...])
        bottom = bottom + dot(other[:, at], block[...])
    return top, bottom


def embed_add_kernel(n, k, groups, mine, other, total, *refs):
    items = mine.shape[0]
    top, bottom = add_blocks(n, k, mine, other, (total[:items], total[items:]), refs[:groups])
    refs[groups][:items] = top
    refs[groups][items:] = bottom


def embed_last_kernel(n, k, groups, mine, other, pick, total, *refs):
    items = mine.shape[0]
    top, bottom = add_blocks(n, k, mine, other, (total[:items], total[items:]), refs[:groups])
    rows, rows_t, query = refs[groups:]
    rows[:items] = top.astype(BF16)
    rows[items:] = bottom.astype(BF16)
    query[...] = dot(pick[...], rows[...]).astype(BF16)
    rows_t[...] = jnp.transpose(rows[...])


def attend_kernel(k, query, key_t, value, rows_t, rows, scale, out):
    cands, width = query.shape
    heads = width // HS
    lane = iota((cands, width), 1) // HS
    part = query[...] * (0.5 * HS ** -0.5)
    zero = jnp.zeros_like(part)
    split = jnp.concatenate([jnp.where(lane == h, part, zero) for h in range(heads)], axis=0)
    events = key_t.shape[1]

    def weigh(keys, factor):
        half = dot(split, keys)
        gated = half + half * jnp.tanh(half)
        return (gated * jnp.concatenate([factor] * heads, axis=0)).astype(BF16)

    mixed = dot(weigh(key_t[...], scale[k, :, :events]), value[...])
    mixed = mixed + dot(weigh(rows_t[...], scale[k, :, events:]), rows[...])
    total = jnp.zeros((cands, width), F32)
    for h in range(heads):
        total = total + jnp.where(lane == h, mixed[h * cands : (h + 1) * cands], 0.0)
    out[...] = total.astype(out.dtype)


def gate_kernel(query, own, *refs):
    parts, keep, send = refs[:-2], refs[-2], refs[-1]
    total = own[...]
    for part in parts:
        total = total + part[...].astype(F32)
    gate = query[...].astype(F32)
    scored = (gate * jax.nn.sigmoid(gate) * total).astype(BF16)
    half = keep.shape[0]
    keep[...] = scored[:half]
    send[...] = scored[half:]


def join_kernel(keep, got, out):
    width = keep.shape[1]
    first = lax.axis_index("rep") == 0
    out[:, :width] = jnp.where(first, keep[...], got[...])
    out[:, width:] = jnp.where(first, got[...], keep[...])


def shift(value, axis, k):
    count = lax.axis_size(axis)
    return lax.ppermute(value, axis, [(i, (i + k) % count) for i in range(count)])


def shift_order(n):
    return sorted(range(1, n), key=lambda k: min(k, n - k))


def fast_body(
    item_feats, adapter, hist_emb, key_weight, value_weight, routes, cand_index, item_user, hist_user
):
    n, groups = lax.axis_size("hist"), lax.axis_size("groups")
    items, _ = item_feats.shape
    depth, cols = adapter.shape
    width = cols // 2
    cands = 2 * cand_index.shape[0]
    events, dim = hist_emb.shape
    order = shift_order(n)

    block, own_share = call(
        share_kernel,
        (shape((depth, width), BF16), shape((depth // groups, width), BF16)),
        (adapter,),
        specs=[HBM],
        scratch=[pltpu.SemaphoreType.DMA((2,))],
    )
    along = {k: shift(own_share, "hist", k) for k in order}
    feats_other = shift(item_feats, "rep", 1)
    mine = jnp.concatenate([item_user, routes[:, 0], cand_index, cand_index, hist_user]).reshape(1, -1)
    other = shift(mine, "rep", 1)
    keys = events + 2 * items
    pay, hot, pick = call(
        users_kernel,
        (
            shape((8 + 8 * ((n + 7) // 8), USERS), F32),
            shape((USERS, keys), BF16),
            shape((cands, 2 * items), BF16),
        ),
        (mine, other),
    )
    pays = [pay] + [shift(pay, "hist", k) for k in range(1, n)]
    key_t, value = call(
        project_kernel,
        (shape((width, events), BF16), shape((events, width), BF16)),
        (hist_emb, key_weight, value_weight),
        flops=4 * events * dim * width,
        bytes_accessed=4 << 20,
        specs=[HBM] * 3,
        scratch=[
            pltpu.VMEM((events, dim), BF16),
            pltpu.VMEM((dim, width), BF16),
            pltpu.VMEM((dim, width), BF16),
            pltpu.SemaphoreType.DMA((3,)),
        ],
    )
    total = call(
        embed_own_kernel,
        shape((2 * items, width), F32),
        (item_feats, feats_other, block),
        flops=4 * items * depth * width,
        bytes_accessed=4 << 20,
    )
    scale = call(
        functools.partial(scale_kernel, n, items),
        shape((n, cands, keys), F32),
        (mine, other, hot, *pays),
        bytes_accessed=4 << 20,
    )
    across = {k: [along[k]] + [shift(along[k], "groups", g) for g in range(1, groups)] for k in order}
    for k in order[:-1]:
        total = call(
            functools.partial(embed_add_kernel, n, k, groups),
            shape((2 * items, width), F32),
            (item_feats, feats_other, total, *across[k]),
            flops=4 * items * depth * width,
            bytes_accessed=2 << 20,
        )
    k = order[-1]
    rows, rows_t, query = call(
        functools.partial(embed_last_kernel, n, k, groups),
        (shape((2 * items, width), BF16), shape((width, 2 * items), BF16), shape((cands, width), BF16)),
        (item_feats, feats_other, pick, total, *across[k]),
        flops=4 * items * depth * width,
        bytes_accessed=2 << 20,
    )
    queries = {k: shift(query, "hist", k) for k in order}

    def attend(k, block, dtype):
        return call(
            functools.partial(attend_kernel, k),
            shape((cands, width), dtype),
            (block, key_t, value, rows_t, rows, scale),
            flops=8 * cands * keys * width,
            bytes_accessed=1 << 20,
        )

    own = attend(0, query, F32)
    parts = [shift(attend(k, queries[k], BF16), "hist", n - k) for k in order]
    keep, send = call(
        gate_kernel,
        (shape((cands // 2, width), BF16), shape((cands // 2, width), BF16)),
        (query, own, *parts),
    )
    got = shift(send, "rep", 1)
    return call(join_kernel, shape((cands // 2, cols), BF16), (keep, got))


def body(*args):
    item_feats, adapter, cand_index = args[0], args[1], args[6]
    fits = (
        lax.axis_size("rep") == 2
        and lax.axis_size("hist") > 1
        and adapter.shape[0] % (128 * lax.axis_size("groups")) == 0
        and adapter.shape[1] % 256 == 0
        and 2 * cand_index.shape[0] == 128
        and item_feats.shape[0] % 128 == 0
    )
    return fast_body(*args) if fits else generic_body(*args)


def solution(mesh):
    placed = (
        P(("groups", "hist", "rep"), None),
        P("hist", "head"),
        P(("groups", "hist"), None),
        P(None, "head"),
        P(None, "head"),
        P(("groups", "hist", "rep"), None),
        P(("groups", "hist", "rep")),
        P(("groups", "hist", "rep")),
        P(("groups", "hist")),
    )
    return jax.shard_map(
        body,
        mesh=mesh,
        in_specs=placed,
        out_specs=P(("groups", "hist", "rep"), "head"),
        check_vma=False,
    )
```

profile of v0, /device:TPU:0, one launch (start us, length us, event | category | flops | bytes accessed | tf_op | source)
XLA Modules:
  0.0 48.7 jit_solution(8630764035821917420)
XLA Ops:
  0.0 0.5 %collective-permute-start = (bf16[256,4096]{1,0:T(8,128)(2,1)}, bf16[256,4096]{1,0:T(8,128)(2,1)S(1)}, u32[]{:S(2)}, u32[]{:S(2)}) collective-permute-start(bf16[256,4096]{1,0:T(8,128)(2,1)} %mine.7), channel_id=1, source_target_pairs={{0,1},{1,0},{2,3},{3,2},{4,5},{5,4},{6,7},{7,6},{8,9},{9,8},{10,11... | collective-permute-start | bytes 6291464 | tf_op jit(solution)/shard_map/ppermute | solution.py:318
  0.5 1.0 %copy-done.3 = bf16[1024,256]{1,0:T(8,128)(2,1)S(1)} copy-done((bf16[1024,256]{1,0:T(8,128)(2,1)S(1)}, bf16[1024,256]{1,0:T(8,128)(2,1)}, u32[]{:S(2)}) %copy-start.3) | copy-done | bytes 524312
  1.5 0.1 shard_map.92
  1.6 2.6 %collective-permute-start.2 = (bf16[512,128]{1,0:T(8,128)(2,1)S(1)}, bf16[512,128]{1,0:T(8,128)(2,1)S(1)}, u32[]{:S(2)}, u32[]{:S(2)}) collective-permute-start(bf16[512,128]{1,0:T(8,128)(2,1)S(1)} %get-tuple-element.19), channel_id=1, source_target_pairs={{0,4},{4,8},{8,12},{12,0},{1,5},{5,9},{9,13},{13,1},{2,6},{6,10},{... | collective-permute-start | bytes 393224 | tf_op jit(solution)/shard_map/ppermute | solution.py:318
  4.2 2.1 %collective-permute-start.4 = (bf16[512,128]{1,0:T(8,128)(2,1)S(1)}, bf16[512,128]{1,0:T(8,128)(2,1)S(1)}, u32[]{:S(2)}, u32[]{:S(2)}) collective-permute-start(bf16[512,128]{1,0:T(8,128)(2,1)S(1)} %get-tuple-element.19), channel_id=1, source_target_pairs={{0,12},{4,0},{8,4},{12,8},{1,13},{5,1},{9,5},{13,9},{2,14},{6,2},{... | collective-permute-start | bytes 393224 | tf_op jit(solution)/shard_map/ppermute | solution.py:318
  6.3 0.9 %collective-permute-start.6 = (bf16[512,128]{1,0:T(8,128)(2,1)S(1)}, bf16[512,128]{1,0:T(8,128)(2,1)S(1)}, u32[]{:S(2)}, u32[]{:S(2)}) collective-permute-start(bf16[512,128]{1,0:T(8,128)(2,1)S(1)} %get-tuple-element.19), channel_id=1, source_target_pairs={{0,8},{4,12},{8,0},{12,4},{1,9},{5,13},{9,1},{13,5},{2,10},{6,14},... | collective-permute-start | bytes 393224 | tf_op jit(solution)/shard_map/ppermute | solution.py:318
  7.3 3.4 %collective-permute-done.2.refs_0_ = bf16[512,128]{1,0:T(8,128)(2,1)S(1)} collective-permute-done((bf16[512,128]{1,0:T(8,128)(2,1)S(1)}, bf16[512,128]{1,0:T(8,128)(2,1)S(1)}, u32[]{:S(2)}, u32[]{:S(2)}) %collective-permute-start.2) | collective-permute-done | bytes 131104 | tf_op jit(solution)/shard_map/ppermute | solution.py:318
  10.7 1.7 %collective-permute-start.3 = (bf16[512,128]{1,0:T(8,128)(2,1)S(1)}, bf16[512,128]{1,0:T(8,128)(2,1)S(1)}, u32[]{:S(2)}, u32[]{:S(2)}) collective-permute-start(bf16[512,128]{1,0:T(8,128)(2,1)S(1)} %collective-permute-done.2.refs_0_), channel_id=1, source_target_pairs={{0,16},{16,0},{1,17},{17,1},{2,18},{18,2},{3,19},{19,3},{4,20},{20... | collective-permute-start | bytes 393224 | tf_op jit(solution)/shard_map/ppermute | solution.py:318
  12.4 0.3 collective-permute-done.4.refs_0_
  12.7 1.5 %collective-permute-start.5 = (bf16[512,128]{1,0:T(8,128)(2,1)S(1)}, bf16[512,128]{1,0:T(8,128)(2,1)S(1)}, u32[]{:S(2)}, u32[]{:S(2)}) collective-permute-start(bf16[512,128]{1,0:T(8,128)(2,1)S(1)} %collective-permute-done.4.refs_0_), channel_id=1, source_target_pairs={{0,16},{16,0},{1,17},{17,1},{2,18},{18,2},{3,19},{19,3},{4,20},{20... | collective-permute-start | bytes 393224 | tf_op jit(solution)/shard_map/ppermute | solution.py:318
  14.2 4.7 %collective-permute-done.6.refs_0_ = bf16[512,128]{1,0:T(8,128)(2,1)S(1)} collective-permute-done((bf16[512,128]{1,0:T(8,128)(2,1)S(1)}, bf16[512,128]{1,0:T(8,128)(2,1)S(1)}, u32[]{:S(2)}, u32[]{:S(2)}) %collective-permute-start.6) | collective-permute-done | bytes 131104 | tf_op jit(solution)/shard_map/ppermute | solution.py:318
  18.9 1.5 %collective-permute-start.7 = (bf16[512,128]{1,0:T(8,128)(2,1)S(1)}, bf16[512,128]{1,0:T(8,128)(2,1)S(1)}, u32[]{:S(2)}, u32[]{:S(2)}) collective-permute-start(bf16[512,128]{1,0:T(8,128)(2,1)S(1)} %collective-permute-done.6.refs_0_), channel_id=1, source_target_pairs={{0,16},{16,0},{1,17},{17,1},{2,18},{18,2},{3,19},{19,3},{4,20},{20... | collective-permute-start | bytes 393224 | tf_op jit(solution)/shard_map/ppermute | solution.py:318
  20.4 0.8 %concatenate.3 = s32[1664]{0:T(1024)S(1)} concatenate(s32[256]{0:T(256)} %param.16, s32[256]{0:T(256)} %bitcast.1, s32[64]{0:T(128)} %param.15, s32[64]{0:T(128)} %param.15, s32[1024]{0:T(1024)} %param.17), dimensions={0} | concatenate | bytes 13312 | tf_op jit(solution)/shard_map/concatenate | solution.py:345
  21.2 0.0 collective-permute-start.1
  21.2 1.2 %collective-permute-done.1.other = s32[1,1664]{1,0:T(1,128)S(1)} collective-permute-done((s32[1,1664]{1,0:T(1,128)S(1)}, s32[1,1664]{1,0:T(1,128)S(1)}, u32[]{:S(2)}, u32[]{:S(2)}) %collective-permute-start.1) | collective-permute-done | bytes 6688 | tf_op jit(solution)/shard_map/ppermute | solution.py:318
  22.4 0.5 %shard_map.91 = (f32[16,256]{1,0:T(8,128)S(1)}, bf16[256,1536]{1,0:T(8,128)(2,1)S(1)}, bf16[128,512]{1,0:T(8,128)(2,1)S(1)}) custom-call(s32[1,1664]{1,0:T(1,128)S(1)} %reshape.3.mine, s32[1,1664]{1,0:T(1,128)S(1)} %collective-permute-done.1.other), custom_call_target="tpu_custom_call" | custom-call | bytes 262144 | tf_op jit(solution)/shard_map/pallas_call | solution.py:122
  22.9 0.0 collective-permute-done.other
  22.9 1.6 %copy-done = bf16[256,4096]{1,0:T(8,128)(2,1)S(1)} copy-done((bf16[256,4096]{1,0:T(8,128)(2,1)S(1)}, bf16[256,4096]{1,0:T(8,128)(2,1)}, u32[]{:S(2)}) %copy-start) | copy-done | bytes 2097176
  24.5 0.4 shard_map.93.total
  24.9 1.2 %copy-done.1 = bf16[256,4096]{1,0:T(8,128)(2,1)S(1)} copy-done((bf16[256,4096]{1,0:T(8,128)(2,1)S(1)}, bf16[256,4096]{1,0:T(8,128)(2,1)}, u32[]{:S(2)}) %copy-start.1) | copy-done | bytes 2097176
  26.1 0.4 shard_map.94.total
  26.5 0.4 shard_map.95.total
  27.0 0.0 copy-start.2
  27.0 0.0 copy-start.4
  27.0 0.0 copy-start.5
  27.0 0.6 %shard_map.96 = (bf16[512,128]{1,0:T(8,128)(2,1)S(1)}, bf16[128,512]{1,0:T(8,128)(2,1)S(1)}, bf16[128,128]{1,0:T(8,128)(2,1)S(1)}) custom-call(bf16[256,4096]{1,0:T(8,128)(2,1)S(1)} %copy-done.1, bf16[256,4096]{1,0:T(8,128)(2,1)S(1)} %collective-permute-done.other, bf16[128,512]{1,0:T(8,128)(2,1)S(1)} %get-tuple-element.17.pick, ...), custom_call_target="tpu_custom_call" | custom-call | flops 134217728 | bytes 2097152 | tf_op jit(solution)/shard_map/pallas_call | solution.py:122
  27.6 0.1 collective-permute-start.11
  27.7 1.0 %collective-permute-start.8 = (f32[16,256]{1,0:T(8,128)S(1)}, f32[16,256]{1,0:T(8,128)S(1)}, u32[]{:S(2)}, u32[]{:S(2)}) collective-permute-start(f32[16,256]{1,0:T(8,128)S(1)} %get-tuple-element.26.refs_0_), channel_id=1, source_target_pairs={{0,4},{4,8},{8,12},{12,0},{1,5},{5,9},{9,13},{13,1},{2,6},{6,10},{... | collective-permute-start | bytes 49160 | tf_op jit(solution)/shard_map/ppermute | solution.py:318
  28.7 3.4 %collective-permute-start.9 = (f32[16,256]{1,0:T(8,128)S(1)}, f32[16,256]{1,0:T(8,128)S(1)}, u32[]{:S(2)}, u32[]{:S(2)}) collective-permute-start(f32[16,256]{1,0:T(8,128)S(1)} %get-tuple-element.26.refs_0_), channel_id=1, source_target_pairs={{0,8},{4,12},{8,0},{12,4},{1,9},{5,13},{9,1},{13,5},{2,10},{6,14},... | collective-permute-start | bytes 49160 | tf_op jit(solution)/shard_map/ppermute | solution.py:318
  32.1 0.7 %collective-permute-start.10 = (f32[16,256]{1,0:T(8,128)S(1)}, f32[16,256]{1,0:T(8,128)S(1)}, u32[]{:S(2)}, u32[]{:S(2)}) collective-permute-start(f32[16,256]{1,0:T(8,128)S(1)} %get-tuple-element.26.refs_0_), channel_id=1, source_target_pairs={{0,12},{4,0},{8,4},{12,8},{1,13},{5,1},{9,5},{13,9},{2,14},{6,2},{... | collective-permute-start | bytes 49160 | tf_op jit(solution)/shard_map/ppermute | solution.py:318
  32.8 0.7 %collective-permute-start.13 = (bf16[128,128]{1,0:T(8,128)(2,1)S(1)}, bf16[128,128]{1,0:T(8,128)(2,1)S(1)}, u32[]{:S(2)}, u32[]{:S(2)}) collective-permute-start(bf16[128,128]{1,0:T(8,128)(2,1)S(1)} %get-tuple-element.20.query), channel_id=1, source_target_pairs={{0,12},{4,0},{8,4},{12,8},{1,13},{5,1},{9,5},{13,9},{2,14},{6,2},{... | collective-permute-start | bytes 98312 | tf_op jit(solution)/shard_map/ppermute | solution.py:318
  33.5 0.9 %shard_map.97 = (bf16[128,1024]{1,0:T(8,128)(2,1)S(1)}, bf16[1024,128]{1,0:T(8,128)(2,1)S(1)}) custom-call(bf16[1024,512]{1,0:T(8,128)(2,1)S(1)} %copy-done.2, bf16[512,256]{1,0:T(8,128)(2,1)S(1)} %copy-done.4, bf16[512,256]{1,0:T(8,128)(2,1)S(1)} %copy-done.5), custom_call_target="tpu_custom_call" | custom-call | flops 268435456 | bytes 4194304 | tf_op jit(solution)/shard_map/pallas_call | solution.py:122
  34.5 1.3 %collective-permute-done.10.refs_3_ = f32[16,256]{1,0:T(8,128)S(1)} collective-permute-done((f32[16,256]{1,0:T(8,128)S(1)}, f32[16,256]{1,0:T(8,128)S(1)}, u32[]{:S(2)}, u32[]{:S(2)}) %collective-permute-start.10) | collective-permute-done | bytes 16416 | tf_op jit(solution)/shard_map/ppermute | solution.py:318
  35.8 0.6 %shard_map.98.scale = f32[4,128,1536]{2,1,0:T(8,128)S(1)} custom-call(s32[1,1664]{1,0:T(1,128)S(1)} %reshape.3.mine, s32[1,1664]{1,0:T(1,128)S(1)} %collective-permute-done.1.other, bf16[256,1536]{1,0:T(8,128)(2,1)S(1)} %get-tuple-element.25.hot, f32[16,256]{1,0:T(8,128)S(1)} %get-tuple-element.26.refs_0_, f32[16,256]{1,0:T(8,128)S(1)} %collective-permute-done.8.refs_1_, ...), custom_call_target="tpu_custom_call" | custom-call | bytes 4194304 | tf_op jit(solution)/shard_map/pallas_call | solution.py:122
  36.4 1.1 %collective-permute-start.15 = (bf16[128,128]{1,0:T(8,128)(2,1)S(1)}, bf16[128,128]{1,0:T(8,128)(2,1)S(1)}, u32[]{:S(2)}, u32[]{:S(2)}) collective-permute-start(bf16[128,128]{1,0:T(8,128)(2,1)S(1)} %get-tuple-element.20.query), channel_id=1, source_target_pairs={{0,8},{4,12},{8,0},{12,4},{1,9},{5,13},{9,1},{13,5},{2,10},{6,14},... | collective-permute-start | bytes 98312 | tf_op jit(solution)/shard_map/ppermute | solution.py:318
  37.5 0.7 %shard_map.100 = bf16[128,128]{1,0:T(8,128)(2,1)S(1)} custom-call(bf16[128,128]{1,0:T(8,128)(2,1)S(1)} %collective-permute-done.11.query, bf16[128,1024]{1,0:T(8,128)(2,1)S(1)} %get-tuple-element.21.key_t, bf16[1024,128]{1,0:T(8,128)(2,1)S(1)} %get-tuple-element.22.value, bf16[128,512]{1,0:T(8,128)(2,1)S(1)} %get-tuple-element.23.rows_t, ...), custom_call_target="tpu_custom_call" | custom-call | flops 201326592 | bytes 1048576 | tf_op jit(solution)/shard_map/pallas_call | solution.py:122
  38.2 1.5 %collective-permute-start.12 = (bf16[128,128]{1,0:T(8,128)(2,1)S(1)}, bf16[128,128]{1,0:T(8,128)(2,1)S(1)}, u32[]{:S(2)}, u32[]{:S(2)}) collective-permute-start(bf16[128,128]{1,0:T(8,128)(2,1)S(1)} %shard_map.100), channel_id=1, source_target_pairs={{0,12},{4,0},{8,4},{12,8},{1,13},{5,1},{9,5},{13,9},{2,14},{6,2},{... | collective-permute-start | bytes 98312 | tf_op jit(solution)/shard_map/ppermute | solution.py:318
  39.7 0.7 %shard_map.101 = bf16[128,128]{1,0:T(8,128)(2,1)S(1)} custom-call(bf16[128,128]{1,0:T(8,128)(2,1)S(1)} %collective-permute-done.13.query, bf16[128,1024]{1,0:T(8,128)(2,1)S(1)} %get-tuple-element.21.key_t, bf16[1024,128]{1,0:T(8,128)(2,1)S(1)} %get-tuple-element.22.value, bf16[128,512]{1,0:T(8,128)(2,1)S(1)} %get-tuple-element.23.rows_t, ...), custom_call_target="tpu_custom_call" | custom-call | flops 201326592 | bytes 1048576 | tf_op jit(solution)/shard_map/pallas_call | solution.py:122
  40.4 0.6 %collective-permute-start.14 = (bf16[128,128]{1,0:T(8,128)(2,1)S(1)}, bf16[128,128]{1,0:T(8,128)(2,1)S(1)}, u32[]{:S(2)}, u32[]{:S(2)}) collective-permute-start(bf16[128,128]{1,0:T(8,128)(2,1)S(1)} %shard_map.101), channel_id=1, source_target_pairs={{0,4},{4,8},{8,12},{12,0},{1,5},{5,9},{9,13},{13,1},{2,6},{6,10},{... | collective-permute-start | bytes 98312 | tf_op jit(solution)/shard_map/ppermute | solution.py:318
  41.0 0.2 collective-permute-done.15.query
  41.3 0.7 %shard_map.102 = bf16[128,128]{1,0:T(8,128)(2,1)S(1)} custom-call(bf16[128,128]{1,0:T(8,128)(2,1)S(1)} %collective-permute-done.15.query, bf16[128,1024]{1,0:T(8,128)(2,1)S(1)} %get-tuple-element.21.key_t, bf16[1024,128]{1,0:T(8,128)(2,1)S(1)} %get-tuple-element.22.value, bf16[128,512]{1,0:T(8,128)(2,1)S(1)} %get-tuple-element.23.rows_t, ...), custom_call_target="tpu_custom_call" | custom-call | flops 201326592 | bytes 1048576 | tf_op jit(solution)/shard_map/pallas_call | solution.py:122
  41.9 1.7 %collective-permute-start.16 = (bf16[128,128]{1,0:T(8,128)(2,1)S(1)}, bf16[128,128]{1,0:T(8,128)(2,1)S(1)}, u32[]{:S(2)}, u32[]{:S(2)}) collective-permute-start(bf16[128,128]{1,0:T(8,128)(2,1)S(1)} %shard_map.102), channel_id=1, source_target_pairs={{0,8},{4,12},{8,0},{12,4},{1,9},{5,13},{9,1},{13,5},{2,10},{6,14},... | collective-permute-start | bytes 98312 | tf_op jit(solution)/shard_map/ppermute | solution.py:318
  43.6 0.7 %shard_map.99.own = f32[128,128]{1,0:T(8,128)S(1)} custom-call(bf16[128,128]{1,0:T(8,128)(2,1)S(1)} %get-tuple-element.20.query, bf16[128,1024]{1,0:T(8,128)(2,1)S(1)} %get-tuple-element.21.key_t, bf16[1024,128]{1,0:T(8,128)(2,1)S(1)} %get-tuple-element.22.value, bf16[128,512]{1,0:T(8,128)(2,1)S(1)} %get-tuple-element.23.rows_t, ...), custom_call_target="tpu_custom_call" | custom-call | flops 201326592 | bytes 1048576 | tf_op jit(solution)/shard_map/pallas_call | solution.py:122
  44.3 1.9 %collective-permute-done.14.refs_1_ = bf16[128,128]{1,0:T(8,128)(2,1)S(1)} collective-permute-done((bf16[128,128]{1,0:T(8,128)(2,1)S(1)}, bf16[128,128]{1,0:T(8,128)(2,1)S(1)}, u32[]{:S(2)}, u32[]{:S(2)}) %collective-permute-start.14) | collective-permute-done | bytes 32800 | tf_op jit(solution)/shard_map/ppermute | solution.py:318
  46.2 0.6 %collective-permute-done.16.refs_2_ = bf16[128,128]{1,0:T(8,128)(2,1)S(1)} collective-permute-done((bf16[128,128]{1,0:T(8,128)(2,1)S(1)}, bf16[128,128]{1,0:T(8,128)(2,1)S(1)}, u32[]{:S(2)}, u32[]{:S(2)}) %collective-permute-start.16) | collective-permute-done | bytes 32800 | tf_op jit(solution)/shard_map/ppermute | solution.py:318
  46.8 0.1 collective-permute-start.17
  46.9 1.2 %collective-permute-done.17.got = bf16[64,128]{1,0:T(8,128)(2,1)S(1)} collective-permute-done((bf16[64,128]{1,0:T(8,128)(2,1)S(1)}, bf16[64,128]{1,0:T(8,128)(2,1)S(1)}, u32[]{:S(2)}, u32[]{:S(2)}) %collective-permute-start.17) | collective-permute-done | bytes 16416 | tf_op jit(solution)/shard_map/ppermute | solution.py:318
  48.1 0.6 %shard_map.104 = bf16[64,256]{1,0:T(8,128)(2,1)} custom-call(bf16[64,128]{1,0:T(8,128)(2,1)S(1)} %get-tuple-element.27.keep, bf16[64,128]{1,0:T(8,128)(2,1)S(1)} %collective-permute-done.17.got), custom_call_target="tpu_custom_call" | custom-call | bytes 262144 | tf_op jit(solution)/shard_map/pallas_call | solution.py:122
  (16 shorter events, 0.1 us)
Async XLA Ops:
  0.0 22.9 %collective-permute-start = (bf16[256,4096]{1,0:T(8,128)(2,1)}, bf16[256,4096]{1,0:T(8,128)(2,1)S(1)}, u32[]{:S(2)}, u32[]{:S(2)}) collective-permute-start(bf16[256,4096]{1,0:T(8,128)(2,1)} %mine.7), channel_id=1, source_target_pairs={{0,1},{1,0},{2,3},{3,2},{4,5},{5,4},{6,7},{7,6},{8,9},{9,8},{10,11... | collective-permute-start | bytes 6291464 | tf_op jit(solution)/shard_map/ppermute | solution.py:318
  0.5 1.0 %copy-start.3 = (bf16[1024,256]{1,0:T(8,128)(2,1)S(1)}, bf16[1024,256]{1,0:T(8,128)(2,1)}, u32[]{:S(2)}) copy-start(bf16[1024,256]{1,0:T(8,128)(2,1)} %adapter.1) | copy-start | bytes 1572868
  1.6 9.0 %collective-permute-start.2 = (bf16[512,128]{1,0:T(8,128)(2,1)S(1)}, bf16[512,128]{1,0:T(8,128)(2,1)S(1)}, u32[]{:S(2)}, u32[]{:S(2)}) collective-permute-start(bf16[512,128]{1,0:T(8,128)(2,1)S(1)} %get-tuple-element.19), channel_id=1, source_target_pairs={{0,4},{4,8},{8,12},{12,0},{1,5},{5,9},{9,13},{13,1},{2,6},{6,10},{... | collective-permute-start | bytes 393224 | tf_op jit(solution)/shard_map/ppermute | solution.py:318
  4.2 8.4 %collective-permute-start.4 = (bf16[512,128]{1,0:T(8,128)(2,1)S(1)}, bf16[512,128]{1,0:T(8,128)(2,1)S(1)}, u32[]{:S(2)}, u32[]{:S(2)}) collective-permute-start(bf16[512,128]{1,0:T(8,128)(2,1)S(1)} %get-tuple-element.19), channel_id=1, source_target_pairs={{0,12},{4,0},{8,4},{12,8},{1,13},{5,1},{9,5},{13,9},{2,14},{6,2},{... | collective-permute-start | bytes 393224 | tf_op jit(solution)/shard_map/ppermute | solution.py:318
  6.3 12.5 %collective-permute-start.6 = (bf16[512,128]{1,0:T(8,128)(2,1)S(1)}, bf16[512,128]{1,0:T(8,128)(2,1)S(1)}, u32[]{:S(2)}, u32[]{:S(2)}) collective-permute-start(bf16[512,128]{1,0:T(8,128)(2,1)S(1)} %get-tuple-element.19), channel_id=1, source_target_pairs={{0,8},{4,12},{8,0},{12,4},{1,9},{5,13},{9,1},{13,5},{2,10},{6,14},... | collective-permute-start | bytes 393224 | tf_op jit(solution)/shard_map/ppermute | solution.py:318
  10.7 14.3 %collective-permute-start.3 = (bf16[512,128]{1,0:T(8,128)(2,1)S(1)}, bf16[512,128]{1,0:T(8,128)(2,1)S(1)}, u32[]{:S(2)}, u32[]{:S(2)}) collective-permute-start(bf16[512,128]{1,0:T(8,128)(2,1)S(1)} %collective-permute-done.2.refs_0_), channel_id=1, source_target_pairs={{0,16},{16,0},{1,17},{17,1},{2,18},{18,2},{3,19},{19,3},{4,20},{20... | collective-permute-start | bytes 393224 | tf_op jit(solution)/shard_map/ppermute | solution.py:318
  12.7 13.8 %collective-permute-start.5 = (bf16[512,128]{1,0:T(8,128)(2,1)S(1)}, bf16[512,128]{1,0:T(8,128)(2,1)S(1)}, u32[]{:S(2)}, u32[]{:S(2)}) collective-permute-start(bf16[512,128]{1,0:T(8,128)(2,1)S(1)} %collective-permute-done.4.refs_0_), channel_id=1, source_target_pairs={{0,16},{16,0},{1,17},{17,1},{2,18},{18,2},{3,19},{19,3},{4,20},{20... | collective-permute-start | bytes 393224 | tf_op jit(solution)/shard_map/ppermute | solution.py:318
  18.9 8.1 %collective-permute-start.7 = (bf16[512,128]{1,0:T(8,128)(2,1)S(1)}, bf16[512,128]{1,0:T(8,128)(2,1)S(1)}, u32[]{:S(2)}, u32[]{:S(2)}) collective-permute-start(bf16[512,128]{1,0:T(8,128)(2,1)S(1)} %collective-permute-done.6.refs_0_), channel_id=1, source_target_pairs={{0,16},{16,0},{1,17},{17,1},{2,18},{18,2},{3,19},{19,3},{4,20},{20... | collective-permute-start | bytes 393224 | tf_op jit(solution)/shard_map/ppermute | solution.py:318
  21.2 1.2 %collective-permute-start.1 = (s32[1,1664]{1,0:T(1,128)S(1)}, s32[1,1664]{1,0:T(1,128)S(1)}, u32[]{:S(2)}, u32[]{:S(2)}) collective-permute-start(s32[1,1664]{1,0:T(1,128)S(1)} %reshape.3.mine), channel_id=1, source_target_pairs={{0,1},{1,0},{2,3},{3,2},{4,5},{5,4},{6,7},{7,6},{8,9},{9,8},{10,11... | collective-permute-start | bytes 19976 | tf_op jit(solution)/shard_map/ppermute | solution.py:318
  22.9 1.6 %copy-start = (bf16[256,4096]{1,0:T(8,128)(2,1)S(1)}, bf16[256,4096]{1,0:T(8,128)(2,1)}, u32[]{:S(2)}) copy-start(bf16[256,4096]{1,0:T(8,128)(2,1)} %mine.7) | copy-start | bytes 6291460
  24.5 1.6 %copy-start.1 = (bf16[256,4096]{1,0:T(8,128)(2,1)S(1)}, bf16[256,4096]{1,0:T(8,128)(2,1)}, u32[]{:S(2)}) copy-start(bf16[256,4096]{1,0:T(8,128)(2,1)} %mine.7) | copy-start | bytes 6291460
  27.0 6.6 %copy-start.2 = (bf16[1024,512]{1,0:T(8,128)(2,1)S(1)}, bf16[1024,512]{1,0:T(8,128)(2,1)}, u32[]{:S(2)}) copy-start(bf16[1024,512]{1,0:T(8,128)(2,1)} %hist_emb.1) | copy-start | bytes 3145732
  27.0 6.6 %copy-start.4 = (bf16[512,256]{1,0:T(8,128)(2,1)S(1)}, bf16[512,256]{1,0:T(8,128)(2,1)}, u32[]{:S(2)}) copy-start(bf16[512,256]{1,0:T(8,128)(2,1)} %key_weight.1) | copy-start | bytes 786436
  27.0 6.6 %copy-start.5 = (bf16[512,256]{1,0:T(8,128)(2,1)S(1)}, bf16[512,256]{1,0:T(8,128)(2,1)}, u32[]{:S(2)}) copy-start(bf16[512,256]{1,0:T(8,128)(2,1)} %value_weight.1) | copy-start | bytes 786436
  27.6 9.9 %collective-permute-start.11 = (bf16[128,128]{1,0:T(8,128)(2,1)S(1)}, bf16[128,128]{1,0:T(8,128)(2,1)S(1)}, u32[]{:S(2)}, u32[]{:S(2)}) collective-permute-start(bf16[128,128]{1,0:T(8,128)(2,1)S(1)} %get-tuple-element.20.query), channel_id=1, source_target_pairs={{0,4},{4,8},{8,12},{12,0},{1,5},{5,9},{9,13},{13,1},{2,6},{6,10},{... | collective-permute-start | bytes 98312 | tf_op jit(solution)/shard_map/ppermute | solution.py:318
  27.7 6.8 %collective-permute-start.8 = (f32[16,256]{1,0:T(8,128)S(1)}, f32[16,256]{1,0:T(8,128)S(1)}, u32[]{:S(2)}, u32[]{:S(2)}) collective-permute-start(f32[16,256]{1,0:T(8,128)S(1)} %get-tuple-element.26.refs_0_), channel_id=1, source_target_pairs={{0,4},{4,8},{8,12},{12,0},{1,5},{5,9},{9,13},{13,1},{2,6},{6,10},{... | collective-permute-start | bytes 49160 | tf_op jit(solution)/shard_map/ppermute | solution.py:318
  28.7 5.8 %collective-permute-start.9 = (f32[16,256]{1,0:T(8,128)S(1)}, f32[16,256]{1,0:T(8,128)S(1)}, u32[]{:S(2)}, u32[]{:S(2)}) collective-permute-start(f32[16,256]{1,0:T(8,128)S(1)} %get-tuple-element.26.refs_0_), channel_id=1, source_target_pairs={{0,8},{4,12},{8,0},{12,4},{1,9},{5,13},{9,1},{13,5},{2,10},{6,14},... | collective-permute-start | bytes 49160 | tf_op jit(solution)/shard_map/ppermute | solution.py:318
  32.1 3.7 %collective-permute-start.10 = (f32[16,256]{1,0:T(8,128)S(1)}, f32[16,256]{1,0:T(8,128)S(1)}, u32[]{:S(2)}, u32[]{:S(2)}) collective-permute-start(f32[16,256]{1,0:T(8,128)S(1)} %get-tuple-element.26.refs_0_), channel_id=1, source_target_pairs={{0,12},{4,0},{8,4},{12,8},{1,13},{5,1},{9,5},{13,9},{2,14},{6,2},{... | collective-permute-start | bytes 49160 | tf_op jit(solution)/shard_map/ppermute | solution.py:318
  32.8 6.9 %collective-permute-start.13 = (bf16[128,128]{1,0:T(8,128)(2,1)S(1)}, bf16[128,128]{1,0:T(8,128)(2,1)S(1)}, u32[]{:S(2)}, u32[]{:S(2)}) collective-permute-start(bf16[128,128]{1,0:T(8,128)(2,1)S(1)} %get-tuple-element.20.query), channel_id=1, source_target_pairs={{0,12},{4,0},{8,4},{12,8},{1,13},{5,1},{9,5},{13,9},{2,14},{6,2},{... | collective-permute-start | bytes 98312 | tf_op jit(solution)/shard_map/ppermute | solution.py:318
  36.4 4.9 %collective-permute-start.15 = (bf16[128,128]{1,0:T(8,128)(2,1)S(1)}, bf16[128,128]{1,0:T(8,128)(2,1)S(1)}, u32[]{:S(2)}, u32[]{:S(2)}) collective-permute-start(bf16[128,128]{1,0:T(8,128)(2,1)S(1)} %get-tuple-element.20.query), channel_id=1, source_target_pairs={{0,8},{4,12},{8,0},{12,4},{1,9},{5,13},{9,1},{13,5},{2,10},{6,14},... | collective-permute-start | bytes 98312 | tf_op jit(solution)/shard_map/ppermute | solution.py:318
  38.2 6.1 %collective-permute-start.12 = (bf16[128,128]{1,0:T(8,128)(2,1)S(1)}, bf16[128,128]{1,0:T(8,128)(2,1)S(1)}, u32[]{:S(2)}, u32[]{:S(2)}) collective-permute-start(bf16[128,128]{1,0:T(8,128)(2,1)S(1)} %shard_map.100), channel_id=1, source_target_pairs={{0,12},{4,0},{8,4},{12,8},{1,13},{5,1},{9,5},{13,9},{2,14},{6,2},{... | collective-permute-start | bytes 98312 | tf_op jit(solution)/shard_map/ppermute | solution.py:318
  40.4 5.8 %collective-permute-start.14 = (bf16[128,128]{1,0:T(8,128)(2,1)S(1)}, bf16[128,128]{1,0:T(8,128)(2,1)S(1)}, u32[]{:S(2)}, u32[]{:S(2)}) collective-permute-start(bf16[128,128]{1,0:T(8,128)(2,1)S(1)} %shard_map.101), channel_id=1, source_target_pairs={{0,4},{4,8},{8,12},{12,0},{1,5},{5,9},{9,13},{13,1},{2,6},{6,10},{... | collective-permute-start | bytes 98312 | tf_op jit(solution)/shard_map/ppermute | solution.py:318
  41.9 4.9 %collective-permute-start.16 = (bf16[128,128]{1,0:T(8,128)(2,1)S(1)}, bf16[128,128]{1,0:T(8,128)(2,1)S(1)}, u32[]{:S(2)}, u32[]{:S(2)}) collective-permute-start(bf16[128,128]{1,0:T(8,128)(2,1)S(1)} %shard_map.102), channel_id=1, source_target_pairs={{0,8},{4,12},{8,0},{12,4},{1,9},{5,13},{9,1},{13,5},{2,10},{6,14},... | collective-permute-start | bytes 98312 | tf_op jit(solution)/shard_map/ppermute | solution.py:318
  46.8 1.2 %collective-permute-start.17 = (bf16[64,128]{1,0:T(8,128)(2,1)S(1)}, bf16[64,128]{1,0:T(8,128)(2,1)S(1)}, u32[]{:S(2)}, u32[]{:S(2)}) collective-permute-start(bf16[64,128]{1,0:T(8,128)(2,1)S(1)} %get-tuple-element.28), channel_id=1, source_target_pairs={{0,1},{1,0},{2,3},{3,2},{4,5},{5,4},{6,7},{7,6},{8,9},{9,8},{10,11... | collective-permute-start | bytes 49160 | tf_op jit(solution)/shard_map/ppermute | solution.py:318
where the time goes:
time: 49 us; the launch traced here: 48.7 us
  starting transfers between devices  21.9 us (45%)
  waiting for transfers between devices  14.7 us (30%)
  Pallas kernels  7.29 us (15%)
  local copies, waits for them, and re-layouts  4.64 us (9%)
    ppermute x18, starting transfers between devices, shift(): lax.ppermute(value, axis, [(i, (i + k) % count) for i in range(count)])  21.9 us
    ppermute x18, waiting for transfers between devices, shift(): lax.ppermute(value, axis, [(i, (i + k) % count) for i in range(count)])  14.7 us
    pallas_call x14, Pallas kernels, call(): pl.pallas_call(kernel, out_shape=outs, in_specs=specs or [VM] * len(args)...  7.29 us
    unnamed x12, local copies, waits for them, and re-layouts  3.81 us
  transfers between devices with their start and end apart: 18, of which 9 were waited for; matrix products, arithmetic and copies ran while one was open for 2% of the time, Pallas kernels for 12%

commit v1 on v0

--- a/solution.py
+++ b/solution.py
@@ -11,6 +11,7 @@
 
 HS = 64
 USERS = 256
+LISTED = 32
 VM = pl.BlockSpec(memory_space=pltpu.VMEM)
 HBM = pl.BlockSpec(memory_space=pltpu.HBM)
 F32 = jnp.float32
@@ -119,6 +120,8 @@
 
 
 def call(kernel, outs, args, flops=0, bytes_accessed=1 << 18, vmem=16, specs=None, scratch=()):
+    if specs:
+        args = [pltpu.with_memory_space_constraint(arg, pltpu.HBM) for arg in args]
     return pl.pallas_call(
         kernel,
         out_shape=outs,
@@ -146,62 +149,86 @@
     return pl.multiple_of(lax.axis_index("rep") * width, width)
 
 
-def share_kernel(adapter, block, out, sems):
-    rows, cols = out.shape
+def one_hot(dims, axis, at):
+    return (iota(dims, axis) == at).astype(F32).astype(BF16)
+
+
+def share_kernel(
+    adapter, item_user, routes, cand_index, hist_user, block, out, mine, user, owner, cand, event, events, sems
+):
+    _, cols = block.shape
+    rows = out.shape[0] - LISTED
     row = pl.multiple_of(lax.axis_index("groups") * rows, rows)
     columns = pl.ds(col_start(cols), cols)
+    part = event.shape[1]
     copies = [
-        pltpu.make_async_copy(adapter.at[pl.ds(row, rows), columns], out, sems.at[0]),
-        pltpu.make_async_copy(adapter.at[:, columns], block, sems.at[1]),
+        pltpu.make_async_copy(item_user, user, sems.at[0]),
+        pltpu.make_async_copy(routes, owner, sems.at[1]),
+        pltpu.make_async_copy(cand_index, cand, sems.at[2]),
+        pltpu.make_async_copy(hist_user.at[:, pl.ds(col_start(part), part)], event, sems.at[3]),
+        pltpu.make_async_copy(adapter.at[pl.ds(row, rows), columns], out.at[pl.ds(0, rows)], sems.at[4]),
+        pltpu.make_async_copy(adapter.at[:, columns], block, sems.at[5]),
+        pltpu.make_async_copy(hist_user, events, sems.at[6]),
     ]
     for copy in copies:
         copy.start()
-    for copy in copies:
+    for copy in copies[:4]:
         copy.wait()
-
-
-def users_kernel(mine, other, pay, hot, pick):
-    items = pick.shape[1] // 2
-    owners = pay.shape[0] - 8
+    items = user.shape[1]
+    cands = cand.shape[1]
+    mine[:, :items] = user[...]
+    mine[:, items : 2 * items] = owner[...]
+    mine[:, 2 * items : 2 * items + 2 * cands] = jnp.concatenate([cand[...], cand[...]], axis=1)
+    items_hot = one_hot((USERS, items), 0, user[...])
+    counts = dot(one_hot((8, items), 0, owner[...]), items_hot, ((1,), (1,)))
+    here = jnp.zeros((1, part), jnp.int32) + lax.axis_index("hist")
+    counts = counts + dot(one_hot((8, part), 0, here), one_hot((USERS, part), 0, event[...]), ((1,), (1,)))
+    chosen = one_hot((items, cands), 0, cand[...])
+    users = dot(jnp.broadcast_to(user[...], (8, items)).astype(F32).astype(BF16), chosen)
+    users = jnp.concatenate([users, jnp.zeros((8, USERS - cands), F32)], axis=1)
+    high = jnp.floor(counts * (1.0 / 256.0))
+    low = jnp.where(iota(counts.shape, 0) == 7, users, counts - 256.0 * high)
+    half = USERS // 2
+    listed = jnp.concatenate([low[:, :half], low[:, half:], high[:, :half], high[:, half:]], axis=0)
+    out[rows:] = listed.astype(BF16)
+    for copy in copies[4:]:
+        copy.wait()
+    mine[:, 2 * items + 2 * cands :] = events[...]
+
+
+def users_kernel(mine, other, hot, pick):
+    lanes, both = pick.shape
+    items = both // 2
+    half = lanes // 2
     both_user = jnp.concatenate([mine[:, :items], other[:, :items]], axis=1)
-    both_owner = jnp.concatenate([mine[:, items : 2 * items], other[:, items : 2 * items]], axis=1)
-    lanes = pick.shape[0]
-    half = lanes // 2
-    lane = iota((1, lanes), 1)
-    cand = jnp.where(
-        lane < half,
-        mine[:, 2 * items : 2 * items + lanes],
-        pltpu.roll(jnp.broadcast_to(other[:, 2 * items : 2 * items + lanes], (8, lanes)), half, 1)[:1] + items,
-    )
+    at = slice(2 * items, 2 * items + lanes)
+    moved = pltpu.roll(jnp.broadcast_to(other[:, at], (8, lanes)), half, 1)[:1] + items
+    cand = jnp.where(iota((1, lanes), 1) < half, mine[:, at], moved)
+    event_user = mine[:, 2 * items + lanes :]
+    events = event_user.shape[1]
+    hot[:, :events] = one_hot((USERS, events), 0, event_user)
+    hot[:, events:] = one_hot((USERS, both), 0, both_user)
+    chosen = (iota((both, lanes), 0) == cand).astype(F32)
+    pick[...] = jnp.transpose(chosen).astype(BF16)
+
+
+def tally_kernel(*refs):
+    out = refs[-1]
+    total = jnp.zeros((8, USERS), F32)
+    for k, ref in enumerate(refs[:-1]):
+        listed = ref[ref.shape[0] - LISTED :].astype(F32)
+        low = jnp.concatenate([listed[:8], listed[8:16]], axis=1)
+        high = jnp.concatenate([listed[16:24], listed[24:]], axis=1)
+        total = total + low + 256.0 * high
+        out[8 + k : 9 + k] = low[7:8]
+    out[:8] = total
+
+
+def scale_kernel(items, mine, other, hot, tally, tally_other, out):
+    n, lanes, _ = out.shape
     hist_user = mine[:, 2 * items + lanes :]
     events = hist_user.shape[1]
-    here = lax.axis_index("hist")
-    item_hot = (iota((USERS, 2 * items), 0) == both_user).astype(F32).astype(BF16)
-    event_hot = (iota((USERS, events), 0) == hist_user).astype(F32).astype(BF16)
-    hot[:, :events] = event_hot
-    hot[:, events:] = item_hot
-    rows = pay.shape[0]
-    owns_item = (iota((rows, 2 * items), 0) == both_owner).astype(F32).astype(BF16)
-    owns_event = (iota((rows, events), 0) == here).astype(F32).astype(BF16)
-    counts = dot(owns_item, item_hot, ((1,), (1,))) + dot(owns_event, event_hot, ((1,), (1,)))
-    chosen = (iota((2 * items, lanes), 0) == cand).astype(F32)
-    users = dot(jnp.broadcast_to(both_user, (8, 2 * items)).astype(F32).astype(BF16), chosen.astype(BF16))
-    padded = jnp.concatenate([users, jnp.zeros((8, USERS - lanes), F32)], axis=1)
-    pay[...] = counts
-    pay[owners:, :] = padded
-    pick[...] = jnp.transpose(chosen).astype(BF16)
-
-
-def scale_kernel(n, items, mine, other, hot, *refs):
-    pays, out = refs[:n], refs[n]
-    rows = pays[0].shape[0]
-    owners = rows - 8
-    lanes = out.shape[1]
-    hist_user = mine[:, 2 * items + lanes :]
-    events = hist_user.shape[1]
-    total = pays[0][...]
-    for pay in pays[1:]:
-        total = total + pay[...]
+    total = tally[:8] + tally_other[:8]
     high = jnp.floor(total * (1.0 / 256.0))
     low = total - 256.0 * high
     counts = 256.0 * dot(high.astype(BF16), hot[...]) + dot(low.astype(BF16), hot[...])
@@ -212,9 +239,12 @@
     inverse = 1.0 / jnp.maximum(count, 1.0)
     user = jnp.concatenate([hist_user, mine[:, :items], other[:, :items]], axis=1).astype(F32)
     diagonal = iota((lanes, lanes), 0) == iota((lanes, lanes), 1)
+    first = iota((8, lanes), 1) < lanes // 2
+    near = tally[8:16, :lanes]
+    far = pltpu.roll(tally_other[8:16, :lanes], lanes // 2, 1)
+    cand = jnp.where(first, near, far)
     for k in range(n):
-        row = pays[k][owners : owners + 1, :lanes]
-        column = jnp.sum(jnp.where(diagonal, row, 0.0), axis=1, keepdims=True)
+        column = jnp.sum(jnp.where(diagonal, cand[k : k + 1], 0.0), axis=1, keepdims=True)
         out[k] = jnp.where(column == user, inverse, 0.0)
 
 
@@ -243,15 +273,15 @@
 
 
 def add_blocks(n, k, mine, other, base, blocks):
-    depth = blocks[0].shape[0]
+    depth = blocks[0].shape[0] - LISTED
     groups = len(blocks)
     source = lax.rem(lax.axis_index("hist") + n - k, n)
     top, bottom = base
     for step, block in enumerate(blocks):
         group = lax.rem(lax.axis_index("groups") + groups - step, groups)
         at = pl.ds(pl.multiple_of((source * groups + group) * depth, depth), depth)
-        top = top + dot(mine[:, at], block[...])
-        bottom = bottom + dot(other[:, at], block[...])
+        top = top + dot(mine[:, at], block[:depth])
+        bottom = bottom + dot(other[:, at], block[:depth])
     return top, bottom
 
 
@@ -333,28 +363,37 @@
     events, dim = hist_emb.shape
     order = shift_order(n)
 
-    block, own_share = call(
+    block, own_share, mine = call(
         share_kernel,
-        (shape((depth, width), BF16), shape((depth // groups, width), BF16)),
-        (adapter,),
-        specs=[HBM],
-        scratch=[pltpu.SemaphoreType.DMA((2,))],
+        (
+            shape((depth, width), BF16),
+            shape((depth // groups + LISTED, width), BF16),
+            shape((1, 2 * items + cands + events), jnp.int32),
+        ),
+        (
+            adapter,
+            item_user.reshape(1, -1),
+            routes.reshape(1, -1),
+            cand_index.reshape(1, -1),
+            hist_user.reshape(1, -1),
+        ),
+        specs=[HBM] * 5,
+        scratch=[
+            pltpu.VMEM((1, items), jnp.int32),
+            pltpu.VMEM((1, items), jnp.int32),
+            pltpu.VMEM((1, cands // 2), jnp.int32),
+            pltpu.VMEM((1, events // 2), jnp.int32),
+            pltpu.VMEM((1, events), jnp.int32),
+            pltpu.SemaphoreType.DMA((7,)),
+        ],
     )
     along = {k: shift(own_share, "hist", k) for k in order}
     feats_other = shift(item_feats, "rep", 1)
-    mine = jnp.concatenate([item_user, routes[:, 0], cand_index, cand_index, hist_user]).reshape(1, -1)
     other = shift(mine, "rep", 1)
     keys = events + 2 * items
-    pay, hot, pick = call(
-        users_kernel,
-        (
-            shape((8 + 8 * ((n + 7) // 8), USERS), F32),
-            shape((USERS, keys), BF16),
-            shape((cands, 2 * items), BF16),
-        ),
-        (mine, other),
-    )
-    pays = [pay] + [shift(pay, "hist", k) for k in range(1, n)]
+    hot, pick = call(
+        users_kernel, (shape((USERS, keys), BF16), shape((cands, 2 * items), BF16)), (mine, other)
+    )
     key_t, value = call(
         project_kernel,
         (shape((width, events), BF16), shape((events, width), BF16)),
@@ -376,10 +415,13 @@
         flops=4 * items * depth * width,
         bytes_accessed=4 << 20,
     )
+    tally = call(
+        tally_kernel, shape((16, USERS), F32), (own_share, *[along[k] for k in range(1, n)])
+    )
     scale = call(
-        functools.partial(scale_kernel, n, items),
+        functools.partial(scale_kernel, items),
         shape((n, cands, keys), F32),
-        (mine, other, hot, *pays),
+        (mine, other, hot, tally, shift(tally, "rep", 1)),
         bytes_accessed=4 << 20,
     )
     across = {k: [along[k]] + [shift(along[k], "groups", g) for g in range(1, groups)] for k in order}
@@ -422,10 +464,11 @@
 
 
 def body(*args):
-    item_feats, adapter, cand_index = args[0], args[1], args[6]
+    item_feats, adapter, cand_index, hist_user = args[0], args[1], args[6], args[8]
     fits = (
         lax.axis_size("rep") == 2
-        and lax.axis_size("hist") > 1
+        and 1 < lax.axis_size("hist") < 8
+        and hist_user.shape[0] % 256 == 0
         and adapter.shape[0] % (128 * lax.axis_size("groups")) == 0
         and adapter.shape[1] % 256 == 0
         and 2 * cand_index.shape[0] == 128

time: 49 us -> 46.8 us (0.955)
  starting transfers between devices: 21.9 us -> 18.6 us
  Pallas kernels: 7.29 us -> 9.33 us
  local copies, waits for them, and re-layouts: 4.64 us -> 2.74 us
  waiting for transfers between devices: 14.7 us -> 15.7 us
    ppermute x18 -> x16, starting transfers between devices: 21.9 us -> 18.6 us  [shift(): lax.ppermute(value, axis, [(i, (i + k) % count) for i in range(count)])]
    pallas_call x14 -> x15, Pallas kernels: 7.29 us -> 9.33 us  [call(): pl.pallas_call(kernel, out_shape=outs, in_specs=specs or [VM] * len(args)...]
    unnamed x12 -> x4, local copies, waits for them, and re-layouts: 3.81 us -> 2.74 us
    ppermute x18 -> x16, waiting for transfers between devices: 14.7 us -> 15.7 us  [shift(): lax.ppermute(value, axis, [(i, (i + k) % count) for i in range(count)])]
    concatenate x1 -> x0, local copies, waits for them, and re-layouts: 0.82 us -> none  [fast_body(): jnp.concatenate([item_user, routes[:, 0], cand_index, cand_index, hist_us...]
  transfers between devices with their start and end apart: 18 -> 16, of which waited for: 9 -> 7; matrix products, arithmetic and copies ran while one was open for 2% -> 0% of each run, Pallas kernels for 12% -> 17%
where the time goes in v1:
time: 46.8 us; the launch traced here: 46.6 us
  starting transfers between devices  18.6 us (40%)
  waiting for transfers between devices  15.7 us (34%)
  Pallas kernels  9.33 us (20%)
  local copies, waits for them, and re-layouts  2.74 us (6%)
    ppermute x16, starting transfers between devices, shift(): lax.ppermute(value, axis, [(i, (i + k) % count) for i in range(count)])  18.6 us
    ppermute x16, waiting for transfers between devices, shift(): lax.ppermute(value, axis, [(i, (i + k) % count) for i in range(count)])  15.7 us
    pallas_call x15, Pallas kernels, call(): pl.pallas_call(kernel, out_shape=outs, in_specs=specs or [VM] * len(args)...  9.33 us
    unnamed x4, local copies, waits for them, and re-layouts  2.74 us
  transfers between devices with their start and end apart: 16, of which 7 were waited for; matrix products, arithmetic and copies ran while one was open for 0% of the time, Pallas kernels for 17%

profile of v1, /device:TPU:0, one launch (start us, length us, event | category | flops | bytes accessed | tf_op | source)
XLA Modules:
  0.0 46.6 jit_solution(16373660518454176593)
XLA Ops:
  0.0 0.5 %collective-permute-start = (bf16[256,4096]{1,0:T(8,128)(2,1)}, bf16[256,4096]{1,0:T(8,128)(2,1)S(1)}, u32[]{:S(2)}, u32[]{:S(2)}) collective-permute-start(bf16[256,4096]{1,0:T(8,128)(2,1)} %mine.7), channel_id=1, source_target_pairs={{0,1},{1,0},{2,3},{3,2},{4,5},{5,4},{6,7},{7,6},{8,9},{9,8},{10,11... | collective-permute-start | bytes 6291464 | tf_op jit(solution)/shard_map/ppermute | solution.py:348
  0.5 1.1 %shard_map.91 = (bf16[1024,128]{1,0:T(8,128)(2,1)S(1)}, bf16[544,128]{1,0:T(8,128)(2,1)S(1)}, s32[1,1664]{1,0:T(1,128)S(1)}) custom-call(bf16[1024,256]{1,0:T(8,128)(2,1)} %adapter.1, s32[1,256]{1,0:T(1,128)} %bitcast.5, s32[1,256]{1,0:T(1,128)} %bitcast.6, s32[1,64]{1,0:T(1,128)} %bitcast.7, s32[1,1024]{1,0:T(1,128)} %bitcast.4), custom_call_target="tpu_custom_call" | custom-call | bytes 262144 | tf_op jit(solution)/shard_map/pallas_call | solution.py:125
  1.6 2.6 %collective-permute-start.2 = (bf16[544,128]{1,0:T(8,128)(2,1)S(1)}, bf16[544,128]{1,0:T(8,128)(2,1)S(1)}, u32[]{:S(2)}, u32[]{:S(2)}) collective-permute-start(bf16[544,128]{1,0:T(8,128)(2,1)S(1)} %get-tuple-element.20.refs_0_), channel_id=1, source_target_pairs={{0,4},{4,8},{8,12},{12,0},{1,5},{5,9},{9,13},{13,1},{2,6},{6,10},{... | collective-permute-start | bytes 417800 | tf_op jit(solution)/shard_map/ppermute | solution.py:348
  4.3 2.1 %collective-permute-start.4 = (bf16[544,128]{1,0:T(8,128)(2,1)S(1)}, bf16[544,128]{1,0:T(8,128)(2,1)S(1)}, u32[]{:S(2)}, u32[]{:S(2)}) collective-permute-start(bf16[544,128]{1,0:T(8,128)(2,1)S(1)} %get-tuple-element.20.refs_0_), channel_id=1, source_target_pairs={{0,12},{4,0},{8,4},{12,8},{1,13},{5,1},{9,5},{13,9},{2,14},{6,2},{... | collective-permute-start | bytes 417800 | tf_op jit(solution)/shard_map/ppermute | solution.py:348
  6.3 0.9 %collective-permute-start.6 = (bf16[544,128]{1,0:T(8,128)(2,1)S(1)}, bf16[544,128]{1,0:T(8,128)(2,1)S(1)}, u32[]{:S(2)}, u32[]{:S(2)}) collective-permute-start(bf16[544,128]{1,0:T(8,128)(2,1)S(1)} %get-tuple-element.20.refs_0_), channel_id=1, source_target_pairs={{0,8},{4,12},{8,0},{12,4},{1,9},{5,13},{9,1},{13,5},{2,10},{6,14},... | collective-permute-start | bytes 417800 | tf_op jit(solution)/shard_map/ppermute | solution.py:348
  7.3 3.6 %collective-permute-done.2.refs_0_.refs_1_ = bf16[544,128]{1,0:T(8,128)(2,1)S(1)} collective-permute-done((bf16[544,128]{1,0:T(8,128)(2,1)S(1)}, bf16[544,128]{1,0:T(8,128)(2,1)S(1)}, u32[]{:S(2)}, u32[]{:S(2)}) %collective-permute-start.2) | collective-permute-done | bytes 139296 | tf_op jit(solution)/shard_map/ppermute | solution.py:348
  10.9 1.7 %collective-permute-start.3 = (bf16[544,128]{1,0:T(8,128)(2,1)S(1)}, bf16[544,128]{1,0:T(8,128)(2,1)S(1)}, u32[]{:S(2)}, u32[]{:S(2)}) collective-permute-start(bf16[544,128]{1,0:T(8,128)(2,1)S(1)} %collective-permute-done.2.refs_0_.refs_1_), channel_id=1, source_target_pairs={{0,16},{16,0},{1,17},{17,1},{2,18},{18,2},{3,19},{19,3},{4,20},{20... | collective-permute-start | bytes 417800 | tf_op jit(solution)/shard_map/ppermute | solution.py:348
  12.6 0.5 collective-permute-done.4.refs_0_.refs_3_
  13.0 1.5 %collective-permute-start.5 = (bf16[544,128]{1,0:T(8,128)(2,1)S(1)}, bf16[544,128]{1,0:T(8,128)(2,1)S(1)}, u32[]{:S(2)}, u32[]{:S(2)}) collective-permute-start(bf16[544,128]{1,0:T(8,128)(2,1)S(1)} %collective-permute-done.4.refs_0_.refs_3_), channel_id=1, source_target_pairs={{0,16},{16,0},{1,17},{17,1},{2,18},{18,2},{3,19},{19,3},{4,20},{20... | collective-permute-start | bytes 417800 | tf_op jit(solution)/shard_map/ppermute | solution.py:348
  14.6 5.0 %collective-permute-done.6.refs_0_.refs_2_ = bf16[544,128]{1,0:T(8,128)(2,1)S(1)} collective-permute-done((bf16[544,128]{1,0:T(8,128)(2,1)S(1)}, bf16[544,128]{1,0:T(8,128)(2,1)S(1)}, u32[]{:S(2)}, u32[]{:S(2)}) %collective-permute-start.6) | collective-permute-done | bytes 139296 | tf_op jit(solution)/shard_map/ppermute | solution.py:348
  19.6 1.5 %collective-permute-start.7 = (bf16[544,128]{1,0:T(8,128)(2,1)S(1)}, bf16[544,128]{1,0:T(8,128)(2,1)S(1)}, u32[]{:S(2)}, u32[]{:S(2)}) collective-permute-start(bf16[544,128]{1,0:T(8,128)(2,1)S(1)} %collective-permute-done.6.refs_0_.refs_2_), channel_id=1, source_target_pairs={{0,16},{16,0},{1,17},{17,1},{2,18},{18,2},{3,19},{19,3},{4,20},{20... | collective-permute-start | bytes 417800 | tf_op jit(solution)/shard_map/ppermute | solution.py:348
  21.1 0.0 collective-permute-start.1
  21.1 1.2 %collective-permute-done.1.other = s32[1,1664]{1,0:T(1,128)S(1)} collective-permute-done((s32[1,1664]{1,0:T(1,128)S(1)}, s32[1,1664]{1,0:T(1,128)S(1)}, u32[]{:S(2)}, u32[]{:S(2)}) %collective-permute-start.1) | collective-permute-done | bytes 6688 | tf_op jit(solution)/shard_map/ppermute | solution.py:348
  22.3 0.2 shard_map.92
  22.5 0.0 collective-permute-done.other
  22.5 0.0 copy-start
  22.5 1.6 %copy-done = bf16[256,4096]{1,0:T(8,128)(2,1)S(1)} copy-done((bf16[256,4096]{1,0:T(8,128)(2,1)S(1)}, bf16[256,4096]{1,0:T(8,128)(2,1)}, u32[]{:S(2)}) %copy-start) | copy-done | bytes 2097176
  24.1 0.4 shard_map.93.total
  24.5 0.0 collective-permute-done.3.refs_1_
  24.6 1.1 %copy-done.1 = bf16[256,4096]{1,0:T(8,128)(2,1)S(1)} copy-done((bf16[256,4096]{1,0:T(8,128)(2,1)S(1)}, bf16[256,4096]{1,0:T(8,128)(2,1)}, u32[]{:S(2)}) %copy-start.1) | copy-done | bytes 2097176
  25.7 0.4 shard_map.94.total
  26.1 0.0 collective-permute-done.5.refs_1_
  26.1 0.4 shard_map.95.total
  26.6 0.0 collective-permute-done.7.refs_1_
  26.6 0.6 %shard_map.96 = (bf16[512,128]{1,0:T(8,128)(2,1)S(1)}, bf16[128,512]{1,0:T(8,128)(2,1)S(1)}, bf16[128,128]{1,0:T(8,128)(2,1)S(1)}) custom-call(bf16[256,4096]{1,0:T(8,128)(2,1)S(1)} %copy-done.1, bf16[256,4096]{1,0:T(8,128)(2,1)S(1)} %collective-permute-done.other, bf16[128,512]{1,0:T(8,128)(2,1)S(1)} %get-tuple-element.18.pick, ...), custom_call_target="tpu_custom_call" | custom-call | flops 134217728 | bytes 2097152 | tf_op jit(solution)/shard_map/pallas_call | solution.py:125
  27.2 0.1 collective-permute-start.9
  27.3 0.2 collective-permute-start.8
  27.5 3.7 %collective-permute-start.11 = (bf16[128,128]{1,0:T(8,128)(2,1)S(1)}, bf16[128,128]{1,0:T(8,128)(2,1)S(1)}, u32[]{:S(2)}, u32[]{:S(2)}) collective-permute-start(bf16[128,128]{1,0:T(8,128)(2,1)S(1)} %get-tuple-element.21.query), channel_id=1, source_target_pairs={{0,12},{4,0},{8,4},{12,8},{1,13},{5,1},{9,5},{13,9},{2,14},{6,2},{... | collective-permute-start | bytes 98312 | tf_op jit(solution)/shard_map/ppermute | solution.py:348
  31.2 2.1 %shard_map.97 = (bf16[128,1024]{1,0:T(8,128)(2,1)S(1)}, bf16[1024,128]{1,0:T(8,128)(2,1)S(1)}) custom-call(bf16[1024,512]{1,0:T(8,128)(2,1)} %hist_emb.1, bf16[512,256]{1,0:T(8,128)(2,1)} %key_weight.1, bf16[512,256]{1,0:T(8,128)(2,1)} %value_weight.1), custom_call_target="tpu_custom_call" | custom-call | flops 268435456 | bytes 4194304 | tf_op jit(solution)/shard_map/pallas_call | solution.py:125
  33.4 0.0 collective-permute-done.8.tally_other
  33.4 0.6 %shard_map.99.scale = f32[4,128,1536]{2,1,0:T(8,128)S(1)} custom-call(s32[1,1664]{1,0:T(1,128)S(1)} %get-tuple-element.17.mine, s32[1,1664]{1,0:T(1,128)S(1)} %collective-permute-done.1.other, bf16[256,1536]{1,0:T(8,128)(2,1)S(1)} %get-tuple-element.26.hot, f32[16,256]{1,0:T(8,128)S(1)} %shard_map.98.tally, f32[16,256]{1,0:T(8,128)S(1)} %collective-permute-done.8.tally_other), custom_call_target="tpu_custom_call" | custom-call | bytes 4194304 | tf_op jit(solution)/shard_map/pallas_call | solution.py:125
  34.0 0.1 collective-permute-start.13
  34.0 0.0 collective-permute-done.9.query
  34.0 0.7 %shard_map.101 = bf16[128,128]{1,0:T(8,128)(2,1)S(1)} custom-call(bf16[128,128]{1,0:T(8,128)(2,1)S(1)} %collective-permute-done.9.query, bf16[128,1024]{1,0:T(8,128)(2,1)S(1)} %get-tuple-element.22.key_t, bf16[1024,128]{1,0:T(8,128)(2,1)S(1)} %get-tuple-element.23.value, bf16[128,512]{1,0:T(8,128)(2,1)S(1)} %get-tuple-element.24.rows_t, ...), custom_call_target="tpu_custom_call" | custom-call | flops 201326592 | bytes 1048576 | tf_op jit(solution)/shard_map/pallas_call | solution.py:125
  34.7 0.7 %collective-permute-start.10 = (bf16[128,128]{1,0:T(8,128)(2,1)S(1)}, bf16[128,128]{1,0:T(8,128)(2,1)S(1)}, u32[]{:S(2)}, u32[]{:S(2)}) collective-permute-start(bf16[128,128]{1,0:T(8,128)(2,1)S(1)} %shard_map.101), channel_id=1, source_target_pairs={{0,12},{4,0},{8,4},{12,8},{1,13},{5,1},{9,5},{13,9},{2,14},{6,2},{... | collective-permute-start | bytes 98312 | tf_op jit(solution)/shard_map/ppermute | solution.py:348
  35.4 0.0 collective-permute-done.11.query
  35.4 0.7 %shard_map.102 = bf16[128,128]{1,0:T(8,128)(2,1)S(1)} custom-call(bf16[128,128]{1,0:T(8,128)(2,1)S(1)} %collective-permute-done.11.query, bf16[128,1024]{1,0:T(8,128)(2,1)S(1)} %get-tuple-element.22.key_t, bf16[1024,128]{1,0:T(8,128)(2,1)S(1)} %get-tuple-element.23.value, bf16[128,512]{1,0:T(8,128)(2,1)S(1)} %get-tuple-element.24.rows_t, ...), custom_call_target="tpu_custom_call" | custom-call | flops 201326592 | bytes 1048576 | tf_op jit(solution)/shard_map/pallas_call | solution.py:125
  36.1 1.4 %collective-permute-start.12 = (bf16[128,128]{1,0:T(8,128)(2,1)S(1)}, bf16[128,128]{1,0:T(8,128)(2,1)S(1)}, u32[]{:S(2)}, u32[]{:S(2)}) collective-permute-start(bf16[128,128]{1,0:T(8,128)(2,1)S(1)} %shard_map.102), channel_id=1, source_target_pairs={{0,4},{4,8},{8,12},{12,0},{1,5},{5,9},{9,13},{13,1},{2,6},{6,10},{... | collective-permute-start | bytes 98312 | tf_op jit(solution)/shard_map/ppermute | solution.py:348
  37.5 1.6 %collective-permute-done.13.query = bf16[128,128]{1,0:T(8,128)(2,1)S(1)} collective-permute-done((bf16[128,128]{1,0:T(8,128)(2,1)S(1)}, bf16[128,128]{1,0:T(8,128)(2,1)S(1)}, u32[]{:S(2)}, u32[]{:S(2)}) %collective-permute-start.13) | collective-permute-done | bytes 32800 | tf_op jit(solution)/shard_map/ppermute | solution.py:348
  39.1 0.7 %shard_map.103 = bf16[128,128]{1,0:T(8,128)(2,1)S(1)} custom-call(bf16[128,128]{1,0:T(8,128)(2,1)S(1)} %collective-permute-done.13.query, bf16[128,1024]{1,0:T(8,128)(2,1)S(1)} %get-tuple-element.22.key_t, bf16[1024,128]{1,0:T(8,128)(2,1)S(1)} %get-tuple-element.23.value, bf16[128,512]{1,0:T(8,128)(2,1)S(1)} %get-tuple-element.24.rows_t, ...), custom_call_target="tpu_custom_call" | custom-call | flops 201326592 | bytes 1048576 | tf_op jit(solution)/shard_map/pallas_call | solution.py:125
  39.8 1.4 %collective-permute-start.14 = (bf16[128,128]{1,0:T(8,128)(2,1)S(1)}, bf16[128,128]{1,0:T(8,128)(2,1)S(1)}, u32[]{:S(2)}, u32[]{:S(2)}) collective-permute-start(bf16[128,128]{1,0:T(8,128)(2,1)S(1)} %shard_map.103), channel_id=1, source_target_pairs={{0,8},{4,12},{8,0},{12,4},{1,9},{5,13},{9,1},{13,5},{2,10},{6,14},... | collective-permute-start | bytes 98312 | tf_op jit(solution)/shard_map/ppermute | solution.py:348
  41.2 0.7 %shard_map.100.own = f32[128,128]{1,0:T(8,128)S(1)} custom-call(bf16[128,128]{1,0:T(8,128)(2,1)S(1)} %get-tuple-element.21.query, bf16[128,1024]{1,0:T(8,128)(2,1)S(1)} %get-tuple-element.22.key_t, bf16[1024,128]{1,0:T(8,128)(2,1)S(1)} %get-tuple-element.23.value, bf16[128,512]{1,0:T(8,128)(2,1)S(1)} %get-tuple-element.24.rows_t, ...), custom_call_target="tpu_custom_call" | custom-call | flops 201326592 | bytes 1048576 | tf_op jit(solution)/shard_map/pallas_call | solution.py:125
  41.9 0.0 collective-permute-done.10.refs_0_
  41.9 0.0 collective-permute-done.12.refs_1_
  41.9 2.8 %collective-permute-done.14.refs_2_ = bf16[128,128]{1,0:T(8,128)(2,1)S(1)} collective-permute-done((bf16[128,128]{1,0:T(8,128)(2,1)S(1)}, bf16[128,128]{1,0:T(8,128)(2,1)S(1)}, u32[]{:S(2)}, u32[]{:S(2)}) %collective-permute-start.14) | collective-permute-done | bytes 32800 | tf_op jit(solution)/shard_map/ppermute | solution.py:348
  44.7 0.1 collective-permute-start.15
  44.8 1.2 %collective-permute-done.15.got = bf16[64,128]{1,0:T(8,128)(2,1)S(1)} collective-permute-done((bf16[64,128]{1,0:T(8,128)(2,1)S(1)}, bf16[64,128]{1,0:T(8,128)(2,1)S(1)}, u32[]{:S(2)}, u32[]{:S(2)}) %collective-permute-start.15) | collective-permute-done | bytes 16416 | tf_op jit(solution)/shard_map/ppermute | solution.py:348
  46.0 0.6 %shard_map.105 = bf16[64,256]{1,0:T(8,128)(2,1)} custom-call(bf16[64,128]{1,0:T(8,128)(2,1)S(1)} %get-tuple-element.27.keep, bf16[64,128]{1,0:T(8,128)(2,1)S(1)} %collective-permute-done.15.got), custom_call_target="tpu_custom_call" | custom-call | bytes 262144 | tf_op jit(solution)/shard_map/pallas_call | solution.py:125
  (3 shorter events, 0.0 us)
Async XLA Ops:
  0.0 22.5 %collective-permute-start = (bf16[256,4096]{1,0:T(8,128)(2,1)}, bf16[256,4096]{1,0:T(8,128)(2,1)S(1)}, u32[]{:S(2)}, u32[]{:S(2)}) collective-permute-start(bf16[256,4096]{1,0:T(8,128)(2,1)} %mine.7), channel_id=1, source_target_pairs={{0,1},{1,0},{2,3},{3,2},{4,5},{5,4},{6,7},{7,6},{8,9},{9,8},{10,11... | collective-permute-start | bytes 6291464 | tf_op jit(solution)/shard_map/ppermute | solution.py:348
  1.6 9.2 %collective-permute-start.2 = (bf16[544,128]{1,0:T(8,128)(2,1)S(1)}, bf16[544,128]{1,0:T(8,128)(2,1)S(1)}, u32[]{:S(2)}, u32[]{:S(2)}) collective-permute-start(bf16[544,128]{1,0:T(8,128)(2,1)S(1)} %get-tuple-element.20.refs_0_), channel_id=1, source_target_pairs={{0,4},{4,8},{8,12},{12,0},{1,5},{5,9},{9,13},{13,1},{2,6},{6,10},{... | collective-permute-start | bytes 417800 | tf_op jit(solution)/shard_map/ppermute | solution.py:348
  4.3 8.8 %collective-permute-start.4 = (bf16[544,128]{1,0:T(8,128)(2,1)S(1)}, bf16[544,128]{1,0:T(8,128)(2,1)S(1)}, u32[]{:S(2)}, u32[]{:S(2)}) collective-permute-start(bf16[544,128]{1,0:T(8,128)(2,1)S(1)} %get-tuple-element.20.refs_0_), channel_id=1, source_target_pairs={{0,12},{4,0},{8,4},{12,8},{1,13},{5,1},{9,5},{13,9},{2,14},{6,2},{... | collective-permute-start | bytes 417800 | tf_op jit(solution)/shard_map/ppermute | solution.py:348
  6.3 13.2 %collective-permute-start.6 = (bf16[544,128]{1,0:T(8,128)(2,1)S(1)}, bf16[544,128]{1,0:T(8,128)(2,1)S(1)}, u32[]{:S(2)}, u32[]{:S(2)}) collective-permute-start(bf16[544,128]{1,0:T(8,128)(2,1)S(1)} %get-tuple-element.20.refs_0_), channel_id=1, source_target_pairs={{0,8},{4,12},{8,0},{12,4},{1,9},{5,13},{9,1},{13,5},{2,10},{6,14},... | collective-permute-start | bytes 417800 | tf_op jit(solution)/shard_map/ppermute | solution.py:348
  10.9 13.7 %collective-permute-start.3 = (bf16[544,128]{1,0:T(8,128)(2,1)S(1)}, bf16[544,128]{1,0:T(8,128)(2,1)S(1)}, u32[]{:S(2)}, u32[]{:S(2)}) collective-permute-start(bf16[544,128]{1,0:T(8,128)(2,1)S(1)} %collective-permute-done.2.refs_0_.refs_1_), channel_id=1, source_target_pairs={{0,16},{16,0},{1,17},{17,1},{2,18},{18,2},{3,19},{19,3},{4,20},{20... | collective-permute-start | bytes 417800 | tf_op jit(solution)/shard_map/ppermute | solution.py:348
  13.0 13.1 %collective-permute-start.5 = (bf16[544,128]{1,0:T(8,128)(2,1)S(1)}, bf16[544,128]{1,0:T(8,128)(2,1)S(1)}, u32[]{:S(2)}, u32[]{:S(2)}) collective-permute-start(bf16[544,128]{1,0:T(8,128)(2,1)S(1)} %collective-permute-done.4.refs_0_.refs_3_), channel_id=1, source_target_pairs={{0,16},{16,0},{1,17},{17,1},{2,18},{18,2},{3,19},{19,3},{4,20},{20... | collective-permute-start | bytes 417800 | tf_op jit(solution)/shard_map/ppermute | solution.py:348
  19.6 7.0 %collective-permute-start.7 = (bf16[544,128]{1,0:T(8,128)(2,1)S(1)}, bf16[544,128]{1,0:T(8,128)(2,1)S(1)}, u32[]{:S(2)}, u32[]{:S(2)}) collective-permute-start(bf16[544,128]{1,0:T(8,128)(2,1)S(1)} %collective-permute-done.6.refs_0_.refs_2_), channel_id=1, source_target_pairs={{0,16},{16,0},{1,17},{17,1},{2,18},{18,2},{3,19},{19,3},{4,20},{20... | collective-permute-start | bytes 417800 | tf_op jit(solution)/shard_map/ppermute | solution.py:348
  21.1 1.2 %collective-permute-start.1 = (s32[1,1664]{1,0:T(1,128)S(1)}, s32[1,1664]{1,0:T(1,128)S(1)}, u32[]{:S(2)}, u32[]{:S(2)}) collective-permute-start(s32[1,1664]{1,0:T(1,128)S(1)} %get-tuple-element.17.mine), channel_id=1, source_target_pairs={{0,1},{1,0},{2,3},{3,2},{4,5},{5,4},{6,7},{7,6},{8,9},{9,8},{10,11... | collective-permute-start | bytes 19976 | tf_op jit(solution)/shard_map/ppermute | solution.py:348
  22.5 1.6 %copy-start = (bf16[256,4096]{1,0:T(8,128)(2,1)S(1)}, bf16[256,4096]{1,0:T(8,128)(2,1)}, u32[]{:S(2)}) copy-start(bf16[256,4096]{1,0:T(8,128)(2,1)} %mine.7) | copy-start | bytes 6291460
  24.1 1.6 %copy-start.1 = (bf16[256,4096]{1,0:T(8,128)(2,1)S(1)}, bf16[256,4096]{1,0:T(8,128)(2,1)}, u32[]{:S(2)}) copy-start(bf16[256,4096]{1,0:T(8,128)(2,1)} %mine.7) | copy-start | bytes 6291460
  27.2 6.8 %collective-permute-start.9 = (bf16[128,128]{1,0:T(8,128)(2,1)S(1)}, bf16[128,128]{1,0:T(8,128)(2,1)S(1)}, u32[]{:S(2)}, u32[]{:S(2)}) collective-permute-start(bf16[128,128]{1,0:T(8,128)(2,1)S(1)} %get-tuple-element.21.query), channel_id=1, source_target_pairs={{0,4},{4,8},{8,12},{12,0},{1,5},{5,9},{9,13},{13,1},{2,6},{6,10},{... | collective-permute-start | bytes 98312 | tf_op jit(solution)/shard_map/ppermute | solution.py:348
  27.3 6.1 %collective-permute-start.8 = (f32[16,256]{1,0:T(8,128)S(1)}, f32[16,256]{1,0:T(8,128)S(1)}, u32[]{:S(2)}, u32[]{:S(2)}) collective-permute-start(f32[16,256]{1,0:T(8,128)S(1)} %shard_map.98.tally), channel_id=1, source_target_pairs={{0,1},{1,0},{2,3},{3,2},{4,5},{5,4},{6,7},{7,6},{8,9},{9,8},{10,11... | collective-permute-start | bytes 49160 | tf_op jit(solution)/shard_map/ppermute | solution.py:348
  27.5 7.9 %collective-permute-start.11 = (bf16[128,128]{1,0:T(8,128)(2,1)S(1)}, bf16[128,128]{1,0:T(8,128)(2,1)S(1)}, u32[]{:S(2)}, u32[]{:S(2)}) collective-permute-start(bf16[128,128]{1,0:T(8,128)(2,1)S(1)} %get-tuple-element.21.query), channel_id=1, source_target_pairs={{0,12},{4,0},{8,4},{12,8},{1,13},{5,1},{9,5},{13,9},{2,14},{6,2},{... | collective-permute-start | bytes 98312 | tf_op jit(solution)/shard_map/ppermute | solution.py:348
  34.0 5.2 %collective-permute-start.13 = (bf16[128,128]{1,0:T(8,128)(2,1)S(1)}, bf16[128,128]{1,0:T(8,128)(2,1)S(1)}, u32[]{:S(2)}, u32[]{:S(2)}) collective-permute-start(bf16[128,128]{1,0:T(8,128)(2,1)S(1)} %get-tuple-element.21.query), channel_id=1, source_target_pairs={{0,8},{4,12},{8,0},{12,4},{1,9},{5,13},{9,1},{13,5},{2,10},{6,14},... | collective-permute-start | bytes 98312 | tf_op jit(solution)/shard_map/ppermute | solution.py:348
  34.7 7.2 %collective-permute-start.10 = (bf16[128,128]{1,0:T(8,128)(2,1)S(1)}, bf16[128,128]{1,0:T(8,128)(2,1)S(1)}, u32[]{:S(2)}, u32[]{:S(2)}) collective-permute-start(bf16[128,128]{1,0:T(8,128)(2,1)S(1)} %shard_map.101), channel_id=1, source_target_pairs={{0,12},{4,0},{8,4},{12,8},{1,13},{5,1},{9,5},{13,9},{2,14},{6,2},{... | collective-permute-start | bytes 98312 | tf_op jit(solution)/shard_map/ppermute | solution.py:348
  36.1 5.8 %collective-permute-start.12 = (bf16[128,128]{1,0:T(8,128)(2,1)S(1)}, bf16[128,128]{1,0:T(8,128)(2,1)S(1)}, u32[]{:S(2)}, u32[]{:S(2)}) collective-permute-start(bf16[128,128]{1,0:T(8,128)(2,1)S(1)} %shard_map.102), channel_id=1, source_target_pairs={{0,4},{4,8},{8,12},{12,0},{1,5},{5,9},{9,13},{13,1},{2,6},{6,10},{... | collective-permute-start | bytes 98312 | tf_op jit(solution)/shard_map/ppermute | solution.py:348
  39.8 4.9 %collective-permute-start.14 = (bf16[128,128]{1,0:T(8,128)(2,1)S(1)}, bf16[128,128]{1,0:T(8,128)(2,1)S(1)}, u32[]{:S(2)}, u32[]{:S(2)}) collective-permute-start(bf16[128,128]{1,0:T(8,128)(2,1)S(1)} %shard_map.103), channel_id=1, source_target_pairs={{0,8},{4,12},{8,0},{12,4},{1,9},{5,13},{9,1},{13,5},{2,10},{6,14},... | collective-permute-start | bytes 98312 | tf_op jit(solution)/shard_map/ppermute | solution.py:348
  44.7 1.2 %collective-permute-start.15 = (bf16[64,128]{1,0:T(8,128)(2,1)S(1)}, bf16[64,128]{1,0:T(8,128)(2,1)S(1)}, u32[]{:S(2)}, u32[]{:S(2)}) collective-permute-start(bf16[64,128]{1,0:T(8,128)(2,1)S(1)} %get-tuple-element.28), channel_id=1, source_target_pairs={{0,1},{1,0},{2,3},{3,2},{4,5},{5,4},{6,7},{7,6},{8,9},{9,8},{10,11... | collective-permute-start | bytes 49160 | tf_op jit(solution)/shard_map/ppermute | solution.py:348

commit v2 on v1

--- a/solution.py
+++ b/solution.py
@@ -272,30 +272,29 @@
     total[items:] = dot(other[:, at], block[...])
 
 
-def add_blocks(n, k, mine, other, base, blocks):
-    depth = blocks[0].shape[0] - LISTED
-    groups = len(blocks)
+def add_block(n, groups, k, step, mine, other, top, bottom, block):
+    depth = block.shape[0] - LISTED
     source = lax.rem(lax.axis_index("hist") + n - k, n)
-    top, bottom = base
-    for step, block in enumerate(blocks):
-        group = lax.rem(lax.axis_index("groups") + groups - step, groups)
-        at = pl.ds(pl.multiple_of((source * groups + group) * depth, depth), depth)
-        top = top + dot(mine[:, at], block[:depth])
-        bottom = bottom + dot(other[:, at], block[:depth])
-    return top, bottom
-
-
-def embed_add_kernel(n, k, groups, mine, other, total, *refs):
+    group = lax.rem(lax.axis_index("groups") + groups - step, groups)
+    at = pl.ds(pl.multiple_of((source * groups + group) * depth, depth), depth)
+    return top + dot(mine[:, at], block[:depth]), bottom + dot(other[:, at], block[:depth])
+
+
+def embed_add_kernel(n, groups, which, mine, other, total, *refs):
     items = mine.shape[0]
-    top, bottom = add_blocks(n, k, mine, other, (total[:items], total[items:]), refs[:groups])
-    refs[groups][:items] = top
-    refs[groups][items:] = bottom
-
-
-def embed_last_kernel(n, k, groups, mine, other, pick, total, *refs):
+    top, bottom = total[:items], total[items:]
+    for (k, step), block in zip(which, refs):
+        top, bottom = add_block(n, groups, k, step, mine, other, top, bottom, block)
+    refs[-1][:items] = top
+    refs[-1][items:] = bottom
+
+
+def embed_last_kernel(n, groups, which, mine, other, pick, total, *refs):
     items = mine.shape[0]
-    top, bottom = add_blocks(n, k, mine, other, (total[:items], total[items:]), refs[:groups])
-    rows, rows_t, query = refs[groups:]
+    top, bottom = total[:items], total[items:]
+    for (k, step), block in zip(which, refs):
+        top, bottom = add_block(n, groups, k, step, mine, other, top, bottom, block)
+    rows, rows_t, query = refs[len(which) :]
     rows[:items] = top.astype(BF16)
     rows[items:] = bottom.astype(BF16)
     query[...] = dot(pick[...], rows[...]).astype(BF16)
@@ -387,13 +386,17 @@
             pltpu.SemaphoreType.DMA((7,)),
         ],
     )
-    along = {k: shift(own_share, "hist", k) for k in order}
+    along = {}
+    for k in order:
+        if k in (1, n - 1):
+            along[k] = shift(own_share, "hist", k)
+        else:
+            step = 1 if k <= n // 2 else n - 1
+            along[k] = shift(along[(k - step) % n], "hist", step)
     feats_other = shift(item_feats, "rep", 1)
     other = shift(mine, "rep", 1)
     keys = events + 2 * items
-    hot, pick = call(
-        users_kernel, (shape((USERS, keys), BF16), shape((cands, 2 * items), BF16)), (mine, other)
-    )
+    hot, pick = call(users_kernel, (shape((USERS, keys), BF16), shape((cands, 2 * items), BF16)), (mine, other))
     key_t, value = call(
         project_kernel,
         (shape((width, events), BF16), shape((events, width), BF16)),
@@ -415,9 +418,7 @@
         flops=4 * items * depth * width,
         bytes_accessed=4 << 20,
     )
-    tally = call(
-        tally_kernel, shape((16, USERS), F32), (own_share, *[along[k] for k in range(1, n)])
-    )
+    tally = call(tally_kernel, shape((16, USERS), F32), (own_share, *[along[k] for k in range(1, n)]))
     scale = call(
         functools.partial(scale_kernel, items),
         shape((n, cands, keys), F32),
@@ -425,19 +426,23 @@
         bytes_accessed=4 << 20,
     )
     across = {k: [along[k]] + [shift(along[k], "groups", g) for g in range(1, groups)] for k in order}
-    for k in order[:-1]:
+    blocks = [((k, step), across[k][step]) for k in order for step in range(groups)]
+    chunks = [blocks[at : at + groups] for at in range(0, len(blocks) - groups, groups)]
+    chunks += [blocks[-groups:-1]]
+    for k, chunk in zip(order, chunks):
+        which, arrived = zip(*chunk)
         total = call(
-            functools.partial(embed_add_kernel, n, k, groups),
+            functools.partial(embed_add_kernel, n, groups, which),
             shape((2 * items, width), F32),
-            (item_feats, feats_other, total, *across[k]),
+            (item_feats, feats_other, total, *arrived),
             flops=4 * items * depth * width,
             bytes_accessed=2 << 20,
         )
-    k = order[-1]
+    which, arrived = zip(*blocks[-1:])
     rows, rows_t, query = call(
-        functools.partial(embed_last_kernel, n, k, groups),
+        functools.partial(embed_last_kernel, n, groups, which),
         (shape((2 * items, width), BF16), shape((width, 2 * items), BF16), shape((cands, width), BF16)),
-        (item_feats, feats_other, pick, total, *across[k]),
+        (item_feats, feats_other, pick, total, *arrived),
         flops=4 * items * depth * width,
         bytes_accessed=2 << 20,
     )
@@ -455,9 +460,7 @@
     own = attend(0, query, F32)
     parts = [shift(attend(k, queries[k], BF16), "hist", n - k) for k in order]
     keep, send = call(
-        gate_kernel,
-        (shape((cands // 2, width), BF16), shape((cands // 2, width), BF16)),
-        (query, own, *parts),
+        gate_kernel, (shape((cands // 2, width), BF16), shape((cands // 2, width), BF16)), (query, own, *parts)
     )
     got = shift(send, "rep", 1)
     return call(join_kernel, shape((cands // 2, cols), BF16), (keep, got))

time: 46.8 us -> 45.9 us (0.981)
  starting transfers between devices: 18.6 us -> 17.6 us
    ppermute x16, starting transfers between devices: 18.6 us -> 17.6 us  [shift(): lax.ppermute(value, axis, [(i, (i + k) % count) for i in range(count)])]
    pallas_call x15 -> x16, Pallas kernels: 9.33 us -> 9.47 us  [call(): pl.pallas_call(kernel, out_shape=outs, in_specs=specs or [VM] * len(args)...]
  transfers between devices with their start and end apart: 16 -> 16, of which waited for: 7 -> 7; matrix products, arithmetic and copies ran while one was open for 0% -> 0% of each run, Pallas kernels for 17% -> 18%
where the time goes in v2:
time: 45.9 us; the launch traced here: 45.7 us
  starting transfers between devices  17.6 us (38%)
  waiting for transfers between devices  15.6 us (34%)
  Pallas kernels  9.47 us (21%)
  local copies, waits for them, and re-layouts  2.74 us (6%)
    ppermute x16, starting transfers between devices, shift(): lax.ppermute(value, axis, [(i, (i + k) % count) for i in range(count)])  17.6 us
    ppermute x16, waiting for transfers between devices, shift(): lax.ppermute(value, axis, [(i, (i + k) % count) for i in range(count)])  15.6 us
    pallas_call x16, Pallas kernels, call(): pl.pallas_call(kernel, out_shape=outs, in_specs=specs or [VM] * len(args)...  9.47 us
    unnamed x4, local copies, waits for them, and re-layouts  2.74 us
  transfers between devices with their start and end apart: 16, of which 7 were waited for; matrix products, arithmetic and copies ran while one was open for 0% of the time, Pallas kernels for 18%

profile of v2, /device:TPU:0, one launch (start us, length us, event | category | flops | bytes accessed | tf_op | source)
XLA Modules:
  0.0 45.7 jit_solution(1039439600608751944)
XLA Ops:
  0.0 0.5 %collective-permute-start = (bf16[256,4096]{1,0:T(8,128)(2,1)}, bf16[256,4096]{1,0:T(8,128)(2,1)S(1)}, u32[]{:S(2)}, u32[]{:S(2)}) collective-permute-start(bf16[256,4096]{1,0:T(8,128)(2,1)} %mine.9), channel_id=1, source_target_pairs={{0,1},{1,0},{2,3},{3,2},{4,5},{5,4},{6,7},{7,6},{8,9},{9,8},{10,11... | collective-permute-start | bytes 6291464 | tf_op jit(solution)/shard_map/ppermute | solution.py:347
  0.5 1.1 %shard_map.91 = (bf16[1024,128]{1,0:T(8,128)(2,1)S(1)}, bf16[544,128]{1,0:T(8,128)(2,1)S(1)}, s32[1,1664]{1,0:T(1,128)S(1)}) custom-call(bf16[1024,256]{1,0:T(8,128)(2,1)} %adapter.1, s32[1,256]{1,0:T(1,128)} %bitcast.5, s32[1,256]{1,0:T(1,128)} %bitcast.6, s32[1,64]{1,0:T(1,128)} %bitcast.7, s32[1,1024]{1,0:T(1,128)} %bitcast.4), custom_call_target="tpu_custom_call" | custom-call | bytes 262144 | tf_op jit(solution)/shard_map/pallas_call | solution.py:125
  1.6 2.6 %collective-permute-start.2 = (bf16[544,128]{1,0:T(8,128)(2,1)S(1)}, bf16[544,128]{1,0:T(8,128)(2,1)S(1)}, u32[]{:S(2)}, u32[]{:S(2)}) collective-permute-start(bf16[544,128]{1,0:T(8,128)(2,1)S(1)} %get-tuple-element.20.refs_0_), channel_id=1, source_target_pairs={{0,4},{4,8},{8,12},{12,0},{1,5},{5,9},{9,13},{13,1},{2,6},{6,10},{... | collective-permute-start | bytes 417800 | tf_op jit(solution)/shard_map/ppermute | solution.py:347
  4.3 2.1 %collective-permute-start.4 = (bf16[544,128]{1,0:T(8,128)(2,1)S(1)}, bf16[544,128]{1,0:T(8,128)(2,1)S(1)}, u32[]{:S(2)}, u32[]{:S(2)}) collective-permute-start(bf16[544,128]{1,0:T(8,128)(2,1)S(1)} %get-tuple-element.20.refs_0_), channel_id=1, source_target_pairs={{0,12},{4,0},{8,4},{12,8},{1,13},{5,1},{9,5},{13,9},{2,14},{6,2},{... | collective-permute-start | bytes 417800 | tf_op jit(solution)/shard_map/ppermute | solution.py:347
  6.3 4.5 %collective-permute-done.2.refs_0_.refs_1_ = bf16[544,128]{1,0:T(8,128)(2,1)S(1)} collective-permute-done((bf16[544,128]{1,0:T(8,128)(2,1)S(1)}, bf16[544,128]{1,0:T(8,128)(2,1)S(1)}, u32[]{:S(2)}, u32[]{:S(2)}) %collective-permute-start.2) | collective-permute-done | bytes 139296 | tf_op jit(solution)/shard_map/ppermute | solution.py:347
  10.9 0.0 collective-permute-start.6
  10.9 1.7 %collective-permute-start.3 = (bf16[544,128]{1,0:T(8,128)(2,1)S(1)}, bf16[544,128]{1,0:T(8,128)(2,1)S(1)}, u32[]{:S(2)}, u32[]{:S(2)}) collective-permute-start(bf16[544,128]{1,0:T(8,128)(2,1)S(1)} %collective-permute-done.2.refs_0_.refs_1_), channel_id=1, source_target_pairs={{0,16},{16,0},{1,17},{17,1},{2,18},{18,2},{3,19},{19,3},{4,20},{20... | collective-permute-start | bytes 417800 | tf_op jit(solution)/shard_map/ppermute | solution.py:347
  12.6 0.5 collective-permute-done.4.refs_0_.refs_3_
  13.0 1.5 %collective-permute-start.5 = (bf16[544,128]{1,0:T(8,128)(2,1)S(1)}, bf16[544,128]{1,0:T(8,128)(2,1)S(1)}, u32[]{:S(2)}, u32[]{:S(2)}) collective-permute-start(bf16[544,128]{1,0:T(8,128)(2,1)S(1)} %collective-permute-done.4.refs_0_.refs_3_), channel_id=1, source_target_pairs={{0,16},{16,0},{1,17},{17,1},{2,18},{18,2},{3,19},{19,3},{4,20},{20... | collective-permute-start | bytes 417800 | tf_op jit(solution)/shard_map/ppermute | solution.py:347
  14.6 3.9 %collective-permute-done.6.refs_0_.refs_2_ = bf16[544,128]{1,0:T(8,128)(2,1)S(1)} collective-permute-done((bf16[544,128]{1,0:T(8,128)(2,1)S(1)}, bf16[544,128]{1,0:T(8,128)(2,1)S(1)}, u32[]{:S(2)}, u32[]{:S(2)}) %collective-permute-start.6) | collective-permute-done | bytes 139296 | tf_op jit(solution)/shard_map/ppermute | solution.py:347
  18.5 1.5 %collective-permute-start.7 = (bf16[544,128]{1,0:T(8,128)(2,1)S(1)}, bf16[544,128]{1,0:T(8,128)(2,1)S(1)}, u32[]{:S(2)}, u32[]{:S(2)}) collective-permute-start(bf16[544,128]{1,0:T(8,128)(2,1)S(1)} %collective-permute-done.6.refs_0_.refs_2_), channel_id=1, source_target_pairs={{0,16},{16,0},{1,17},{17,1},{2,18},{18,2},{3,19},{19,3},{4,20},{20... | collective-permute-start | bytes 417800 | tf_op jit(solution)/shard_map/ppermute | solution.py:347
  20.0 0.0 collective-permute-start.1
  20.0 1.2 %collective-permute-done.1.other = s32[1,1664]{1,0:T(1,128)S(1)} collective-permute-done((s32[1,1664]{1,0:T(1,128)S(1)}, s32[1,1664]{1,0:T(1,128)S(1)}, u32[]{:S(2)}, u32[]{:S(2)}) %collective-permute-start.1) | collective-permute-done | bytes 6688 | tf_op jit(solution)/shard_map/ppermute | solution.py:347
  21.2 0.2 shard_map.92
  21.4 0.0 collective-permute-done.other
  21.4 0.0 copy-start
  21.5 1.6 %copy-done = bf16[256,4096]{1,0:T(8,128)(2,1)S(1)} copy-done((bf16[256,4096]{1,0:T(8,128)(2,1)S(1)}, bf16[256,4096]{1,0:T(8,128)(2,1)}, u32[]{:S(2)}) %copy-start) | copy-done | bytes 2097176
  23.0 0.4 shard_map.93.total
  23.5 0.0 collective-permute-done.3.refs_1_
  23.5 1.2 %copy-done.1 = bf16[256,4096]{1,0:T(8,128)(2,1)S(1)} copy-done((bf16[256,4096]{1,0:T(8,128)(2,1)S(1)}, bf16[256,4096]{1,0:T(8,128)(2,1)}, u32[]{:S(2)}) %copy-start.1) | copy-done | bytes 2097176
  24.6 0.4 shard_map.94.total
  25.0 0.0 collective-permute-done.5.refs_1_
  25.1 0.4 shard_map.95.total
  25.5 0.3 shard_map.96.total
  25.8 0.0 collective-permute-done.7.refs_0_
  25.8 0.5 %shard_map.97 = (bf16[512,128]{1,0:T(8,128)(2,1)S(1)}, bf16[128,512]{1,0:T(8,128)(2,1)S(1)}, bf16[128,128]{1,0:T(8,128)(2,1)S(1)}) custom-call(bf16[256,4096]{1,0:T(8,128)(2,1)S(1)} %copy-done.1, bf16[256,4096]{1,0:T(8,128)(2,1)S(1)} %collective-permute-done.other, bf16[128,512]{1,0:T(8,128)(2,1)S(1)} %get-tuple-element.18.pick, ...), custom_call_target="tpu_custom_call" | custom-call | flops 134217728 | bytes 2097152 | tf_op jit(solution)/shard_map/pallas_call | solution.py:125
  26.3 0.1 collective-permute-start.9
  26.4 0.2 collective-permute-start.8
  26.6 3.7 %collective-permute-start.11 = (bf16[128,128]{1,0:T(8,128)(2,1)S(1)}, bf16[128,128]{1,0:T(8,128)(2,1)S(1)}, u32[]{:S(2)}, u32[]{:S(2)}) collective-permute-start(bf16[128,128]{1,0:T(8,128)(2,1)S(1)} %get-tuple-element.21.query), channel_id=1, source_target_pairs={{0,12},{4,0},{8,4},{12,8},{1,13},{5,1},{9,5},{13,9},{2,14},{6,2},{... | collective-permute-start | bytes 98312 | tf_op jit(solution)/shard_map/ppermute | solution.py:347
  30.3 2.1 %shard_map.98 = (bf16[128,1024]{1,0:T(8,128)(2,1)S(1)}, bf16[1024,128]{1,0:T(8,128)(2,1)S(1)}) custom-call(bf16[1024,512]{1,0:T(8,128)(2,1)} %hist_emb.1, bf16[512,256]{1,0:T(8,128)(2,1)} %key_weight.1, bf16[512,256]{1,0:T(8,128)(2,1)} %value_weight.1), custom_call_target="tpu_custom_call" | custom-call | flops 268435456 | bytes 4194304 | tf_op jit(solution)/shard_map/pallas_call | solution.py:125
  32.5 0.0 collective-permute-done.8.tally_other
  32.5 0.6 %shard_map.100.scale = f32[4,128,1536]{2,1,0:T(8,128)S(1)} custom-call(s32[1,1664]{1,0:T(1,128)S(1)} %get-tuple-element.17.mine, s32[1,1664]{1,0:T(1,128)S(1)} %collective-permute-done.1.other, bf16[256,1536]{1,0:T(8,128)(2,1)S(1)} %get-tuple-element.26.hot, f32[16,256]{1,0:T(8,128)S(1)} %shard_map.99.tally, f32[16,256]{1,0:T(8,128)S(1)} %collective-permute-done.8.tally_other), custom_call_target="tpu_custom_call" | custom-call | bytes 4194304 | tf_op jit(solution)/shard_map/pallas_call | solution.py:125
  33.0 0.1 collective-permute-start.13
  33.1 0.0 collective-permute-done.9.query
  33.1 0.7 %shard_map.102 = bf16[128,128]{1,0:T(8,128)(2,1)S(1)} custom-call(bf16[128,128]{1,0:T(8,128)(2,1)S(1)} %collective-permute-done.9.query, bf16[128,1024]{1,0:T(8,128)(2,1)S(1)} %get-tuple-element.22.key_t, bf16[1024,128]{1,0:T(8,128)(2,1)S(1)} %get-tuple-element.23.value, bf16[128,512]{1,0:T(8,128)(2,1)S(1)} %get-tuple-element.24.rows_t, ...), custom_call_target="tpu_custom_call" | custom-call | flops 201326592 | bytes 1048576 | tf_op jit(solution)/shard_map/pallas_call | solution.py:125
  33.8 0.7 %collective-permute-start.10 = (bf16[128,128]{1,0:T(8,128)(2,1)S(1)}, bf16[128,128]{1,0:T(8,128)(2,1)S(1)}, u32[]{:S(2)}, u32[]{:S(2)}) collective-permute-start(bf16[128,128]{1,0:T(8,128)(2,1)S(1)} %shard_map.102), channel_id=1, source_target_pairs={{0,12},{4,0},{8,4},{12,8},{1,13},{5,1},{9,5},{13,9},{2,14},{6,2},{... | collective-permute-start | bytes 98312 | tf_op jit(solution)/shard_map/ppermute | solution.py:347
  34.5 0.7 %shard_map.103 = bf16[128,128]{1,0:T(8,128)(2,1)S(1)} custom-call(bf16[128,128]{1,0:T(8,128)(2,1)S(1)} %collective-permute-done.11.query, bf16[128,1024]{1,0:T(8,128)(2,1)S(1)} %get-tuple-element.22.key_t, bf16[1024,128]{1,0:T(8,128)(2,1)S(1)} %get-tuple-element.23.value, bf16[128,512]{1,0:T(8,128)(2,1)S(1)} %get-tuple-element.24.rows_t, ...), custom_call_target="tpu_custom_call" | custom-call | flops 201326592 | bytes 1048576 | tf_op jit(solution)/shard_map/pallas_call | solution.py:125
  35.2 1.4 %collective-permute-start.12 = (bf16[128,128]{1,0:T(8,128)(2,1)S(1)}, bf16[128,128]{1,0:T(8,128)(2,1)S(1)}, u32[]{:S(2)}, u32[]{:S(2)}) collective-permute-start(bf16[128,128]{1,0:T(8,128)(2,1)S(1)} %shard_map.103), channel_id=1, source_target_pairs={{0,4},{4,8},{8,12},{12,0},{1,5},{5,9},{9,13},{13,1},{2,6},{6,10},{... | collective-permute-start | bytes 98312 | tf_op jit(solution)/shard_map/ppermute | solution.py:347
  36.6 1.6 %collective-permute-done.13.query = bf16[128,128]{1,0:T(8,128)(2,1)S(1)} collective-permute-done((bf16[128,128]{1,0:T(8,128)(2,1)S(1)}, bf16[128,128]{1,0:T(8,128)(2,1)S(1)}, u32[]{:S(2)}, u32[]{:S(2)}) %collective-permute-start.13) | collective-permute-done | bytes 32800 | tf_op jit(solution)/shard_map/ppermute | solution.py:347
  38.2 0.7 %shard_map.104 = bf16[128,128]{1,0:T(8,128)(2,1)S(1)} custom-call(bf16[128,128]{1,0:T(8,128)(2,1)S(1)} %collective-permute-done.13.query, bf16[128,1024]{1,0:T(8,128)(2,1)S(1)} %get-tuple-element.22.key_t, bf16[1024,128]{1,0:T(8,128)(2,1)S(1)} %get-tuple-element.23.value, bf16[128,512]{1,0:T(8,128)(2,1)S(1)} %get-tuple-element.24.rows_t, ...), custom_call_target="tpu_custom_call" | custom-call | flops 201326592 | bytes 1048576 | tf_op jit(solution)/shard_map/pallas_call | solution.py:125
  38.9 1.4 %collective-permute-start.14 = (bf16[128,128]{1,0:T(8,128)(2,1)S(1)}, bf16[128,128]{1,0:T(8,128)(2,1)S(1)}, u32[]{:S(2)}, u32[]{:S(2)}) collective-permute-start(bf16[128,128]{1,0:T(8,128)(2,1)S(1)} %shard_map.104), channel_id=1, source_target_pairs={{0,8},{4,12},{8,0},{12,4},{1,9},{5,13},{9,1},{13,5},{2,10},{6,14},... | collective-permute-start | bytes 98312 | tf_op jit(solution)/shard_map/ppermute | solution.py:347
  40.3 0.7 %shard_map.101.own = f32[128,128]{1,0:T(8,128)S(1)} custom-call(bf16[128,128]{1,0:T(8,128)(2,1)S(1)} %get-tuple-element.21.query, bf16[128,1024]{1,0:T(8,128)(2,1)S(1)} %get-tuple-element.22.key_t, bf16[1024,128]{1,0:T(8,128)(2,1)S(1)} %get-tuple-element.23.value, bf16[128,512]{1,0:T(8,128)(2,1)S(1)} %get-tuple-element.24.rows_t, ...), custom_call_target="tpu_custom_call" | custom-call | flops 201326592 | bytes 1048576 | tf_op jit(solution)/shard_map/pallas_call | solution.py:125
  41.0 0.0 collective-permute-done.10.refs_0_
  41.0 0.0 collective-permute-done.12.refs_1_
  41.0 2.8 %collective-permute-done.14.refs_2_ = bf16[128,128]{1,0:T(8,128)(2,1)S(1)} collective-permute-done((bf16[128,128]{1,0:T(8,128)(2,1)S(1)}, bf16[128,128]{1,0:T(8,128)(2,1)S(1)}, u32[]{:S(2)}, u32[]{:S(2)}) %collective-permute-start.14) | collective-permute-done | bytes 32800 | tf_op jit(solution)/shard_map/ppermute | solution.py:347
  43.8 0.1 collective-permute-start.15
  43.9 1.2 %collective-permute-done.15.got = bf16[64,128]{1,0:T(8,128)(2,1)S(1)} collective-permute-done((bf16[64,128]{1,0:T(8,128)(2,1)S(1)}, bf16[64,128]{1,0:T(8,128)(2,1)S(1)}, u32[]{:S(2)}, u32[]{:S(2)}) %collective-permute-start.15) | collective-permute-done | bytes 16416 | tf_op jit(solution)/shard_map/ppermute | solution.py:347
  45.0 0.6 %shard_map.106 = bf16[64,256]{1,0:T(8,128)(2,1)} custom-call(bf16[64,128]{1,0:T(8,128)(2,1)S(1)} %get-tuple-element.27.keep, bf16[64,128]{1,0:T(8,128)(2,1)S(1)} %collective-permute-done.15.got), custom_call_target="tpu_custom_call" | custom-call | bytes 262144 | tf_op jit(solution)/shard_map/pallas_call | solution.py:125
  (4 shorter events, 0.1 us)
Async XLA Ops:
  0.0 21.4 %collective-permute-start = (bf16[256,4096]{1,0:T(8,128)(2,1)}, bf16[256,4096]{1,0:T(8,128)(2,1)S(1)}, u32[]{:S(2)}, u32[]{:S(2)}) collective-permute-start(bf16[256,4096]{1,0:T(8,128)(2,1)} %mine.9), channel_id=1, source_target_pairs={{0,1},{1,0},{2,3},{3,2},{4,5},{5,4},{6,7},{7,6},{8,9},{9,8},{10,11... | collective-permute-start | bytes 6291464 | tf_op jit(solution)/shard_map/ppermute | solution.py:347
  1.6 9.2 %collective-permute-start.2 = (bf16[544,128]{1,0:T(8,128)(2,1)S(1)}, bf16[544,128]{1,0:T(8,128)(2,1)S(1)}, u32[]{:S(2)}, u32[]{:S(2)}) collective-permute-start(bf16[544,128]{1,0:T(8,128)(2,1)S(1)} %get-tuple-element.20.refs_0_), channel_id=1, source_target_pairs={{0,4},{4,8},{8,12},{12,0},{1,5},{5,9},{9,13},{13,1},{2,6},{6,10},{... | collective-permute-start | bytes 417800 | tf_op jit(solution)/shard_map/ppermute | solution.py:347
  4.3 8.8 %collective-permute-start.4 = (bf16[544,128]{1,0:T(8,128)(2,1)S(1)}, bf16[544,128]{1,0:T(8,128)(2,1)S(1)}, u32[]{:S(2)}, u32[]{:S(2)}) collective-permute-start(bf16[544,128]{1,0:T(8,128)(2,1)S(1)} %get-tuple-element.20.refs_0_), channel_id=1, source_target_pairs={{0,12},{4,0},{8,4},{12,8},{1,13},{5,1},{9,5},{13,9},{2,14},{6,2},{... | collective-permute-start | bytes 417800 | tf_op jit(solution)/shard_map/ppermute | solution.py:347
  10.9 7.7 %collective-permute-start.6 = (bf16[544,128]{1,0:T(8,128)(2,1)S(1)}, bf16[544,128]{1,0:T(8,128)(2,1)S(1)}, u32[]{:S(2)}, u32[]{:S(2)}) collective-permute-start(bf16[544,128]{1,0:T(8,128)(2,1)S(1)} %collective-permute-done.2.refs_0_.refs_1_), channel_id=1, source_target_pairs={{0,4},{4,8},{8,12},{12,0},{1,5},{5,9},{9,13},{13,1},{2,6},{6,10},{... | collective-permute-start | bytes 417800 | tf_op jit(solution)/shard_map/ppermute | solution.py:347
  10.9 12.6 %collective-permute-start.3 = (bf16[544,128]{1,0:T(8,128)(2,1)S(1)}, bf16[544,128]{1,0:T(8,128)(2,1)S(1)}, u32[]{:S(2)}, u32[]{:S(2)}) collective-permute-start(bf16[544,128]{1,0:T(8,128)(2,1)S(1)} %collective-permute-done.2.refs_0_.refs_1_), channel_id=1, source_target_pairs={{0,16},{16,0},{1,17},{17,1},{2,18},{18,2},{3,19},{19,3},{4,20},{20... | collective-permute-start | bytes 417800 | tf_op jit(solution)/shard_map/ppermute | solution.py:347
  13.0 12.0 %collective-permute-start.5 = (bf16[544,128]{1,0:T(8,128)(2,1)S(1)}, bf16[544,128]{1,0:T(8,128)(2,1)S(1)}, u32[]{:S(2)}, u32[]{:S(2)}) collective-permute-start(bf16[544,128]{1,0:T(8,128)(2,1)S(1)} %collective-permute-done.4.refs_0_.refs_3_), channel_id=1, source_target_pairs={{0,16},{16,0},{1,17},{17,1},{2,18},{18,2},{3,19},{19,3},{4,20},{20... | collective-permute-start | bytes 417800 | tf_op jit(solution)/shard_map/ppermute | solution.py:347
  18.5 7.3 %collective-permute-start.7 = (bf16[544,128]{1,0:T(8,128)(2,1)S(1)}, bf16[544,128]{1,0:T(8,128)(2,1)S(1)}, u32[]{:S(2)}, u32[]{:S(2)}) collective-permute-start(bf16[544,128]{1,0:T(8,128)(2,1)S(1)} %collective-permute-done.6.refs_0_.refs_2_), channel_id=1, source_target_pairs={{0,16},{16,0},{1,17},{17,1},{2,18},{18,2},{3,19},{19,3},{4,20},{20... | collective-permute-start | bytes 417800 | tf_op jit(solution)/shard_map/ppermute | solution.py:347
  20.0 1.2 %collective-permute-start.1 = (s32[1,1664]{1,0:T(1,128)S(1)}, s32[1,1664]{1,0:T(1,128)S(1)}, u32[]{:S(2)}, u32[]{:S(2)}) collective-permute-start(s32[1,1664]{1,0:T(1,128)S(1)} %get-tuple-element.17.mine), channel_id=1, source_target_pairs={{0,1},{1,0},{2,3},{3,2},{4,5},{5,4},{6,7},{7,6},{8,9},{9,8},{10,11... | collective-permute-start | bytes 19976 | tf_op jit(solution)/shard_map/ppermute | solution.py:347
  21.4 1.6 %copy-start = (bf16[256,4096]{1,0:T(8,128)(2,1)S(1)}, bf16[256,4096]{1,0:T(8,128)(2,1)}, u32[]{:S(2)}) copy-start(bf16[256,4096]{1,0:T(8,128)(2,1)} %mine.9) | copy-start | bytes 6291460
  23.0 1.6 %copy-start.1 = (bf16[256,4096]{1,0:T(8,128)(2,1)S(1)}, bf16[256,4096]{1,0:T(8,128)(2,1)}, u32[]{:S(2)}) copy-start(bf16[256,4096]{1,0:T(8,128)(2,1)} %mine.9) | copy-start | bytes 6291460
  26.3 6.8 %collective-permute-start.9 = (bf16[128,128]{1,0:T(8,128)(2,1)S(1)}, bf16[128,128]{1,0:T(8,128)(2,1)S(1)}, u32[]{:S(2)}, u32[]{:S(2)}) collective-permute-start(bf16[128,128]{1,0:T(8,128)(2,1)S(1)} %get-tuple-element.21.query), channel_id=1, source_target_pairs={{0,4},{4,8},{8,12},{12,0},{1,5},{5,9},{9,13},{13,1},{2,6},{6,10},{... | collective-permute-start | bytes 98312 | tf_op jit(solution)/shard_map/ppermute | solution.py:347
  26.4 6.1 %collective-permute-start.8 = (f32[16,256]{1,0:T(8,128)S(1)}, f32[16,256]{1,0:T(8,128)S(1)}, u32[]{:S(2)}, u32[]{:S(2)}) collective-permute-start(f32[16,256]{1,0:T(8,128)S(1)} %shard_map.99.tally), channel_id=1, source_target_pairs={{0,1},{1,0},{2,3},{3,2},{4,5},{5,4},{6,7},{7,6},{8,9},{9,8},{10,11... | collective-permute-start | bytes 49160 | tf_op jit(solution)/shard_map/ppermute | solution.py:347
  26.6 7.9 %collective-permute-start.11 = (bf16[128,128]{1,0:T(8,128)(2,1)S(1)}, bf16[128,128]{1,0:T(8,128)(2,1)S(1)}, u32[]{:S(2)}, u32[]{:S(2)}) collective-permute-start(bf16[128,128]{1,0:T(8,128)(2,1)S(1)} %get-tuple-element.21.query), channel_id=1, source_target_pairs={{0,12},{4,0},{8,4},{12,8},{1,13},{5,1},{9,5},{13,9},{2,14},{6,2},{... | collective-permute-start | bytes 98312 | tf_op jit(solution)/shard_map/ppermute | solution.py:347
  33.0 5.2 %collective-permute-start.13 = (bf16[128,128]{1,0:T(8,128)(2,1)S(1)}, bf16[128,128]{1,0:T(8,128)(2,1)S(1)}, u32[]{:S(2)}, u32[]{:S(2)}) collective-permute-start(bf16[128,128]{1,0:T(8,128)(2,1)S(1)} %get-tuple-element.21.query), channel_id=1, source_target_pairs={{0,8},{4,12},{8,0},{12,4},{1,9},{5,13},{9,1},{13,5},{2,10},{6,14},... | collective-permute-start | bytes 98312 | tf_op jit(solution)/shard_map/ppermute | solution.py:347
  33.8 7.2 %collective-permute-start.10 = (bf16[128,128]{1,0:T(8,128)(2,1)S(1)}, bf16[128,128]{1,0:T(8,128)(2,1)S(1)}, u32[]{:S(2)}, u32[]{:S(2)}) collective-permute-start(bf16[128,128]{1,0:T(8,128)(2,1)S(1)} %shard_map.102), channel_id=1, source_target_pairs={{0,12},{4,0},{8,4},{12,8},{1,13},{5,1},{9,5},{13,9},{2,14},{6,2},{... | collective-permute-start | bytes 98312 | tf_op jit(solution)/shard_map/ppermute | solution.py:347
  35.2 5.8 %collective-permute-start.12 = (bf16[128,128]{1,0:T(8,128)(2,1)S(1)}, bf16[128,128]{1,0:T(8,128)(2,1)S(1)}, u32[]{:S(2)}, u32[]{:S(2)}) collective-permute-start(bf16[128,128]{1,0:T(8,128)(2,1)S(1)} %shard_map.103), channel_id=1, source_target_pairs={{0,4},{4,8},{8,12},{12,0},{1,5},{5,9},{9,13},{13,1},{2,6},{6,10},{... | collective-permute-start | bytes 98312 | tf_op jit(solution)/shard_map/ppermute | solution.py:347
  38.9 4.9 %collective-permute-start.14 = (bf16[128,128]{1,0:T(8,128)(2,1)S(1)}, bf16[128,128]{1,0:T(8,128)(2,1)S(1)}, u32[]{:S(2)}, u32[]{:S(2)}) collective-permute-start(bf16[128,128]{1,0:T(8,128)(2,1)S(1)} %shard_map.104), channel_id=1, source_target_pairs={{0,8},{4,12},{8,0},{12,4},{1,9},{5,13},{9,1},{13,5},{2,10},{6,14},... | collective-permute-start | bytes 98312 | tf_op jit(solution)/shard_map/ppermute | solution.py:347
  43.8 1.2 %collective-permute-start.15 = (bf16[64,128]{1,0:T(8,128)(2,1)S(1)}, bf16[64,128]{1,0:T(8,128)(2,1)S(1)}, u32[]{:S(2)}, u32[]{:S(2)}) collective-permute-start(bf16[64,128]{1,0:T(8,128)(2,1)S(1)} %get-tuple-element.28), channel_id=1, source_target_pairs={{0,1},{1,0},{2,3},{3,2},{4,5},{5,4},{6,7},{7,6},{8,9},{9,8},{10,11... | collective-permute-start | bytes 49160 | tf_op jit(solution)/shard_map/ppermute | solution.py:347

commit v3 on v2

--- a/solution.py
+++ b/solution.py
@@ -11,7 +11,7 @@
 
 HS = 64
 USERS = 256
-LISTED = 32
+LISTED = 16
 VM = pl.BlockSpec(memory_space=pltpu.VMEM)
 HBM = pl.BlockSpec(memory_space=pltpu.HBM)
 F32 = jnp.float32
@@ -186,14 +186,24 @@
     chosen = one_hot((items, cands), 0, cand[...])
     users = dot(jnp.broadcast_to(user[...], (8, items)).astype(F32).astype(BF16), chosen)
     users = jnp.concatenate([users, jnp.zeros((8, USERS - cands), F32)], axis=1)
-    high = jnp.floor(counts * (1.0 / 256.0))
-    low = jnp.where(iota(counts.shape, 0) == 7, users, counts - 256.0 * high)
+    quarter = jnp.floor(counts * 0.25)
+    rest = jnp.sum((counts - 4.0 * quarter) * digit_weight(4.0), axis=0, keepdims=True)
     half = USERS // 2
-    listed = jnp.concatenate([low[:, :half], low[:, half:], high[:, :half], high[:, half:]], axis=0)
-    out[rows:] = listed.astype(BF16)
+    row = iota((8, half), 0)
+    top = jnp.where(row < 4, quarter[:, :half], pltpu.roll(quarter[:, half:], 4, 0))
+    bottom = jnp.where(row == 0, rest[:, :half], jnp.where(row == 1, rest[:, half:], users[:, :half]))
+    out[rows:] = jnp.concatenate([top, jnp.where(row < 3, bottom, 0.0)], axis=0).astype(BF16)
     for copy in copies[4:]:
         copy.wait()
     mine[:, 2 * items + 2 * cands :] = events[...]
+
+
+def digit_weight(base):
+    row = iota((8, 1), 0)
+    weight = jnp.zeros((8, 1), F32)
+    for owner in range(4):
+        weight = jnp.where(row == owner, base ** owner, weight)
+    return weight
 
 
 def users_kernel(mine, other, hot, pick):
@@ -214,13 +224,17 @@
 
 def tally_kernel(*refs):
     out = refs[-1]
+    row = iota((8, USERS // 2), 0)
     total = jnp.zeros((8, USERS), F32)
     for k, ref in enumerate(refs[:-1]):
         listed = ref[ref.shape[0] - LISTED :].astype(F32)
-        low = jnp.concatenate([listed[:8], listed[8:16]], axis=1)
-        high = jnp.concatenate([listed[16:24], listed[24:]], axis=1)
-        total = total + low + 256.0 * high
-        out[8 + k : 9 + k] = low[7:8]
+        top, bottom = listed[:8], listed[8:]
+        low, high = jnp.where(row < 4, top, 0.0), jnp.where(row < 4, pltpu.roll(top, 4, 0), 0.0)
+        rest = jnp.concatenate([bottom[:1], bottom[1:2]], axis=1)
+        digits = jnp.floor(rest * digit_weight(0.25))
+        rest = digits - 4.0 * jnp.floor(digits * 0.25)
+        total = total + 4.0 * jnp.concatenate([low, high], axis=1) + rest
+        out[8 + k : 9 + k] = jnp.concatenate([bottom[2:3], jnp.zeros_like(bottom[2:3])], axis=1)
     out[:8] = total
 
 
@@ -274,9 +288,7 @@
 
 def add_block(n, groups, k, step, mine, other, top, bottom, block):
     depth = block.shape[0] - LISTED
-    source = lax.rem(lax.axis_index("hist") + n - k, n)
-    group = lax.rem(lax.axis_index("groups") + groups - step, groups)
-    at = pl.ds(pl.multiple_of((source * groups + group) * depth, depth), depth)
+    at = columns_of(n, groups, k, step, depth)
     return top + dot(mine[:, at], block[:depth]), bottom + dot(other[:, at], block[:depth])
 
 
@@ -289,15 +301,28 @@
     refs[-1][items:] = bottom
 
 
-def embed_last_kernel(n, groups, which, mine, other, pick, total, *refs):
+def columns_of(n, groups, k, step, depth):
+    source = lax.rem(lax.axis_index("hist") + n - k, n)
+    group = lax.rem(lax.axis_index("groups") + groups - step, groups)
+    return pl.ds(pl.multiple_of((source * groups + group) * depth, depth), depth)
+
+
+def query_part_kernel(n, groups, k, step, mine, other, pick, total, part, feats):
     items = mine.shape[0]
-    top, bottom = total[:items], total[items:]
-    for (k, step), block in zip(which, refs):
-        top, bottom = add_block(n, groups, k, step, mine, other, top, bottom, block)
-    rows, rows_t, query = refs[len(which) :]
+    at = columns_of(n, groups, k, step, feats.shape[1])
+    part[...] = lax.dot(pick[...].astype(F32), total[...], precision=lax.Precision.HIGHEST)
+    feats[...] = (dot(pick[:, :items], mine[:, at]) + dot(pick[:, items:], other[:, at])).astype(BF16)
+
+
+def query_kernel(part, feats, block, query):
+    query[...] = (part[...] + dot(feats[...], block[: feats.shape[1]])).astype(BF16)
+
+
+def embed_last_kernel(n, groups, k, step, mine, other, total, block, rows, rows_t):
+    items = mine.shape[0]
+    top, bottom = add_block(n, groups, k, step, mine, other, total[:items], total[items:], block)
     rows[:items] = top.astype(BF16)
     rows[items:] = bottom.astype(BF16)
-    query[...] = dot(pick[...], rows[...]).astype(BF16)
     rows_t[...] = jnp.transpose(rows[...])
 
 
@@ -438,12 +463,20 @@
             flops=4 * items * depth * width,
             bytes_accessed=2 << 20,
         )
-    which, arrived = zip(*blocks[-1:])
-    rows, rows_t, query = call(
-        functools.partial(embed_last_kernel, n, groups, which),
-        (shape((2 * items, width), BF16), shape((width, 2 * items), BF16), shape((cands, width), BF16)),
-        (item_feats, feats_other, pick, total, *arrived),
-        flops=4 * items * depth * width,
+    (k, step), arrived = blocks[-1]
+    share = depth // groups
+    part, feats = call(
+        functools.partial(query_part_kernel, n, groups, k, step),
+        (shape((cands, width), F32), shape((cands, share), BF16)),
+        (item_feats, feats_other, pick, total),
+        flops=4 * cands * items * (share + 6 * width),
+    )
+    query = call(query_kernel, shape((cands, width), BF16), (part, feats, arrived), flops=2 * cands * share * width)
+    rows, rows_t = call(
+        functools.partial(embed_last_kernel, n, groups, k, step),
+        (shape((2 * items, width), BF16), shape((width, 2 * items), BF16)),
+        (item_feats, feats_other, total, arrived),
+        flops=4 * items * share * width,
         bytes_accessed=2 << 20,
     )
     queries = {k: shift(query, "hist", k) for k in order}
@@ -470,7 +503,8 @@
     item_feats, adapter, cand_index, hist_user = args[0], args[1], args[6], args[8]
     fits = (
         lax.axis_size("rep") == 2
-        and 1 < lax.axis_size("hist") < 8
+        and 1 < lax.axis_size("hist") <= 4
+        and item_feats.shape[0] + hist_user.shape[0] // 2 < 1024
         and hist_user.shape[0] % 256 == 0
         and adapter.shape[0] % (128 * lax.axis_size("groups")) == 0
         and adapter.shape[1] % 256 == 0

time: 45.9 us -> 45.9 us (level)
  waiting for transfers between devices: 15.6 us -> 14.3 us
  starting transfers between devices: 17.6 us -> 18.4 us
  Pallas kernels: 9.47 us -> 10.1 us
    ppermute x16, waiting for transfers between devices: 15.6 us -> 14.3 us  [shift(): lax.ppermute(value, axis, [(i, (i + k) % count) for i in range(count)])]
    ppermute x16, starting transfers between devices: 17.6 us -> 18.4 us  [shift(): lax.ppermute(value, axis, [(i, (i + k) % count) for i in range(count)])]
    pallas_call x16 -> x18, Pallas kernels: 9.47 us -> 10.1 us  [call(): pl.pallas_call(kernel, out_shape=outs, in_specs=specs or [VM] * len(args)...]
  transfers between devices with their start and end apart: 16 -> 16, of which waited for: 7 -> 7; matrix products, arithmetic and copies ran while one was open for 0% -> 0% of each run, Pallas kernels for 18% -> 20%
where the time goes in v3:
time: 45.9 us; the launch traced here: 45.7 us
  starting transfers between devices  18.4 us (40%)
  waiting for transfers between devices  14.3 us (31%)
  Pallas kernels  10.1 us (22%)
  local copies, waits for them, and re-layouts  2.74 us (6%)
    ppermute x16, starting transfers between devices, shift(): lax.ppermute(value, axis, [(i, (i + k) % count) for i in range(count)])  18.4 us
    ppermute x16, waiting for transfers between devices, shift(): lax.ppermute(value, axis, [(i, (i + k) % count) for i in range(count)])  14.3 us
    pallas_call x18, Pallas kernels, call(): pl.pallas_call(kernel, out_shape=outs, in_specs=specs or [VM] * len(args)...  10.1 us
    unnamed x4, local copies, waits for them, and re-layouts  2.74 us
  transfers between devices with their start and end apart: 16, of which 7 were waited for; matrix products, arithmetic and copies ran while one was open for 0% of the time, Pallas kernels for 20%

profile of v3, /device:TPU:0, one launch (start us, length us, event | category | flops | bytes accessed | tf_op | source)
XLA Modules:
  0.0 45.7 jit_solution(3626095049295051564)
XLA Ops:
  0.0 0.5 %collective-permute-start = (bf16[256,4096]{1,0:T(8,128)(2,1)}, bf16[256,4096]{1,0:T(8,128)(2,1)S(1)}, u32[]{:S(2)}, u32[]{:S(2)}) collective-permute-start(bf16[256,4096]{1,0:T(8,128)(2,1)} %mine.11), channel_id=1, source_target_pairs={{0,1},{1,0},{2,3},{3,2},{4,5},{5,4},{6,7},{7,6},{8,9},{9,8},{10,11... | collective-permute-start | bytes 6291464 | tf_op jit(solution)/shard_map/ppermute | solution.py:372
  0.5 1.1 %shard_map.91 = (bf16[1024,128]{1,0:T(8,128)(2,1)S(1)}, bf16[528,128]{1,0:T(8,128)(2,1)S(1)}, s32[1,1664]{1,0:T(1,128)S(1)}) custom-call(bf16[1024,256]{1,0:T(8,128)(2,1)} %adapter.1, s32[1,256]{1,0:T(1,128)} %bitcast.5, s32[1,256]{1,0:T(1,128)} %bitcast.6, s32[1,64]{1,0:T(1,128)} %bitcast.7, s32[1,1024]{1,0:T(1,128)} %bitcast.4), custom_call_target="tpu_custom_call" | custom-call | bytes 262144 | tf_op jit(solution)/shard_map/pallas_call | solution.py:125
  1.6 2.6 %collective-permute-start.2 = (bf16[528,128]{1,0:T(8,128)(2,1)S(1)}, bf16[528,128]{1,0:T(8,128)(2,1)S(1)}, u32[]{:S(2)}, u32[]{:S(2)}) collective-permute-start(bf16[528,128]{1,0:T(8,128)(2,1)S(1)} %get-tuple-element.21.refs_0_), channel_id=1, source_target_pairs={{0,4},{4,8},{8,12},{12,0},{1,5},{5,9},{9,13},{13,1},{2,6},{6,10},{... | collective-permute-start | bytes 405512 | tf_op jit(solution)/shard_map/ppermute | solution.py:372
  4.3 2.1 %collective-permute-start.4 = (bf16[528,128]{1,0:T(8,128)(2,1)S(1)}, bf16[528,128]{1,0:T(8,128)(2,1)S(1)}, u32[]{:S(2)}, u32[]{:S(2)}) collective-permute-start(bf16[528,128]{1,0:T(8,128)(2,1)S(1)} %get-tuple-element.21.refs_0_), channel_id=1, source_target_pairs={{0,12},{4,0},{8,4},{12,8},{1,13},{5,1},{9,5},{13,9},{2,14},{6,2},{... | collective-permute-start | bytes 405512 | tf_op jit(solution)/shard_map/ppermute | solution.py:372
  6.3 4.4 %collective-permute-done.2.refs_0_.refs_1_ = bf16[528,128]{1,0:T(8,128)(2,1)S(1)} collective-permute-done((bf16[528,128]{1,0:T(8,128)(2,1)S(1)}, bf16[528,128]{1,0:T(8,128)(2,1)S(1)}, u32[]{:S(2)}, u32[]{:S(2)}) %collective-permute-start.2) | collective-permute-done | bytes 135200 | tf_op jit(solution)/shard_map/ppermute | solution.py:372
  10.8 0.0 collective-permute-start.6
  10.8 1.7 %collective-permute-start.3 = (bf16[528,128]{1,0:T(8,128)(2,1)S(1)}, bf16[528,128]{1,0:T(8,128)(2,1)S(1)}, u32[]{:S(2)}, u32[]{:S(2)}) collective-permute-start(bf16[528,128]{1,0:T(8,128)(2,1)S(1)} %collective-permute-done.2.refs_0_.refs_1_), channel_id=1, source_target_pairs={{0,16},{16,0},{1,17},{17,1},{2,18},{18,2},{3,19},{19,3},{4,20},{20... | collective-permute-start | bytes 405512 | tf_op jit(solution)/shard_map/ppermute | solution.py:372
  12.5 0.4 collective-permute-done.4.refs_0_.refs_3_
  12.9 1.5 %collective-permute-start.5 = (bf16[528,128]{1,0:T(8,128)(2,1)S(1)}, bf16[528,128]{1,0:T(8,128)(2,1)S(1)}, u32[]{:S(2)}, u32[]{:S(2)}) collective-permute-start(bf16[528,128]{1,0:T(8,128)(2,1)S(1)} %collective-permute-done.4.refs_0_.refs_3_), channel_id=1, source_target_pairs={{0,16},{16,0},{1,17},{17,1},{2,18},{18,2},{3,19},{19,3},{4,20},{20... | collective-permute-start | bytes 405512 | tf_op jit(solution)/shard_map/ppermute | solution.py:372
  14.4 3.9 %collective-permute-done.6.refs_0_.refs_2_ = bf16[528,128]{1,0:T(8,128)(2,1)S(1)} collective-permute-done((bf16[528,128]{1,0:T(8,128)(2,1)S(1)}, bf16[528,128]{1,0:T(8,128)(2,1)S(1)}, u32[]{:S(2)}, u32[]{:S(2)}) %collective-permute-start.6) | collective-permute-done | bytes 135200 | tf_op jit(solution)/shard_map/ppermute | solution.py:372
  18.3 1.5 %collective-permute-start.7 = (bf16[528,128]{1,0:T(8,128)(2,1)S(1)}, bf16[528,128]{1,0:T(8,128)(2,1)S(1)}, u32[]{:S(2)}, u32[]{:S(2)}) collective-permute-start(bf16[528,128]{1,0:T(8,128)(2,1)S(1)} %collective-permute-done.6.refs_0_.refs_2_), channel_id=1, source_target_pairs={{0,16},{16,0},{1,17},{17,1},{2,18},{18,2},{3,19},{19,3},{4,20},{20... | collective-permute-start | bytes 405512 | tf_op jit(solution)/shard_map/ppermute | solution.py:372
  19.8 0.0 collective-permute-start.1
  19.8 1.2 %collective-permute-done.1.other = s32[1,1664]{1,0:T(1,128)S(1)} collective-permute-done((s32[1,1664]{1,0:T(1,128)S(1)}, s32[1,1664]{1,0:T(1,128)S(1)}, u32[]{:S(2)}, u32[]{:S(2)}) %collective-permute-start.1) | collective-permute-done | bytes 6688 | tf_op jit(solution)/shard_map/ppermute | solution.py:372
  21.0 0.2 shard_map.92
  21.2 0.0 collective-permute-done.other
  21.2 0.0 copy-start
  21.2 1.6 %copy-done = bf16[256,4096]{1,0:T(8,128)(2,1)S(1)} copy-done((bf16[256,4096]{1,0:T(8,128)(2,1)S(1)}, bf16[256,4096]{1,0:T(8,128)(2,1)}, u32[]{:S(2)}) %copy-start) | copy-done | bytes 2097176
  22.8 0.4 shard_map.93.total
  23.2 0.0 collective-permute-done.3.refs_1_
  23.3 1.2 %copy-done.1 = bf16[256,4096]{1,0:T(8,128)(2,1)S(1)} copy-done((bf16[256,4096]{1,0:T(8,128)(2,1)S(1)}, bf16[256,4096]{1,0:T(8,128)(2,1)}, u32[]{:S(2)}) %copy-start.1) | copy-done | bytes 2097176
  24.4 0.4 shard_map.94.total
  24.8 0.0 collective-permute-done.5.refs_1_
  24.8 0.4 shard_map.95.total
  25.3 0.3 shard_map.96.total
  25.6 0.4 shard_map.97
  26.0 0.0 collective-permute-done.7.block
  26.0 0.2 shard_map.98.query
  26.2 0.1 collective-permute-start.9
  26.3 0.2 collective-permute-start.8
  26.5 3.7 %collective-permute-start.11 = (bf16[128,128]{1,0:T(8,128)(2,1)S(1)}, bf16[128,128]{1,0:T(8,128)(2,1)S(1)}, u32[]{:S(2)}, u32[]{:S(2)}) collective-permute-start(bf16[128,128]{1,0:T(8,128)(2,1)S(1)} %shard_map.98.query), channel_id=1, source_target_pairs={{0,12},{4,0},{8,4},{12,8},{1,13},{5,1},{9,5},{13,9},{2,14},{6,2},{... | collective-permute-start | bytes 98312 | tf_op jit(solution)/shard_map/ppermute | solution.py:372
  30.2 2.1 %shard_map.99 = (bf16[128,1024]{1,0:T(8,128)(2,1)S(1)}, bf16[1024,128]{1,0:T(8,128)(2,1)S(1)}) custom-call(bf16[1024,512]{1,0:T(8,128)(2,1)} %hist_emb.1, bf16[512,256]{1,0:T(8,128)(2,1)} %key_weight.1, bf16[512,256]{1,0:T(8,128)(2,1)} %value_weight.1), custom_call_target="tpu_custom_call" | custom-call | flops 268435456 | bytes 4194304 | tf_op jit(solution)/shard_map/pallas_call | solution.py:125
  32.4 0.0 collective-permute-done.8.tally_other
  32.4 0.6 %shard_map.102.scale = f32[4,128,1536]{2,1,0:T(8,128)S(1)} custom-call(s32[1,1664]{1,0:T(1,128)S(1)} %get-tuple-element.18.mine, s32[1,1664]{1,0:T(1,128)S(1)} %collective-permute-done.1.other, bf16[256,1536]{1,0:T(8,128)(2,1)S(1)} %get-tuple-element.28.hot, f32[16,256]{1,0:T(8,128)S(1)} %shard_map.101.tally, f32[16,256]{1,0:T(8,128)S(1)} %collective-permute-done.8.tally_other), custom_call_target="tpu_custom_call" | custom-call | bytes 4194304 | tf_op jit(solution)/shard_map/pallas_call | solution.py:125
  33.0 0.1 collective-permute-start.13
  33.0 0.4 shard_map.100
  33.4 0.0 collective-permute-done.9.query
  33.5 0.7 %shard_map.104 = bf16[128,128]{1,0:T(8,128)(2,1)S(1)} custom-call(bf16[128,128]{1,0:T(8,128)(2,1)S(1)} %collective-permute-done.9.query, bf16[128,1024]{1,0:T(8,128)(2,1)S(1)} %get-tuple-element.24.key_t, bf16[1024,128]{1,0:T(8,128)(2,1)S(1)} %get-tuple-element.25.value, bf16[128,512]{1,0:T(8,128)(2,1)S(1)} %get-tuple-element.26.rows_t, ...), custom_call_target="tpu_custom_call" | custom-call | flops 201326592 | bytes 1048576 | tf_op jit(solution)/shard_map/pallas_call | solution.py:125
  34.2 0.7 %collective-permute-start.10 = (bf16[128,128]{1,0:T(8,128)(2,1)S(1)}, bf16[128,128]{1,0:T(8,128)(2,1)S(1)}, u32[]{:S(2)}, u32[]{:S(2)}) collective-permute-start(bf16[128,128]{1,0:T(8,128)(2,1)S(1)} %shard_map.104), channel_id=1, source_target_pairs={{0,12},{4,0},{8,4},{12,8},{1,13},{5,1},{9,5},{13,9},{2,14},{6,2},{... | collective-permute-start | bytes 98312 | tf_op jit(solution)/shard_map/ppermute | solution.py:372
  34.9 0.7 %shard_map.105 = bf16[128,128]{1,0:T(8,128)(2,1)S(1)} custom-call(bf16[128,128]{1,0:T(8,128)(2,1)S(1)} %collective-permute-done.11.query, bf16[128,1024]{1,0:T(8,128)(2,1)S(1)} %get-tuple-element.24.key_t, bf16[1024,128]{1,0:T(8,128)(2,1)S(1)} %get-tuple-element.25.value, bf16[128,512]{1,0:T(8,128)(2,1)S(1)} %get-tuple-element.26.rows_t, ...), custom_call_target="tpu_custom_call" | custom-call | flops 201326592 | bytes 1048576 | tf_op jit(solution)/shard_map/pallas_call | solution.py:125
  35.6 1.4 %collective-permute-start.12 = (bf16[128,128]{1,0:T(8,128)(2,1)S(1)}, bf16[128,128]{1,0:T(8,128)(2,1)S(1)}, u32[]{:S(2)}, u32[]{:S(2)}) collective-permute-start(bf16[128,128]{1,0:T(8,128)(2,1)S(1)} %shard_map.105), channel_id=1, source_target_pairs={{0,4},{4,8},{8,12},{12,0},{1,5},{5,9},{9,13},{13,1},{2,6},{6,10},{... | collective-permute-start | bytes 98312 | tf_op jit(solution)/shard_map/ppermute | solution.py:372
  37.0 0.8 %collective-permute-done.13.query = bf16[128,128]{1,0:T(8,128)(2,1)S(1)} collective-permute-done((bf16[128,128]{1,0:T(8,128)(2,1)S(1)}, bf16[128,128]{1,0:T(8,128)(2,1)S(1)}, u32[]{:S(2)}, u32[]{:S(2)}) %collective-permute-start.13) | collective-permute-done | bytes 32800 | tf_op jit(solution)/shard_map/ppermute | solution.py:372
  37.8 0.7 %shard_map.106 = bf16[128,128]{1,0:T(8,128)(2,1)S(1)} custom-call(bf16[128,128]{1,0:T(8,128)(2,1)S(1)} %collective-permute-done.13.query, bf16[128,1024]{1,0:T(8,128)(2,1)S(1)} %get-tuple-element.24.key_t, bf16[1024,128]{1,0:T(8,128)(2,1)S(1)} %get-tuple-element.25.value, bf16[128,512]{1,0:T(8,128)(2,1)S(1)} %get-tuple-element.26.rows_t, ...), custom_call_target="tpu_custom_call" | custom-call | flops 201326592 | bytes 1048576 | tf_op jit(solution)/shard_map/pallas_call | solution.py:125
  38.6 2.1 %collective-permute-start.14 = (bf16[128,128]{1,0:T(8,128)(2,1)S(1)}, bf16[128,128]{1,0:T(8,128)(2,1)S(1)}, u32[]{:S(2)}, u32[]{:S(2)}) collective-permute-start(bf16[128,128]{1,0:T(8,128)(2,1)S(1)} %shard_map.106), channel_id=1, source_target_pairs={{0,8},{4,12},{8,0},{12,4},{1,9},{5,13},{9,1},{13,5},{2,10},{6,14},... | collective-permute-start | bytes 98312 | tf_op jit(solution)/shard_map/ppermute | solution.py:372
  40.7 0.7 %shard_map.103.own = f32[128,128]{1,0:T(8,128)S(1)} custom-call(bf16[128,128]{1,0:T(8,128)(2,1)S(1)} %shard_map.98.query, bf16[128,1024]{1,0:T(8,128)(2,1)S(1)} %get-tuple-element.24.key_t, bf16[1024,128]{1,0:T(8,128)(2,1)S(1)} %get-tuple-element.25.value, bf16[128,512]{1,0:T(8,128)(2,1)S(1)} %get-tuple-element.26.rows_t, ...), custom_call_target="tpu_custom_call" | custom-call | flops 201326592 | bytes 1048576 | tf_op jit(solution)/shard_map/pallas_call | solution.py:125
  41.4 2.4 %collective-permute-done.14.refs_2_ = bf16[128,128]{1,0:T(8,128)(2,1)S(1)} collective-permute-done((bf16[128,128]{1,0:T(8,128)(2,1)S(1)}, bf16[128,128]{1,0:T(8,128)(2,1)S(1)}, u32[]{:S(2)}, u32[]{:S(2)}) %collective-permute-start.14) | collective-permute-done | bytes 32800 | tf_op jit(solution)/shard_map/ppermute | solution.py:372
  43.8 0.1 collective-permute-start.15
  43.9 1.2 %collective-permute-done.15.got = bf16[64,128]{1,0:T(8,128)(2,1)S(1)} collective-permute-done((bf16[64,128]{1,0:T(8,128)(2,1)S(1)}, bf16[64,128]{1,0:T(8,128)(2,1)S(1)}, u32[]{:S(2)}, u32[]{:S(2)}) %collective-permute-start.15) | collective-permute-done | bytes 16416 | tf_op jit(solution)/shard_map/ppermute | solution.py:372
  45.1 0.6 %shard_map.108 = bf16[64,256]{1,0:T(8,128)(2,1)} custom-call(bf16[64,128]{1,0:T(8,128)(2,1)S(1)} %get-tuple-element.29.keep, bf16[64,128]{1,0:T(8,128)(2,1)S(1)} %collective-permute-done.15.got), custom_call_target="tpu_custom_call" | custom-call | bytes 262144 | tf_op jit(solution)/shard_map/pallas_call | solution.py:125
  (6 shorter events, 0.1 us)
Async XLA Ops:
  0.0 21.2 %collective-permute-start = (bf16[256,4096]{1,0:T(8,128)(2,1)}, bf16[256,4096]{1,0:T(8,128)(2,1)S(1)}, u32[]{:S(2)}, u32[]{:S(2)}) collective-permute-start(bf16[256,4096]{1,0:T(8,128)(2,1)} %mine.11), channel_id=1, source_target_pairs={{0,1},{1,0},{2,3},{3,2},{4,5},{5,4},{6,7},{7,6},{8,9},{9,8},{10,11... | collective-permute-start | bytes 6291464 | tf_op jit(solution)/shard_map/ppermute | solution.py:372
  1.6 9.1 %collective-permute-start.2 = (bf16[528,128]{1,0:T(8,128)(2,1)S(1)}, bf16[528,128]{1,0:T(8,128)(2,1)S(1)}, u32[]{:S(2)}, u32[]{:S(2)}) collective-permute-start(bf16[528,128]{1,0:T(8,128)(2,1)S(1)} %get-tuple-element.21.refs_0_), channel_id=1, source_target_pairs={{0,4},{4,8},{8,12},{12,0},{1,5},{5,9},{9,13},{13,1},{2,6},{6,10},{... | collective-permute-start | bytes 405512 | tf_op jit(solution)/shard_map/ppermute | solution.py:372
  4.3 8.6 %collective-permute-start.4 = (bf16[528,128]{1,0:T(8,128)(2,1)S(1)}, bf16[528,128]{1,0:T(8,128)(2,1)S(1)}, u32[]{:S(2)}, u32[]{:S(2)}) collective-permute-start(bf16[528,128]{1,0:T(8,128)(2,1)S(1)} %get-tuple-element.21.refs_0_), channel_id=1, source_target_pairs={{0,12},{4,0},{8,4},{12,8},{1,13},{5,1},{9,5},{13,9},{2,14},{6,2},{... | collective-permute-start | bytes 405512 | tf_op jit(solution)/shard_map/ppermute | solution.py:372
  10.8 7.5 %collective-permute-start.6 = (bf16[528,128]{1,0:T(8,128)(2,1)S(1)}, bf16[528,128]{1,0:T(8,128)(2,1)S(1)}, u32[]{:S(2)}, u32[]{:S(2)}) collective-permute-start(bf16[528,128]{1,0:T(8,128)(2,1)S(1)} %collective-permute-done.2.refs_0_.refs_1_), channel_id=1, source_target_pairs={{0,4},{4,8},{8,12},{12,0},{1,5},{5,9},{9,13},{13,1},{2,6},{6,10},{... | collective-permute-start | bytes 405512 | tf_op jit(solution)/shard_map/ppermute | solution.py:372
  10.8 12.5 %collective-permute-start.3 = (bf16[528,128]{1,0:T(8,128)(2,1)S(1)}, bf16[528,128]{1,0:T(8,128)(2,1)S(1)}, u32[]{:S(2)}, u32[]{:S(2)}) collective-permute-start(bf16[528,128]{1,0:T(8,128)(2,1)S(1)} %collective-permute-done.2.refs_0_.refs_1_), channel_id=1, source_target_pairs={{0,16},{16,0},{1,17},{17,1},{2,18},{18,2},{3,19},{19,3},{4,20},{20... | collective-permute-start | bytes 405512 | tf_op jit(solution)/shard_map/ppermute | solution.py:372
  12.9 12.0 %collective-permute-start.5 = (bf16[528,128]{1,0:T(8,128)(2,1)S(1)}, bf16[528,128]{1,0:T(8,128)(2,1)S(1)}, u32[]{:S(2)}, u32[]{:S(2)}) collective-permute-start(bf16[528,128]{1,0:T(8,128)(2,1)S(1)} %collective-permute-done.4.refs_0_.refs_3_), channel_id=1, source_target_pairs={{0,16},{16,0},{1,17},{17,1},{2,18},{18,2},{3,19},{19,3},{4,20},{20... | collective-permute-start | bytes 405512 | tf_op jit(solution)/shard_map/ppermute | solution.py:372
  18.3 7.7 %collective-permute-start.7 = (bf16[528,128]{1,0:T(8,128)(2,1)S(1)}, bf16[528,128]{1,0:T(8,128)(2,1)S(1)}, u32[]{:S(2)}, u32[]{:S(2)}) collective-permute-start(bf16[528,128]{1,0:T(8,128)(2,1)S(1)} %collective-permute-done.6.refs_0_.refs_2_), channel_id=1, source_target_pairs={{0,16},{16,0},{1,17},{17,1},{2,18},{18,2},{3,19},{19,3},{4,20},{20... | collective-permute-start | bytes 405512 | tf_op jit(solution)/shard_map/ppermute | solution.py:372
  19.8 1.2 %collective-permute-start.1 = (s32[1,1664]{1,0:T(1,128)S(1)}, s32[1,1664]{1,0:T(1,128)S(1)}, u32[]{:S(2)}, u32[]{:S(2)}) collective-permute-start(s32[1,1664]{1,0:T(1,128)S(1)} %get-tuple-element.18.mine), channel_id=1, source_target_pairs={{0,1},{1,0},{2,3},{3,2},{4,5},{5,4},{6,7},{7,6},{8,9},{9,8},{10,11... | collective-permute-start | bytes 19976 | tf_op jit(solution)/shard_map/ppermute | solution.py:372
  21.2 1.6 %copy-start = (bf16[256,4096]{1,0:T(8,128)(2,1)S(1)}, bf16[256,4096]{1,0:T(8,128)(2,1)}, u32[]{:S(2)}) copy-start(bf16[256,4096]{1,0:T(8,128)(2,1)} %mine.11) | copy-start | bytes 6291460
  22.8 1.6 %copy-start.1 = (bf16[256,4096]{1,0:T(8,128)(2,1)S(1)}, bf16[256,4096]{1,0:T(8,128)(2,1)}, u32[]{:S(2)}) copy-start(bf16[256,4096]{1,0:T(8,128)(2,1)} %mine.11) | copy-start | bytes 6291460
  26.2 7.2 %collective-permute-start.9 = (bf16[128,128]{1,0:T(8,128)(2,1)S(1)}, bf16[128,128]{1,0:T(8,128)(2,1)S(1)}, u32[]{:S(2)}, u32[]{:S(2)}) collective-permute-start(bf16[128,128]{1,0:T(8,128)(2,1)S(1)} %shard_map.98.query), channel_id=1, source_target_pairs={{0,4},{4,8},{8,12},{12,0},{1,5},{5,9},{9,13},{13,1},{2,6},{6,10},{... | collective-permute-start | bytes 98312 | tf_op jit(solution)/shard_map/ppermute | solution.py:372
  26.3 6.1 %collective-permute-start.8 = (f32[16,256]{1,0:T(8,128)S(1)}, f32[16,256]{1,0:T(8,128)S(1)}, u32[]{:S(2)}, u32[]{:S(2)}) collective-permute-start(f32[16,256]{1,0:T(8,128)S(1)} %shard_map.101.tally), channel_id=1, source_target_pairs={{0,1},{1,0},{2,3},{3,2},{4,5},{5,4},{6,7},{7,6},{8,9},{9,8},{10,11... | collective-permute-start | bytes 49160 | tf_op jit(solution)/shard_map/ppermute | solution.py:372
  26.5 8.4 %collective-permute-start.11 = (bf16[128,128]{1,0:T(8,128)(2,1)S(1)}, bf16[128,128]{1,0:T(8,128)(2,1)S(1)}, u32[]{:S(2)}, u32[]{:S(2)}) collective-permute-start(bf16[128,128]{1,0:T(8,128)(2,1)S(1)} %shard_map.98.query), channel_id=1, source_target_pairs={{0,12},{4,0},{8,4},{12,8},{1,13},{5,1},{9,5},{13,9},{2,14},{6,2},{... | collective-permute-start | bytes 98312 | tf_op jit(solution)/shard_map/ppermute | solution.py:372
  33.0 4.9 %collective-permute-start.13 = (bf16[128,128]{1,0:T(8,128)(2,1)S(1)}, bf16[128,128]{1,0:T(8,128)(2,1)S(1)}, u32[]{:S(2)}, u32[]{:S(2)}) collective-permute-start(bf16[128,128]{1,0:T(8,128)(2,1)S(1)} %shard_map.98.query), channel_id=1, source_target_pairs={{0,8},{4,12},{8,0},{12,4},{1,9},{5,13},{9,1},{13,5},{2,10},{6,14},... | collective-permute-start | bytes 98312 | tf_op jit(solution)/shard_map/ppermute | solution.py:372
  34.2 7.2 %collective-permute-start.10 = (bf16[128,128]{1,0:T(8,128)(2,1)S(1)}, bf16[128,128]{1,0:T(8,128)(2,1)S(1)}, u32[]{:S(2)}, u32[]{:S(2)}) collective-permute-start(bf16[128,128]{1,0:T(8,128)(2,1)S(1)} %shard_map.104), channel_id=1, source_target_pairs={{0,12},{4,0},{8,4},{12,8},{1,13},{5,1},{9,5},{13,9},{2,14},{6,2},{... | collective-permute-start | bytes 98312 | tf_op jit(solution)/shard_map/ppermute | solution.py:372
  35.6 5.8 %collective-permute-start.12 = (bf16[128,128]{1,0:T(8,128)(2,1)S(1)}, bf16[128,128]{1,0:T(8,128)(2,1)S(1)}, u32[]{:S(2)}, u32[]{:S(2)}) collective-permute-start(bf16[128,128]{1,0:T(8,128)(2,1)S(1)} %shard_map.105), channel_id=1, source_target_pairs={{0,4},{4,8},{8,12},{12,0},{1,5},{5,9},{9,13},{13,1},{2,6},{6,10},{... | collective-permute-start | bytes 98312 | tf_op jit(solution)/shard_map/ppermute | solution.py:372
  38.6 5.2 %collective-permute-start.14 = (bf16[128,128]{1,0:T(8,128)(2,1)S(1)}, bf16[128,128]{1,0:T(8,128)(2,1)S(1)}, u32[]{:S(2)}, u32[]{:S(2)}) collective-permute-start(bf16[128,128]{1,0:T(8,128)(2,1)S(1)} %shard_map.106), channel_id=1, source_target_pairs={{0,8},{4,12},{8,0},{12,4},{1,9},{5,13},{9,1},{13,5},{2,10},{6,14},... | collective-permute-start | bytes 98312 | tf_op jit(solution)/shard_map/ppermute | solution.py:372
  43.8 1.2 %collective-permute-start.15 = (bf16[64,128]{1,0:T(8,128)(2,1)S(1)}, bf16[64,128]{1,0:T(8,128)(2,1)S(1)}, u32[]{:S(2)}, u32[]{:S(2)}) collective-permute-start(bf16[64,128]{1,0:T(8,128)(2,1)S(1)} %get-tuple-element.30), channel_id=1, source_target_pairs={{0,1},{1,0},{2,3},{3,2},{4,5},{5,4},{6,7},{7,6},{8,9},{9,8},{10,11... | collective-permute-start | bytes 49160 | tf_op jit(solution)/shard_map/ppermute | solution.py:372

commit v4 on v3

--- a/solution.py
+++ b/solution.py
@@ -239,7 +239,7 @@
 
 
 def scale_kernel(items, mine, other, hot, tally, tally_other, out):
-    n, lanes, _ = out.shape
+    n, _, lanes = out.shape
     hist_user = mine[:, 2 * items + lanes :]
     events = hist_user.shape[1]
     total = tally[:8] + tally_other[:8]
@@ -252,18 +252,17 @@
     count = jnp.sum(jnp.where(iota(counts.shape, 0) == owner, counts, 0.0), axis=0, keepdims=True)
     inverse = 1.0 / jnp.maximum(count, 1.0)
     user = jnp.concatenate([hist_user, mine[:, :items], other[:, :items]], axis=1).astype(F32)
-    diagonal = iota((lanes, lanes), 0) == iota((lanes, lanes), 1)
-    first = iota((8, lanes), 1) < lanes // 2
+    columns = jnp.transpose(jnp.where(iota(counts.shape, 0) == 0, user, inverse))
+    entry_user, entry_scale = columns[:, :1], columns[:, 1:2]
     near = tally[8:16, :lanes]
     far = pltpu.roll(tally_other[8:16, :lanes], lanes // 2, 1)
-    cand = jnp.where(first, near, far)
+    cand = jnp.where(iota((8, lanes), 1) < lanes // 2, near, far)
     for k in range(n):
-        column = jnp.sum(jnp.where(diagonal, cand[k : k + 1], 0.0), axis=1, keepdims=True)
-        out[k] = jnp.where(column == user, inverse, 0.0)
-
-
-def project_kernel(hist_emb, key_weight, value_weight, key_t, value, emb, keys, values, sems):
-    width = value.shape[1]
+        out[k] = jnp.where(entry_user == cand[k : k + 1], entry_scale, 0.0)
+
+
+def project_kernel(hist_emb, key_weight, value_weight, key, value_t, emb, keys, values, sems):
+    width = key.shape[1]
     columns = pl.ds(col_start(width), width)
     copies = [
         pltpu.make_async_copy(key_weight.at[:, columns], keys, sems.at[0]),
@@ -274,8 +273,8 @@
         copy.start()
     for copy in copies:
         copy.wait()
-    value[...] = dot(emb[...], values[...]).astype(BF16)
-    key_t[...] = jnp.transpose(dot(emb[...], keys[...]).astype(BF16))
+    key[...] = dot(emb[...], keys[...]).astype(BF16)
+    value_t[...] = jnp.transpose(dot(emb[...], values[...]).astype(BF16))
 
 
 def embed_own_kernel(mine, other, block, total):
@@ -314,8 +313,9 @@
     feats[...] = (dot(pick[:, :items], mine[:, at]) + dot(pick[:, items:], other[:, at])).astype(BF16)
 
 
-def query_kernel(part, feats, block, query):
+def query_kernel(part, feats, block, query, query_t):
     query[...] = (part[...] + dot(feats[...], block[: feats.shape[1]])).astype(BF16)
+    query_t[...] = jnp.transpose(query[...])
 
 
 def embed_last_kernel(n, groups, k, step, mine, other, total, block, rows, rows_t):
@@ -326,25 +326,27 @@
     rows_t[...] = jnp.transpose(rows[...])
 
 
-def attend_kernel(k, query, key_t, value, rows_t, rows, scale, out):
-    cands, width = query.shape
+def attend_kernel(k, query_t, key, value_t, rows, rows_t, scale, out):
+    width, cands = query_t.shape
     heads = width // HS
-    lane = iota((cands, width), 1) // HS
-    part = query[...] * (0.5 * HS ** -0.5)
+    row = iota((width, cands), 0) // HS
+    part = query_t[...] * (0.5 * HS ** -0.5)
     zero = jnp.zeros_like(part)
-    split = jnp.concatenate([jnp.where(lane == h, part, zero) for h in range(heads)], axis=0)
-    events = key_t.shape[1]
-
-    def weigh(keys, factor):
-        half = dot(split, keys)
-        gated = half + half * jnp.tanh(half)
-        return (gated * jnp.concatenate([factor] * heads, axis=0)).astype(BF16)
-
-    mixed = dot(weigh(key_t[...], scale[k, :, :events]), value[...])
-    mixed = mixed + dot(weigh(rows_t[...], scale[k, :, events:]), rows[...])
-    total = jnp.zeros((cands, width), F32)
+    split = jnp.concatenate([jnp.where(row == h, part, zero) for h in range(heads)], axis=1)
+    events = key.shape[0]
+
+    mixed = jnp.zeros((width, heads * cands), F32)
+    for keys, values, base in ((key, value_t, 0), (rows, rows_t, events)):
+        step = math.gcd(keys.shape[0], 512)
+        for at in range(0, keys.shape[0], step):
+            half = dot(keys[at : at + step], split)
+            gated = half + half * jnp.tanh(half)
+            factor = scale[k, base + at : base + at + step]
+            weight = (gated * jnp.concatenate([factor] * heads, axis=1)).astype(BF16)
+            mixed = mixed + dot(values[:, at : at + step], weight)
+    total = jnp.zeros((width, cands), F32)
     for h in range(heads):
-        total = total + jnp.where(lane == h, mixed[h * cands : (h + 1) * cands], 0.0)
+        total = total + jnp.where(row == h, mixed[:, h * cands : (h + 1) * cands], 0.0)
     out[...] = total.astype(out.dtype)
 
 
@@ -354,7 +356,7 @@
     for part in parts:
         total = total + part[...].astype(F32)
     gate = query[...].astype(F32)
-    scored = (gate * jax.nn.sigmoid(gate) * total).astype(BF16)
+    scored = (gate * jax.nn.sigmoid(gate) * jnp.transpose(total)).astype(BF16)
     half = keep.shape[0]
     keep[...] = scored[:half]
     send[...] = scored[half:]
@@ -422,9 +424,9 @@
     other = shift(mine, "rep", 1)
     keys = events + 2 * items
     hot, pick = call(users_kernel, (shape((USERS, keys), BF16), shape((cands, 2 * items), BF16)), (mine, other))
-    key_t, value = call(
+    key, value_t = call(
         project_kernel,
-        (shape((width, events), BF16), shape((events, width), BF16)),
+        (shape((events, width), BF16), shape((width, events), BF16)),
         (hist_emb, key_weight, value_weight),
         flops=4 * events * dim * width,
         bytes_accessed=4 << 20,
@@ -446,7 +448,7 @@
     tally = call(tally_kernel, shape((16, USERS), F32), (own_share, *[along[k] for k in range(1, n)]))
     scale = call(
         functools.partial(scale_kernel, items),
-        shape((n, cands, keys), F32),
+        shape((n, keys, cands), F32),
         (mine, other, hot, tally, shift(tally, "rep", 1)),
         bytes_accessed=4 << 20,
     )
@@ -471,7 +473,12 @@
         (item_feats, feats_other, pick, total),
         flops=4 * cands * items * (share + 6 * width),
     )
-    query = call(query_kernel, shape((cands, width), BF16), (part, feats, arrived), flops=2 * cands * share * width)
+    query, query_t = call(
+        query_kernel,
+        (shape((cands, width), BF16), shape((width, cands), BF16)),
+        (part, feats, arrived),
+        flops=2 * cands * share * width,
+    )
     rows, rows_t = call(
         functools.partial(embed_last_kernel, n, groups, k, step),
         (shape((2 * items, width), BF16), shape((width, 2 * items), BF16)),
@@ -479,18 +486,18 @@
         flops=4 * items * share * width,
         bytes_accessed=2 << 20,
     )
-    queries = {k: shift(query, "hist", k) for k in order}
+    queries = {k: shift(query_t, "hist", k) for k in order}
 
     def attend(k, block, dtype):
         return call(
             functools.partial(attend_kernel, k),
-            shape((cands, width), dtype),
-            (block, key_t, value, rows_t, rows, scale),
+            shape((width, cands), dtype),
+            (block, key, value_t, rows, rows_t, scale),
             flops=8 * cands * keys * width,
             bytes_accessed=1 << 20,
         )
 
-    own = attend(0, query, F32)
+    own = attend(0, query_t, F32)
     parts = [shift(attend(k, queries[k], BF16), "hist", n - k) for k in order]
     keep, send = call(
         gate_kernel, (shape((cands // 2, width), BF16), shape((cands // 2, width), BF16)), (query, own, *parts)

time: 45.9 us -> 44.9 us (0.978)
  waiting for transfers between devices: 14.3 us -> 12.1 us
  starting transfers between devices: 18.4 us -> 19.2 us
    ppermute x16, waiting for transfers between devices: 14.3 us -> 12.1 us  [shift(): lax.ppermute(value, axis, [(i, (i + k) % count) for i in range(count)])]
    ppermute x16, starting transfers between devices: 18.4 us -> 19.2 us  [shift(): lax.ppermute(value, axis, [(i, (i + k) % count) for i in range(count)])]
  transfers between devices with their start and end apart: 16 -> 16, of which waited for: 7 -> 7; matrix products, arithmetic and copies ran while one was open for 0% -> 0% of each run, Pallas kernels for 20% -> 21%
where the time goes in v4:
time: 44.9 us; the launch traced here: 44.6 us
  starting transfers between devices  19.2 us (43%)
  waiting for transfers between devices  12.1 us (27%)
  Pallas kernels  10.4 us (23%)
  local copies, waits for them, and re-layouts  2.74 us (6%)
    ppermute x16, starting transfers between devices, shift(): lax.ppermute(value, axis, [(i, (i + k) % count) for i in range(count)])  19.2 us
    ppermute x16, waiting for transfers between devices, shift(): lax.ppermute(value, axis, [(i, (i + k) % count) for i in range(count)])  12.1 us
    pallas_call x18, Pallas kernels, call(): pl.pallas_call(kernel, out_shape=outs, in_specs=specs or [VM] * len(args)...  10.4 us
    unnamed x4, local copies, waits for them, and re-layouts  2.74 us
  transfers between devices with their start and end apart: 16, of which 7 were waited for; matrix products, arithmetic and copies ran while one was open for 0% of the time, Pallas kernels for 21%

profile of v4, /device:TPU:0, one launch (start us, length us, event | category | flops | bytes accessed | tf_op | source)
XLA Modules:
  0.0 44.6 jit_solution(11250590177959700888)
XLA Ops:
  0.0 0.5 %collective-permute-start = (bf16[256,4096]{1,0:T(8,128)(2,1)}, bf16[256,4096]{1,0:T(8,128)(2,1)S(1)}, u32[]{:S(2)}, u32[]{:S(2)}) collective-permute-start(bf16[256,4096]{1,0:T(8,128)(2,1)} %mine.11), channel_id=1, source_target_pairs={{0,1},{1,0},{2,3},{3,2},{4,5},{5,4},{6,7},{7,6},{8,9},{9,8},{10,11... | collective-permute-start | bytes 6291464 | tf_op jit(solution)/shard_map/ppermute | solution.py:374
  0.5 1.1 %shard_map.91 = (bf16[1024,128]{1,0:T(8,128)(2,1)S(1)}, bf16[528,128]{1,0:T(8,128)(2,1)S(1)}, s32[1,1664]{1,0:T(1,128)S(1)}) custom-call(bf16[1024,256]{1,0:T(8,128)(2,1)} %adapter.1, s32[1,256]{1,0:T(1,128)} %bitcast.5, s32[1,256]{1,0:T(1,128)} %bitcast.6, s32[1,64]{1,0:T(1,128)} %bitcast.7, s32[1,1024]{1,0:T(1,128)} %bitcast.4), custom_call_target="tpu_custom_call" | custom-call | bytes 262144 | tf_op jit(solution)/shard_map/pallas_call | solution.py:125
  1.6 2.6 %collective-permute-start.2 = (bf16[528,128]{1,0:T(8,128)(2,1)S(1)}, bf16[528,128]{1,0:T(8,128)(2,1)S(1)}, u32[]{:S(2)}, u32[]{:S(2)}) collective-permute-start(bf16[528,128]{1,0:T(8,128)(2,1)S(1)} %get-tuple-element.23.refs_0_), channel_id=1, source_target_pairs={{0,4},{4,8},{8,12},{12,0},{1,5},{5,9},{9,13},{13,1},{2,6},{6,10},{... | collective-permute-start | bytes 405512 | tf_op jit(solution)/shard_map/ppermute | solution.py:374
  4.3 2.1 %collective-permute-start.4 = (bf16[528,128]{1,0:T(8,128)(2,1)S(1)}, bf16[528,128]{1,0:T(8,128)(2,1)S(1)}, u32[]{:S(2)}, u32[]{:S(2)}) collective-permute-start(bf16[528,128]{1,0:T(8,128)(2,1)S(1)} %get-tuple-element.23.refs_0_), channel_id=1, source_target_pairs={{0,12},{4,0},{8,4},{12,8},{1,13},{5,1},{9,5},{13,9},{2,14},{6,2},{... | collective-permute-start | bytes 405512 | tf_op jit(solution)/shard_map/ppermute | solution.py:374
  6.3 4.4 %collective-permute-done.2.refs_0_.refs_1_ = bf16[528,128]{1,0:T(8,128)(2,1)S(1)} collective-permute-done((bf16[528,128]{1,0:T(8,128)(2,1)S(1)}, bf16[528,128]{1,0:T(8,128)(2,1)S(1)}, u32[]{:S(2)}, u32[]{:S(2)}) %collective-permute-start.2) | collective-permute-done | bytes 135200 | tf_op jit(solution)/shard_map/ppermute | solution.py:374
  10.8 0.0 collective-permute-start.6
  10.8 1.7 %collective-permute-start.3 = (bf16[528,128]{1,0:T(8,128)(2,1)S(1)}, bf16[528,128]{1,0:T(8,128)(2,1)S(1)}, u32[]{:S(2)}, u32[]{:S(2)}) collective-permute-start(bf16[528,128]{1,0:T(8,128)(2,1)S(1)} %collective-permute-done.2.refs_0_.refs_1_), channel_id=1, source_target_pairs={{0,16},{16,0},{1,17},{17,1},{2,18},{18,2},{3,19},{19,3},{4,20},{20... | collective-permute-start | bytes 405512 | tf_op jit(solution)/shard_map/ppermute | solution.py:374
  12.5 0.4 collective-permute-done.4.refs_0_.refs_3_
  12.9 1.5 %collective-permute-start.5 = (bf16[528,128]{1,0:T(8,128)(2,1)S(1)}, bf16[528,128]{1,0:T(8,128)(2,1)S(1)}, u32[]{:S(2)}, u32[]{:S(2)}) collective-permute-start(bf16[528,128]{1,0:T(8,128)(2,1)S(1)} %collective-permute-done.4.refs_0_.refs_3_), channel_id=1, source_target_pairs={{0,16},{16,0},{1,17},{17,1},{2,18},{18,2},{3,19},{19,3},{4,20},{20... | collective-permute-start | bytes 405512 | tf_op jit(solution)/shard_map/ppermute | solution.py:374
  14.4 3.9 %collective-permute-done.6.refs_0_.refs_2_ = bf16[528,128]{1,0:T(8,128)(2,1)S(1)} collective-permute-done((bf16[528,128]{1,0:T(8,128)(2,1)S(1)}, bf16[528,128]{1,0:T(8,128)(2,1)S(1)}, u32[]{:S(2)}, u32[]{:S(2)}) %collective-permute-start.6) | collective-permute-done | bytes 135200 | tf_op jit(solution)/shard_map/ppermute | solution.py:374
  18.3 1.5 %collective-permute-start.7 = (bf16[528,128]{1,0:T(8,128)(2,1)S(1)}, bf16[528,128]{1,0:T(8,128)(2,1)S(1)}, u32[]{:S(2)}, u32[]{:S(2)}) collective-permute-start(bf16[528,128]{1,0:T(8,128)(2,1)S(1)} %collective-permute-done.6.refs_0_.refs_2_), channel_id=1, source_target_pairs={{0,16},{16,0},{1,17},{17,1},{2,18},{18,2},{3,19},{19,3},{4,20},{20... | collective-permute-start | bytes 405512 | tf_op jit(solution)/shard_map/ppermute | solution.py:374
  19.8 0.0 collective-permute-start.1
  19.8 1.2 %collective-permute-done.1.other = s32[1,1664]{1,0:T(1,128)S(1)} collective-permute-done((s32[1,1664]{1,0:T(1,128)S(1)}, s32[1,1664]{1,0:T(1,128)S(1)}, u32[]{:S(2)}, u32[]{:S(2)}) %collective-permute-start.1) | collective-permute-done | bytes 6688 | tf_op jit(solution)/shard_map/ppermute | solution.py:374
  21.0 0.2 shard_map.92
  21.2 0.0 collective-permute-done.other
  21.2 0.0 copy-start
  21.2 1.6 %copy-done = bf16[256,4096]{1,0:T(8,128)(2,1)S(1)} copy-done((bf16[256,4096]{1,0:T(8,128)(2,1)S(1)}, bf16[256,4096]{1,0:T(8,128)(2,1)}, u32[]{:S(2)}) %copy-start) | copy-done | bytes 2097176
  22.8 0.4 shard_map.93.total
  23.2 0.0 collective-permute-done.3.refs_1_
  23.3 1.2 %copy-done.1 = bf16[256,4096]{1,0:T(8,128)(2,1)S(1)} copy-done((bf16[256,4096]{1,0:T(8,128)(2,1)S(1)}, bf16[256,4096]{1,0:T(8,128)(2,1)}, u32[]{:S(2)}) %copy-start.1) | copy-done | bytes 2097176
  24.4 0.4 shard_map.94.total
  24.8 0.4 shard_map.95.total
  25.3 0.3 shard_map.96.total
  25.6 0.4 shard_map.97
  26.0 0.2 shard_map.98
  26.3 1.0 %collective-permute-start.13 = (bf16[128,128]{1,0:T(8,128)(2,1)S(1)}, bf16[128,128]{1,0:T(8,128)(2,1)S(1)}, u32[]{:S(2)}, u32[]{:S(2)}) collective-permute-start(bf16[128,128]{1,0:T(8,128)(2,1)S(1)} %get-tuple-element.27.query_t), channel_id=1, source_target_pairs={{0,8},{4,12},{8,0},{12,4},{1,9},{5,13},{9,1},{13,5},{2,10},{6,14},... | collective-permute-start | bytes 98312 | tf_op jit(solution)/shard_map/ppermute | solution.py:374
  27.3 0.1 collective-permute-start.8
  27.3 1.3 %collective-permute-start.11 = (bf16[128,128]{1,0:T(8,128)(2,1)S(1)}, bf16[128,128]{1,0:T(8,128)(2,1)S(1)}, u32[]{:S(2)}, u32[]{:S(2)}) collective-permute-start(bf16[128,128]{1,0:T(8,128)(2,1)S(1)} %get-tuple-element.27.query_t), channel_id=1, source_target_pairs={{0,12},{4,0},{8,4},{12,8},{1,13},{5,1},{9,5},{13,9},{2,14},{6,2},{... | collective-permute-start | bytes 98312 | tf_op jit(solution)/shard_map/ppermute | solution.py:374
  28.6 2.1 %shard_map.99 = (bf16[1024,128]{1,0:T(8,128)(2,1)S(1)}, bf16[128,1024]{1,0:T(8,128)(2,1)S(1)}) custom-call(bf16[1024,512]{1,0:T(8,128)(2,1)} %hist_emb.1, bf16[512,256]{1,0:T(8,128)(2,1)} %key_weight.1, bf16[512,256]{1,0:T(8,128)(2,1)} %value_weight.1), custom_call_target="tpu_custom_call" | custom-call | flops 268435456 | bytes 4194304 | tf_op jit(solution)/shard_map/pallas_call | solution.py:125
  30.8 0.0 collective-permute-done.8.tally_other
  30.8 1.0 %shard_map.102.scale = f32[4,1536,128]{2,1,0:T(8,128)S(1)} custom-call(s32[1,1664]{1,0:T(1,128)S(1)} %get-tuple-element.20.mine, s32[1,1664]{1,0:T(1,128)S(1)} %collective-permute-done.1.other, bf16[256,1536]{1,0:T(8,128)(2,1)S(1)} %get-tuple-element.32.hot, f32[16,256]{1,0:T(8,128)S(1)} %shard_map.101.tally, f32[16,256]{1,0:T(8,128)S(1)} %collective-permute-done.8.tally_other), custom_call_target="tpu_custom_call" | custom-call | bytes 4194304 | tf_op jit(solution)/shard_map/pallas_call | solution.py:125
  31.8 0.8 %collective-permute-start.9 = (bf16[128,128]{1,0:T(8,128)(2,1)S(1)}, bf16[128,128]{1,0:T(8,128)(2,1)S(1)}, u32[]{:S(2)}, u32[]{:S(2)}) collective-permute-start(bf16[128,128]{1,0:T(8,128)(2,1)S(1)} %get-tuple-element.27.query_t), channel_id=1, source_target_pairs={{0,4},{4,8},{8,12},{12,0},{1,5},{5,9},{9,13},{13,1},{2,6},{6,10},{... | collective-permute-start | bytes 98312 | tf_op jit(solution)/shard_map/ppermute | solution.py:374
  32.7 0.4 shard_map.100
  33.1 0.0 collective-permute-done.13.query_t
  33.1 0.6 %shard_map.106 = bf16[128,128]{1,0:T(8,128)(2,1)S(1)} custom-call(bf16[128,128]{1,0:T(8,128)(2,1)S(1)} %collective-permute-done.13.query_t, bf16[1024,128]{1,0:T(8,128)(2,1)S(1)} %get-tuple-element.28.key, bf16[128,1024]{1,0:T(8,128)(2,1)S(1)} %get-tuple-element.29.value_t, bf16[512,128]{1,0:T(8,128)(2,1)S(1)} %get-tuple-element.30.rows, ...), custom_call_target="tpu_custom_call" | custom-call | flops 201326592 | bytes 1048576 | tf_op jit(solution)/shard_map/pallas_call | solution.py:125
  33.7 2.1 %collective-permute-start.14 = (bf16[128,128]{1,0:T(8,128)(2,1)S(1)}, bf16[128,128]{1,0:T(8,128)(2,1)S(1)}, u32[]{:S(2)}, u32[]{:S(2)}) collective-permute-start(bf16[128,128]{1,0:T(8,128)(2,1)S(1)} %shard_map.106), channel_id=1, source_target_pairs={{0,8},{4,12},{8,0},{12,4},{1,9},{5,13},{9,1},{13,5},{2,10},{6,14},... | collective-permute-start | bytes 98312 | tf_op jit(solution)/shard_map/ppermute | solution.py:374
  35.8 0.0 collective-permute-done.11.query_t
  35.8 0.6 %shard_map.105 = bf16[128,128]{1,0:T(8,128)(2,1)S(1)} custom-call(bf16[128,128]{1,0:T(8,128)(2,1)S(1)} %collective-permute-done.11.query_t, bf16[1024,128]{1,0:T(8,128)(2,1)S(1)} %get-tuple-element.28.key, bf16[128,1024]{1,0:T(8,128)(2,1)S(1)} %get-tuple-element.29.value_t, bf16[512,128]{1,0:T(8,128)(2,1)S(1)} %get-tuple-element.30.rows, ...), custom_call_target="tpu_custom_call" | custom-call | flops 201326592 | bytes 1048576 | tf_op jit(solution)/shard_map/pallas_call | solution.py:125
  36.4 1.6 %collective-permute-start.12 = (bf16[128,128]{1,0:T(8,128)(2,1)S(1)}, bf16[128,128]{1,0:T(8,128)(2,1)S(1)}, u32[]{:S(2)}, u32[]{:S(2)}) collective-permute-start(bf16[128,128]{1,0:T(8,128)(2,1)S(1)} %shard_map.105), channel_id=1, source_target_pairs={{0,4},{4,8},{8,12},{12,0},{1,5},{5,9},{9,13},{13,1},{2,6},{6,10},{... | collective-permute-start | bytes 98312 | tf_op jit(solution)/shard_map/ppermute | solution.py:374
  38.1 0.6 %shard_map.104 = bf16[128,128]{1,0:T(8,128)(2,1)S(1)} custom-call(bf16[128,128]{1,0:T(8,128)(2,1)S(1)} %collective-permute-done.9.query_t, bf16[1024,128]{1,0:T(8,128)(2,1)S(1)} %get-tuple-element.28.key, bf16[128,1024]{1,0:T(8,128)(2,1)S(1)} %get-tuple-element.29.value_t, bf16[512,128]{1,0:T(8,128)(2,1)S(1)} %get-tuple-element.30.rows, ...), custom_call_target="tpu_custom_call" | custom-call | flops 201326592 | bytes 1048576 | tf_op jit(solution)/shard_map/pallas_call | solution.py:125
  38.7 2.3 %collective-permute-start.10 = (bf16[128,128]{1,0:T(8,128)(2,1)S(1)}, bf16[128,128]{1,0:T(8,128)(2,1)S(1)}, u32[]{:S(2)}, u32[]{:S(2)}) collective-permute-start(bf16[128,128]{1,0:T(8,128)(2,1)S(1)} %shard_map.104), channel_id=1, source_target_pairs={{0,12},{4,0},{8,4},{12,8},{1,13},{5,1},{9,5},{13,9},{2,14},{6,2},{... | collective-permute-start | bytes 98312 | tf_op jit(solution)/shard_map/ppermute | solution.py:374
  41.0 0.6 %shard_map.103.own = f32[128,128]{1,0:T(8,128)S(1)} custom-call(bf16[128,128]{1,0:T(8,128)(2,1)S(1)} %get-tuple-element.27.query_t, bf16[1024,128]{1,0:T(8,128)(2,1)S(1)} %get-tuple-element.28.key, bf16[128,1024]{1,0:T(8,128)(2,1)S(1)} %get-tuple-element.29.value_t, bf16[512,128]{1,0:T(8,128)(2,1)S(1)} %get-tuple-element.30.rows, ...), custom_call_target="tpu_custom_call" | custom-call | flops 201326592 | bytes 1048576 | tf_op jit(solution)/shard_map/pallas_call | solution.py:125
  41.6 0.7 %collective-permute-done.12.refs_1_ = bf16[128,128]{1,0:T(8,128)(2,1)S(1)} collective-permute-done((bf16[128,128]{1,0:T(8,128)(2,1)S(1)}, bf16[128,128]{1,0:T(8,128)(2,1)S(1)}, u32[]{:S(2)}, u32[]{:S(2)}) %collective-permute-start.12) | collective-permute-done | bytes 32800 | tf_op jit(solution)/shard_map/ppermute | solution.py:374
  42.3 0.4 collective-permute-done.10.refs_0_
  42.7 0.1 shard_map.107
  42.8 0.1 collective-permute-start.15
  42.8 1.2 %collective-permute-done.15.got = bf16[64,128]{1,0:T(8,128)(2,1)S(1)} collective-permute-done((bf16[64,128]{1,0:T(8,128)(2,1)S(1)}, bf16[64,128]{1,0:T(8,128)(2,1)S(1)}, u32[]{:S(2)}, u32[]{:S(2)}) %collective-permute-start.15) | collective-permute-done | bytes 16416 | tf_op jit(solution)/shard_map/ppermute | solution.py:374
  44.0 0.6 %shard_map.108 = bf16[64,256]{1,0:T(8,128)(2,1)} custom-call(bf16[64,128]{1,0:T(8,128)(2,1)S(1)} %get-tuple-element.33.keep, bf16[64,128]{1,0:T(8,128)(2,1)S(1)} %collective-permute-done.15.got), custom_call_target="tpu_custom_call" | custom-call | bytes 262144 | tf_op jit(solution)/shard_map/pallas_call | solution.py:125
  (6 shorter events, 0.0 us)
Async XLA Ops:
  0.0 21.2 %collective-permute-start = (bf16[256,4096]{1,0:T(8,128)(2,1)}, bf16[256,4096]{1,0:T(8,128)(2,1)S(1)}, u32[]{:S(2)}, u32[]{:S(2)}) collective-permute-start(bf16[256,4096]{1,0:T(8,128)(2,1)} %mine.11), channel_id=1, source_target_pairs={{0,1},{1,0},{2,3},{3,2},{4,5},{5,4},{6,7},{7,6},{8,9},{9,8},{10,11... | collective-permute-start | bytes 6291464 | tf_op jit(solution)/shard_map/ppermute | solution.py:374
  1.6 9.1 %collective-permute-start.2 = (bf16[528,128]{1,0:T(8,128)(2,1)S(1)}, bf16[528,128]{1,0:T(8,128)(2,1)S(1)}, u32[]{:S(2)}, u32[]{:S(2)}) collective-permute-start(bf16[528,128]{1,0:T(8,128)(2,1)S(1)} %get-tuple-element.23.refs_0_), channel_id=1, source_target_pairs={{0,4},{4,8},{8,12},{12,0},{1,5},{5,9},{9,13},{13,1},{2,6},{6,10},{... | collective-permute-start | bytes 405512 | tf_op jit(solution)/shard_map/ppermute | solution.py:374
  4.3 8.6 %collective-permute-start.4 = (bf16[528,128]{1,0:T(8,128)(2,1)S(1)}, bf16[528,128]{1,0:T(8,128)(2,1)S(1)}, u32[]{:S(2)}, u32[]{:S(2)}) collective-permute-start(bf16[528,128]{1,0:T(8,128)(2,1)S(1)} %get-tuple-element.23.refs_0_), channel_id=1, source_target_pairs={{0,12},{4,0},{8,4},{12,8},{1,13},{5,1},{9,5},{13,9},{2,14},{6,2},{... | collective-permute-start | bytes 405512 | tf_op jit(solution)/shard_map/ppermute | solution.py:374
  10.8 7.5 %collective-permute-start.6 = (bf16[528,128]{1,0:T(8,128)(2,1)S(1)}, bf16[528,128]{1,0:T(8,128)(2,1)S(1)}, u32[]{:S(2)}, u32[]{:S(2)}) collective-permute-start(bf16[528,128]{1,0:T(8,128)(2,1)S(1)} %collective-permute-done.2.refs_0_.refs_1_), channel_id=1, source_target_pairs={{0,4},{4,8},{8,12},{12,0},{1,5},{5,9},{9,13},{13,1},{2,6},{6,10},{... | collective-permute-start | bytes 405512 | tf_op jit(solution)/shard_map/ppermute | solution.py:374
  10.8 12.5 %collective-permute-start.3 = (bf16[528,128]{1,0:T(8,128)(2,1)S(1)}, bf16[528,128]{1,0:T(8,128)(2,1)S(1)}, u32[]{:S(2)}, u32[]{:S(2)}) collective-permute-start(bf16[528,128]{1,0:T(8,128)(2,1)S(1)} %collective-permute-done.2.refs_0_.refs_1_), channel_id=1, source_target_pairs={{0,16},{16,0},{1,17},{17,1},{2,18},{18,2},{3,19},{19,3},{4,20},{20... | collective-permute-start | bytes 405512 | tf_op jit(solution)/shard_map/ppermute | solution.py:374
  12.9 12.0 %collective-permute-start.5 = (bf16[528,128]{1,0:T(8,128)(2,1)S(1)}, bf16[528,128]{1,0:T(8,128)(2,1)S(1)}, u32[]{:S(2)}, u32[]{:S(2)}) collective-permute-start(bf16[528,128]{1,0:T(8,128)(2,1)S(1)} %collective-permute-done.4.refs_0_.refs_3_), channel_id=1, source_target_pairs={{0,16},{16,0},{1,17},{17,1},{2,18},{18,2},{3,19},{19,3},{4,20},{20... | collective-permute-start | bytes 405512 | tf_op jit(solution)/shard_map/ppermute | solution.py:374
  18.3 7.7 %collective-permute-start.7 = (bf16[528,128]{1,0:T(8,128)(2,1)S(1)}, bf16[528,128]{1,0:T(8,128)(2,1)S(1)}, u32[]{:S(2)}, u32[]{:S(2)}) collective-permute-start(bf16[528,128]{1,0:T(8,128)(2,1)S(1)} %collective-permute-done.6.refs_0_.refs_2_), channel_id=1, source_target_pairs={{0,16},{16,0},{1,17},{17,1},{2,18},{18,2},{3,19},{19,3},{4,20},{20... | collective-permute-start | bytes 405512 | tf_op jit(solution)/shard_map/ppermute | solution.py:374
  19.8 1.2 %collective-permute-start.1 = (s32[1,1664]{1,0:T(1,128)S(1)}, s32[1,1664]{1,0:T(1,128)S(1)}, u32[]{:S(2)}, u32[]{:S(2)}) collective-permute-start(s32[1,1664]{1,0:T(1,128)S(1)} %get-tuple-element.20.mine), channel_id=1, source_target_pairs={{0,1},{1,0},{2,3},{3,2},{4,5},{5,4},{6,7},{7,6},{8,9},{9,8},{10,11... | collective-permute-start | bytes 19976 | tf_op jit(solution)/shard_map/ppermute | solution.py:374
  21.2 1.6 %copy-start = (bf16[256,4096]{1,0:T(8,128)(2,1)S(1)}, bf16[256,4096]{1,0:T(8,128)(2,1)}, u32[]{:S(2)}) copy-start(bf16[256,4096]{1,0:T(8,128)(2,1)} %mine.11) | copy-start | bytes 6291460
  22.8 1.6 %copy-start.1 = (bf16[256,4096]{1,0:T(8,128)(2,1)S(1)}, bf16[256,4096]{1,0:T(8,128)(2,1)}, u32[]{:S(2)}) copy-start(bf16[256,4096]{1,0:T(8,128)(2,1)} %mine.11) | copy-start | bytes 6291460
  26.3 6.8 %collective-permute-start.13 = (bf16[128,128]{1,0:T(8,128)(2,1)S(1)}, bf16[128,128]{1,0:T(8,128)(2,1)S(1)}, u32[]{:S(2)}, u32[]{:S(2)}) collective-permute-start(bf16[128,128]{1,0:T(8,128)(2,1)S(1)} %get-tuple-element.27.query_t), channel_id=1, source_target_pairs={{0,8},{4,12},{8,0},{12,4},{1,9},{5,13},{9,1},{13,5},{2,10},{6,14},... | collective-permute-start | bytes 98312 | tf_op jit(solution)/shard_map/ppermute | solution.py:374
  27.3 3.5 %collective-permute-start.8 = (f32[16,256]{1,0:T(8,128)S(1)}, f32[16,256]{1,0:T(8,128)S(1)}, u32[]{:S(2)}, u32[]{:S(2)}) collective-permute-start(f32[16,256]{1,0:T(8,128)S(1)} %shard_map.101.tally), channel_id=1, source_target_pairs={{0,1},{1,0},{2,3},{3,2},{4,5},{5,4},{6,7},{7,6},{8,9},{9,8},{10,11... | collective-permute-start | bytes 49160 | tf_op jit(solution)/shard_map/ppermute | solution.py:374
  27.3 8.5 %collective-permute-start.11 = (bf16[128,128]{1,0:T(8,128)(2,1)S(1)}, bf16[128,128]{1,0:T(8,128)(2,1)S(1)}, u32[]{:S(2)}, u32[]{:S(2)}) collective-permute-start(bf16[128,128]{1,0:T(8,128)(2,1)S(1)} %get-tuple-element.27.query_t), channel_id=1, source_target_pairs={{0,12},{4,0},{8,4},{12,8},{1,13},{5,1},{9,5},{13,9},{2,14},{6,2},{... | collective-permute-start | bytes 98312 | tf_op jit(solution)/shard_map/ppermute | solution.py:374
  31.8 6.2 %collective-permute-start.9 = (bf16[128,128]{1,0:T(8,128)(2,1)S(1)}, bf16[128,128]{1,0:T(8,128)(2,1)S(1)}, u32[]{:S(2)}, u32[]{:S(2)}) collective-permute-start(bf16[128,128]{1,0:T(8,128)(2,1)S(1)} %get-tuple-element.27.query_t), channel_id=1, source_target_pairs={{0,4},{4,8},{8,12},{12,0},{1,5},{5,9},{9,13},{13,1},{2,6},{6,10},{... | collective-permute-start | bytes 98312 | tf_op jit(solution)/shard_map/ppermute | solution.py:374
  33.7 7.9 %collective-permute-start.14 = (bf16[128,128]{1,0:T(8,128)(2,1)S(1)}, bf16[128,128]{1,0:T(8,128)(2,1)S(1)}, u32[]{:S(2)}, u32[]{:S(2)}) collective-permute-start(bf16[128,128]{1,0:T(8,128)(2,1)S(1)} %shard_map.106), channel_id=1, source_target_pairs={{0,8},{4,12},{8,0},{12,4},{1,9},{5,13},{9,1},{13,5},{2,10},{6,14},... | collective-permute-start | bytes 98312 | tf_op jit(solution)/shard_map/ppermute | solution.py:374
  36.4 5.9 %collective-permute-start.12 = (bf16[128,128]{1,0:T(8,128)(2,1)S(1)}, bf16[128,128]{1,0:T(8,128)(2,1)S(1)}, u32[]{:S(2)}, u32[]{:S(2)}) collective-permute-start(bf16[128,128]{1,0:T(8,128)(2,1)S(1)} %shard_map.105), channel_id=1, source_target_pairs={{0,4},{4,8},{8,12},{12,0},{1,5},{5,9},{9,13},{13,1},{2,6},{6,10},{... | collective-permute-start | bytes 98312 | tf_op jit(solution)/shard_map/ppermute | solution.py:374
  38.7 4.0 %collective-permute-start.10 = (bf16[128,128]{1,0:T(8,128)(2,1)S(1)}, bf16[128,128]{1,0:T(8,128)(2,1)S(1)}, u32[]{:S(2)}, u32[]{:S(2)}) collective-permute-start(bf16[128,128]{1,0:T(8,128)(2,1)S(1)} %shard_map.104), channel_id=1, source_target_pairs={{0,12},{4,0},{8,4},{12,8},{1,13},{5,1},{9,5},{13,9},{2,14},{6,2},{... | collective-permute-start | bytes 98312 | tf_op jit(solution)/shard_map/ppermute | solution.py:374
  42.8 1.2 %collective-permute-start.15 = (bf16[64,128]{1,0:T(8,128)(2,1)S(1)}, bf16[64,128]{1,0:T(8,128)(2,1)S(1)}, u32[]{:S(2)}, u32[]{:S(2)}) collective-permute-start(bf16[64,128]{1,0:T(8,128)(2,1)S(1)} %get-tuple-element.34), channel_id=1, source_target_pairs={{0,1},{1,0},{2,3},{3,2},{4,5},{5,4},{6,7},{7,6},{8,9},{9,8},{10,11... | collective-permute-start | bytes 49160 | tf_op jit(solution)/shard_map/ppermute | solution.py:374

commit v5 on v3

--- a/solution.py
+++ b/solution.py
@@ -154,10 +154,9 @@
 
 
 def share_kernel(
-    adapter, item_user, routes, cand_index, hist_user, block, out, mine, user, owner, cand, event, events, sems
+    adapter, item_user, routes, cand_index, hist_user, out, mine, user, owner, cand, event, events, sems
 ):
-    _, cols = block.shape
-    rows = out.shape[0] - LISTED
+    rows, cols = out.shape[0] - LISTED, out.shape[1]
     row = pl.multiple_of(lax.axis_index("groups") * rows, rows)
     columns = pl.ds(col_start(cols), cols)
     part = event.shape[1]
@@ -167,8 +166,7 @@
         pltpu.make_async_copy(cand_index, cand, sems.at[2]),
         pltpu.make_async_copy(hist_user.at[:, pl.ds(col_start(part), part)], event, sems.at[3]),
         pltpu.make_async_copy(adapter.at[pl.ds(row, rows), columns], out.at[pl.ds(0, rows)], sems.at[4]),
-        pltpu.make_async_copy(adapter.at[:, columns], block, sems.at[5]),
-        pltpu.make_async_copy(hist_user, events, sems.at[6]),
+        pltpu.make_async_copy(hist_user, events, sems.at[5]),
     ]
     for copy in copies:
         copy.start()
@@ -262,13 +260,14 @@
         out[k] = jnp.where(column == user, inverse, 0.0)
 
 
-def project_kernel(hist_emb, key_weight, value_weight, key_t, value, emb, keys, values, sems):
+def project_kernel(adapter, hist_emb, key_weight, value_weight, key_t, value, block, emb, keys, values, sems):
     width = value.shape[1]
     columns = pl.ds(col_start(width), width)
     copies = [
         pltpu.make_async_copy(key_weight.at[:, columns], keys, sems.at[0]),
         pltpu.make_async_copy(value_weight.at[:, columns], values, sems.at[1]),
         pltpu.make_async_copy(hist_emb, emb, sems.at[2]),
+        pltpu.make_async_copy(adapter.at[:, columns], block, sems.at[3]),
     ]
     for copy in copies:
         copy.start()
@@ -387,10 +386,9 @@
     events, dim = hist_emb.shape
     order = shift_order(n)
 
-    block, own_share, mine = call(
+    own_share, mine = call(
         share_kernel,
         (
-            shape((depth, width), BF16),
             shape((depth // groups + LISTED, width), BF16),
             shape((1, 2 * items + cands + events), jnp.int32),
         ),
@@ -408,7 +406,7 @@
             pltpu.VMEM((1, cands // 2), jnp.int32),
             pltpu.VMEM((1, events // 2), jnp.int32),
             pltpu.VMEM((1, events), jnp.int32),
-            pltpu.SemaphoreType.DMA((7,)),
+            pltpu.SemaphoreType.DMA((6,)),
         ],
     )
     along = {}
@@ -422,18 +420,18 @@
     other = shift(mine, "rep", 1)
     keys = events + 2 * items
     hot, pick = call(users_kernel, (shape((USERS, keys), BF16), shape((cands, 2 * items), BF16)), (mine, other))
-    key_t, value = call(
+    key_t, value, block = call(
         project_kernel,
-        (shape((width, events), BF16), shape((events, width), BF16)),
-        (hist_emb, key_weight, value_weight),
+        (shape((width, events), BF16), shape((events, width), BF16), shape((depth, width), BF16)),
+        (adapter, hist_emb, key_weight, value_weight),
         flops=4 * events * dim * width,
         bytes_accessed=4 << 20,
-        specs=[HBM] * 3,
+        specs=[HBM] * 4,
         scratch=[
             pltpu.VMEM((events, dim), BF16),
             pltpu.VMEM((dim, width), BF16),
             pltpu.VMEM((dim, width), BF16),
-            pltpu.SemaphoreType.DMA((3,)),
+            pltpu.SemaphoreType.DMA((4,)),
         ],
     )
     total = call(

time: 45.9 us -> 42.1 us (0.917)
  local copies, waits for them, and re-layouts: 2.74 us -> 0.01 us
  waiting for transfers between devices: 14.3 us -> 13.2 us
    unnamed x4 -> x2, local copies, waits for them, and re-layouts: 2.74 us -> 0.01 us
    ppermute x16, waiting for transfers between devices: 14.3 us -> 13.2 us  [shift(): lax.ppermute(value, axis, [(i, (i + k) % count) for i in range(count)])]
  transfers between devices with their start and end apart: 16 -> 16, of which waited for: 7 -> 8; matrix products, arithmetic and copies ran while one was open for 0% -> 0% of each run, Pallas kernels for 20% -> 22%
where the time goes in v5:
time: 42.1 us; the launch traced here: 42 us
  starting transfers between devices  18.4 us (44%)
  waiting for transfers between devices  13.2 us (31%)
  Pallas kernels  10.2 us (24%)
    ppermute x16, starting transfers between devices, shift(): lax.ppermute(value, axis, [(i, (i + k) % count) for i in range(count)])  18.4 us
    ppermute x16, waiting for transfers between devices, shift(): lax.ppermute(value, axis, [(i, (i + k) % count) for i in range(count)])  13.2 us
    pallas_call x18, Pallas kernels, call(): pl.pallas_call(kernel, out_shape=outs, in_specs=specs or [VM] * len(args)...  10.2 us
  transfers between devices with their start and end apart: 16, of which 8 were waited for; matrix products, arithmetic and copies ran while one was open for 0% of the time, Pallas kernels for 22%

profile of v5, /device:TPU:0, one launch (start us, length us, event | category | flops | bytes accessed | tf_op | source)
XLA Modules:
  0.0 42.0 jit_solution(15116719544006112976)
XLA Ops:
  0.0 0.5 %collective-permute-start = (bf16[256,4096]{1,0:T(8,128)(2,1)}, bf16[256,4096]{1,0:T(8,128)(2,1)S(1)}, u32[]{:S(2)}, u32[]{:S(2)}) collective-permute-start(bf16[256,4096]{1,0:T(8,128)(2,1)} %mine.11), channel_id=1, source_target_pairs={{0,1},{1,0},{2,3},{3,2},{4,5},{5,4},{6,7},{7,6},{8,9},{9,8},{10,11... | collective-permute-start | bytes 6291464 | tf_op jit(solution)/shard_map/ppermute | solution.py:371
  0.5 1.2 %shard_map.91 = (bf16[528,128]{1,0:T(8,128)(2,1)S(1)}, s32[1,1664]{1,0:T(1,128)S(1)}) custom-call(bf16[1024,256]{1,0:T(8,128)(2,1)} %adapter.3, s32[1,256]{1,0:T(1,128)} %bitcast.5, s32[1,256]{1,0:T(1,128)} %bitcast.6, s32[1,64]{1,0:T(1,128)} %bitcast.7, s32[1,1024]{1,0:T(1,128)} %bitcast.4), custom_call_target="tpu_custom_call" | custom-call | bytes 262144 | tf_op jit(solution)/shard_map/pallas_call | solution.py:125
  1.7 2.6 %collective-permute-start.2 = (bf16[528,128]{1,0:T(8,128)(2,1)S(1)}, bf16[528,128]{1,0:T(8,128)(2,1)S(1)}, u32[]{:S(2)}, u32[]{:S(2)}) collective-permute-start(bf16[528,128]{1,0:T(8,128)(2,1)S(1)} %get-tuple-element.21.refs_0_), channel_id=1, source_target_pairs={{0,4},{4,8},{8,12},{12,0},{1,5},{5,9},{9,13},{13,1},{2,6},{6,10},{... | collective-permute-start | bytes 405512 | tf_op jit(solution)/shard_map/ppermute | solution.py:371
  4.3 2.1 %collective-permute-start.4 = (bf16[528,128]{1,0:T(8,128)(2,1)S(1)}, bf16[528,128]{1,0:T(8,128)(2,1)S(1)}, u32[]{:S(2)}, u32[]{:S(2)}) collective-permute-start(bf16[528,128]{1,0:T(8,128)(2,1)S(1)} %get-tuple-element.21.refs_0_), channel_id=1, source_target_pairs={{0,12},{4,0},{8,4},{12,8},{1,13},{5,1},{9,5},{13,9},{2,14},{6,2},{... | collective-permute-start | bytes 405512 | tf_op jit(solution)/shard_map/ppermute | solution.py:371
  6.4 4.4 %collective-permute-done.2.refs_0_.refs_1_ = bf16[528,128]{1,0:T(8,128)(2,1)S(1)} collective-permute-done((bf16[528,128]{1,0:T(8,128)(2,1)S(1)}, bf16[528,128]{1,0:T(8,128)(2,1)S(1)}, u32[]{:S(2)}, u32[]{:S(2)}) %collective-permute-start.2) | collective-permute-done | bytes 135200 | tf_op jit(solution)/shard_map/ppermute | solution.py:371
  10.8 0.0 collective-permute-start.6
  10.8 1.7 %collective-permute-start.3 = (bf16[528,128]{1,0:T(8,128)(2,1)S(1)}, bf16[528,128]{1,0:T(8,128)(2,1)S(1)}, u32[]{:S(2)}, u32[]{:S(2)}) collective-permute-start(bf16[528,128]{1,0:T(8,128)(2,1)S(1)} %collective-permute-done.2.refs_0_.refs_1_), channel_id=1, source_target_pairs={{0,16},{16,0},{1,17},{17,1},{2,18},{18,2},{3,19},{19,3},{4,20},{20... | collective-permute-start | bytes 405512 | tf_op jit(solution)/shard_map/ppermute | solution.py:371
  12.6 0.2 collective-permute-done.4.refs_0_.refs_3_
  12.8 1.5 %collective-permute-start.5 = (bf16[528,128]{1,0:T(8,128)(2,1)S(1)}, bf16[528,128]{1,0:T(8,128)(2,1)S(1)}, u32[]{:S(2)}, u32[]{:S(2)}) collective-permute-start(bf16[528,128]{1,0:T(8,128)(2,1)S(1)} %collective-permute-done.4.refs_0_.refs_3_), channel_id=1, source_target_pairs={{0,16},{16,0},{1,17},{17,1},{2,18},{18,2},{3,19},{19,3},{4,20},{20... | collective-permute-start | bytes 405512 | tf_op jit(solution)/shard_map/ppermute | solution.py:371
  14.3 3.9 %collective-permute-done.6.refs_0_.refs_2_ = bf16[528,128]{1,0:T(8,128)(2,1)S(1)} collective-permute-done((bf16[528,128]{1,0:T(8,128)(2,1)S(1)}, bf16[528,128]{1,0:T(8,128)(2,1)S(1)}, u32[]{:S(2)}, u32[]{:S(2)}) %collective-permute-start.6) | collective-permute-done | bytes 135200 | tf_op jit(solution)/shard_map/ppermute | solution.py:371
  18.2 1.5 %collective-permute-start.7 = (bf16[528,128]{1,0:T(8,128)(2,1)S(1)}, bf16[528,128]{1,0:T(8,128)(2,1)S(1)}, u32[]{:S(2)}, u32[]{:S(2)}) collective-permute-start(bf16[528,128]{1,0:T(8,128)(2,1)S(1)} %collective-permute-done.6.refs_0_.refs_2_), channel_id=1, source_target_pairs={{0,16},{16,0},{1,17},{17,1},{2,18},{18,2},{3,19},{19,3},{4,20},{20... | collective-permute-start | bytes 405512 | tf_op jit(solution)/shard_map/ppermute | solution.py:371
  19.7 0.0 collective-permute-start.1
  19.7 2.2 %shard_map.93 = (bf16[128,1024]{1,0:T(8,128)(2,1)S(1)}, bf16[1024,128]{1,0:T(8,128)(2,1)S(1)}, bf16[1024,128]{1,0:T(8,128)(2,1)S(1)}) custom-call(bf16[1024,256]{1,0:T(8,128)(2,1)} %adapter.3, bf16[1024,512]{1,0:T(8,128)(2,1)} %hist_emb.1, bf16[512,256]{1,0:T(8,128)(2,1)} %key_weight.1, bf16[512,256]{1,0:T(8,128)(2,1)} %value_weight.1), custom_call_target="tpu_custom_call" | custom-call | flops 268435456 | bytes 4194304 | tf_op jit(solution)/shard_map/pallas_call | solution.py:125
  21.9 0.0 collective-permute-done.1.other
  21.9 0.2 shard_map.92
  22.2 0.0 collective-permute-done.other
  22.2 0.4 %shard_map.94.total = f32[512,128]{1,0:T(8,128)S(1)} custom-call(bf16[256,4096]{1,0:T(8,128)(2,1)S(1)} %copy-done, bf16[256,4096]{1,0:T(8,128)(2,1)S(1)} %collective-permute-done.other, bf16[1024,128]{1,0:T(8,128)(2,1)S(1)} %get-tuple-element.20.block), custom_call_target="tpu_custom_call" | custom-call | flops 134217728 | bytes 4194304 | tf_op jit(solution)/shard_map/pallas_call | solution.py:125
  22.6 0.0 collective-permute-done.3.refs_1_
  22.6 0.4 %shard_map.95.total = f32[512,128]{1,0:T(8,128)S(1)} custom-call(bf16[256,4096]{1,0:T(8,128)(2,1)S(1)} %copy-done, bf16[256,4096]{1,0:T(8,128)(2,1)S(1)} %collective-permute-done.other, f32[512,128]{1,0:T(8,128)S(1)} %shard_map.94.total, bf16[528,128]{1,0:T(8,128)(2,1)S(1)} %collective-permute-done.2.refs_0_.refs_1_, ...), custom_call_target="tpu_custom_call" | custom-call | flops 134217728 | bytes 2097152 | tf_op jit(solution)/shard_map/pallas_call | solution.py:125
  23.1 0.0 collective-permute-done.5.refs_1_
  23.1 0.4 shard_map.96.total
  23.5 0.3 shard_map.97.total
  23.8 0.4 %shard_map.98 = (f32[128,128]{1,0:T(8,128)S(1)}, bf16[128,512]{1,0:T(8,128)(2,1)S(1)}) custom-call(bf16[256,4096]{1,0:T(8,128)(2,1)S(1)} %copy-done, bf16[256,4096]{1,0:T(8,128)(2,1)S(1)} %collective-permute-done.other, bf16[128,512]{1,0:T(8,128)(2,1)S(1)} %get-tuple-element.19.pick, f32[512,128]{1,0:T(8,128)S(1)} %shard_map.97.total), custom_call_target="tpu_custom_call" | custom-call | flops 167772160 | bytes 262144 | tf_op jit(solution)/shard_map/pallas_call | solution.py:125
  24.2 0.0 collective-permute-done.7.block
  24.2 0.2 shard_map.99.query
  24.4 0.1 collective-permute-start.9
  24.5 0.6 %collective-permute-start.8 = (f32[16,256]{1,0:T(8,128)S(1)}, f32[16,256]{1,0:T(8,128)S(1)}, u32[]{:S(2)}, u32[]{:S(2)}) collective-permute-start(f32[16,256]{1,0:T(8,128)S(1)} %shard_map.101.tally), channel_id=1, source_target_pairs={{0,1},{1,0},{2,3},{3,2},{4,5},{5,4},{6,7},{7,6},{8,9},{9,8},{10,11... | collective-permute-start | bytes 49160 | tf_op jit(solution)/shard_map/ppermute | solution.py:371
  25.1 3.5 %collective-permute-start.11 = (bf16[128,128]{1,0:T(8,128)(2,1)S(1)}, bf16[128,128]{1,0:T(8,128)(2,1)S(1)}, u32[]{:S(2)}, u32[]{:S(2)}) collective-permute-start(bf16[128,128]{1,0:T(8,128)(2,1)S(1)} %shard_map.99.query), channel_id=1, source_target_pairs={{0,12},{4,0},{8,4},{12,8},{1,13},{5,1},{9,5},{13,9},{2,14},{6,2},{... | collective-permute-start | bytes 98312 | tf_op jit(solution)/shard_map/ppermute | solution.py:371
  28.6 0.0 collective-permute-done.8.tally_other
  28.6 0.6 %shard_map.102.scale = f32[4,128,1536]{2,1,0:T(8,128)S(1)} custom-call(s32[1,1664]{1,0:T(1,128)S(1)} %get-tuple-element.18.mine, s32[1,1664]{1,0:T(1,128)S(1)} %collective-permute-done.1.other, bf16[256,1536]{1,0:T(8,128)(2,1)S(1)} %get-tuple-element.28.hot, f32[16,256]{1,0:T(8,128)S(1)} %shard_map.101.tally, f32[16,256]{1,0:T(8,128)S(1)} %collective-permute-done.8.tally_other), custom_call_target="tpu_custom_call" | custom-call | bytes 4194304 | tf_op jit(solution)/shard_map/pallas_call | solution.py:125
  29.2 0.1 collective-permute-start.13
  29.3 0.4 shard_map.100
  29.7 0.8 %collective-permute-done.9.query = bf16[128,128]{1,0:T(8,128)(2,1)S(1)} collective-permute-done((bf16[128,128]{1,0:T(8,128)(2,1)S(1)}, bf16[128,128]{1,0:T(8,128)(2,1)S(1)}, u32[]{:S(2)}, u32[]{:S(2)}) %collective-permute-start.9) | collective-permute-done | bytes 32800 | tf_op jit(solution)/shard_map/ppermute | solution.py:371
  30.4 0.7 %shard_map.104 = bf16[128,128]{1,0:T(8,128)(2,1)S(1)} custom-call(bf16[128,128]{1,0:T(8,128)(2,1)S(1)} %collective-permute-done.9.query, bf16[128,1024]{1,0:T(8,128)(2,1)S(1)} %get-tuple-element.24.key_t, bf16[1024,128]{1,0:T(8,128)(2,1)S(1)} %get-tuple-element.25.value, bf16[128,512]{1,0:T(8,128)(2,1)S(1)} %get-tuple-element.26.rows_t, ...), custom_call_target="tpu_custom_call" | custom-call | flops 201326592 | bytes 1048576 | tf_op jit(solution)/shard_map/pallas_call | solution.py:125
  31.1 0.2 collective-permute-start.10
  31.4 0.0 collective-permute-done.11.query
  31.4 0.7 %shard_map.105 = bf16[128,128]{1,0:T(8,128)(2,1)S(1)} custom-call(bf16[128,128]{1,0:T(8,128)(2,1)S(1)} %collective-permute-done.11.query, bf16[128,1024]{1,0:T(8,128)(2,1)S(1)} %get-tuple-element.24.key_t, bf16[1024,128]{1,0:T(8,128)(2,1)S(1)} %get-tuple-element.25.value, bf16[128,512]{1,0:T(8,128)(2,1)S(1)} %get-tuple-element.26.rows_t, ...), custom_call_target="tpu_custom_call" | custom-call | flops 201326592 | bytes 1048576 | tf_op jit(solution)/shard_map/pallas_call | solution.py:125
  32.1 1.9 %collective-permute-start.12 = (bf16[128,128]{1,0:T(8,128)(2,1)S(1)}, bf16[128,128]{1,0:T(8,128)(2,1)S(1)}, u32[]{:S(2)}, u32[]{:S(2)}) collective-permute-start(bf16[128,128]{1,0:T(8,128)(2,1)S(1)} %shard_map.105), channel_id=1, source_target_pairs={{0,4},{4,8},{8,12},{12,0},{1,5},{5,9},{9,13},{13,1},{2,6},{6,10},{... | collective-permute-start | bytes 98312 | tf_op jit(solution)/shard_map/ppermute | solution.py:371
  34.0 0.2 collective-permute-done.13.query
  34.2 0.7 %shard_map.106 = bf16[128,128]{1,0:T(8,128)(2,1)S(1)} custom-call(bf16[128,128]{1,0:T(8,128)(2,1)S(1)} %collective-permute-done.13.query, bf16[128,1024]{1,0:T(8,128)(2,1)S(1)} %get-tuple-element.24.key_t, bf16[1024,128]{1,0:T(8,128)(2,1)S(1)} %get-tuple-element.25.value, bf16[128,512]{1,0:T(8,128)(2,1)S(1)} %get-tuple-element.26.rows_t, ...), custom_call_target="tpu_custom_call" | custom-call | flops 201326592 | bytes 1048576 | tf_op jit(solution)/shard_map/pallas_call | solution.py:125
  34.9 2.0 %collective-permute-start.14 = (bf16[128,128]{1,0:T(8,128)(2,1)S(1)}, bf16[128,128]{1,0:T(8,128)(2,1)S(1)}, u32[]{:S(2)}, u32[]{:S(2)}) collective-permute-start(bf16[128,128]{1,0:T(8,128)(2,1)S(1)} %shard_map.106), channel_id=1, source_target_pairs={{0,8},{4,12},{8,0},{12,4},{1,9},{5,13},{9,1},{13,5},{2,10},{6,14},... | collective-permute-start | bytes 98312 | tf_op jit(solution)/shard_map/ppermute | solution.py:371
  36.9 0.7 %shard_map.103.own = f32[128,128]{1,0:T(8,128)S(1)} custom-call(bf16[128,128]{1,0:T(8,128)(2,1)S(1)} %shard_map.99.query, bf16[128,1024]{1,0:T(8,128)(2,1)S(1)} %get-tuple-element.24.key_t, bf16[1024,128]{1,0:T(8,128)(2,1)S(1)} %get-tuple-element.25.value, bf16[128,512]{1,0:T(8,128)(2,1)S(1)} %get-tuple-element.26.rows_t, ...), custom_call_target="tpu_custom_call" | custom-call | flops 201326592 | bytes 1048576 | tf_op jit(solution)/shard_map/pallas_call | solution.py:125
  37.6 0.0 collective-permute-done.10.refs_0_
  37.6 0.3 collective-permute-done.12.refs_1_
  37.9 2.2 %collective-permute-done.14.refs_2_ = bf16[128,128]{1,0:T(8,128)(2,1)S(1)} collective-permute-done((bf16[128,128]{1,0:T(8,128)(2,1)S(1)}, bf16[128,128]{1,0:T(8,128)(2,1)S(1)}, u32[]{:S(2)}, u32[]{:S(2)}) %collective-permute-start.14) | collective-permute-done | bytes 32800 | tf_op jit(solution)/shard_map/ppermute | solution.py:371
  40.1 0.1 collective-permute-start.15
  40.2 1.2 %collective-permute-done.15.got = bf16[64,128]{1,0:T(8,128)(2,1)S(1)} collective-permute-done((bf16[64,128]{1,0:T(8,128)(2,1)S(1)}, bf16[64,128]{1,0:T(8,128)(2,1)S(1)}, u32[]{:S(2)}, u32[]{:S(2)}) %collective-permute-start.15) | collective-permute-done | bytes 16416 | tf_op jit(solution)/shard_map/ppermute | solution.py:371
  41.4 0.6 %shard_map.108 = bf16[64,256]{1,0:T(8,128)(2,1)} custom-call(bf16[64,128]{1,0:T(8,128)(2,1)S(1)} %get-tuple-element.29.keep, bf16[64,128]{1,0:T(8,128)(2,1)S(1)} %collective-permute-done.15.got), custom_call_target="tpu_custom_call" | custom-call | bytes 262144 | tf_op jit(solution)/shard_map/pallas_call | solution.py:125
  (4 shorter events, 0.1 us)
Async XLA Ops:
  0.0 22.2 %copy-start = (bf16[256,4096]{1,0:T(8,128)(2,1)S(1)}, bf16[256,4096]{1,0:T(8,128)(2,1)}, u32[]{:S(2)}) copy-start(bf16[256,4096]{1,0:T(8,128)(2,1)} %mine.11) | copy-start | bytes 6291460
  0.0 22.2 %collective-permute-start = (bf16[256,4096]{1,0:T(8,128)(2,1)}, bf16[256,4096]{1,0:T(8,128)(2,1)S(1)}, u32[]{:S(2)}, u32[]{:S(2)}) collective-permute-start(bf16[256,4096]{1,0:T(8,128)(2,1)} %mine.11), channel_id=1, source_target_pairs={{0,1},{1,0},{2,3},{3,2},{4,5},{5,4},{6,7},{7,6},{8,9},{9,8},{10,11... | collective-permute-start | bytes 6291464 | tf_op jit(solution)/shard_map/ppermute | solution.py:371
  1.7 9.1 %collective-permute-start.2 = (bf16[528,128]{1,0:T(8,128)(2,1)S(1)}, bf16[528,128]{1,0:T(8,128)(2,1)S(1)}, u32[]{:S(2)}, u32[]{:S(2)}) collective-permute-start(bf16[528,128]{1,0:T(8,128)(2,1)S(1)} %get-tuple-element.21.refs_0_), channel_id=1, source_target_pairs={{0,4},{4,8},{8,12},{12,0},{1,5},{5,9},{9,13},{13,1},{2,6},{6,10},{... | collective-permute-start | bytes 405512 | tf_op jit(solution)/shard_map/ppermute | solution.py:371
  4.3 8.5 %collective-permute-start.4 = (bf16[528,128]{1,0:T(8,128)(2,1)S(1)}, bf16[528,128]{1,0:T(8,128)(2,1)S(1)}, u32[]{:S(2)}, u32[]{:S(2)}) collective-permute-start(bf16[528,128]{1,0:T(8,128)(2,1)S(1)} %get-tuple-element.21.refs_0_), channel_id=1, source_target_pairs={{0,12},{4,0},{8,4},{12,8},{1,13},{5,1},{9,5},{13,9},{2,14},{6,2},{... | collective-permute-start | bytes 405512 | tf_op jit(solution)/shard_map/ppermute | solution.py:371
  10.8 7.4 %collective-permute-start.6 = (bf16[528,128]{1,0:T(8,128)(2,1)S(1)}, bf16[528,128]{1,0:T(8,128)(2,1)S(1)}, u32[]{:S(2)}, u32[]{:S(2)}) collective-permute-start(bf16[528,128]{1,0:T(8,128)(2,1)S(1)} %collective-permute-done.2.refs_0_.refs_1_), channel_id=1, source_target_pairs={{0,4},{4,8},{8,12},{12,0},{1,5},{5,9},{9,13},{13,1},{2,6},{6,10},{... | collective-permute-start | bytes 405512 | tf_op jit(solution)/shard_map/ppermute | solution.py:371
  10.8 11.8 %collective-permute-start.3 = (bf16[528,128]{1,0:T(8,128)(2,1)S(1)}, bf16[528,128]{1,0:T(8,128)(2,1)S(1)}, u32[]{:S(2)}, u32[]{:S(2)}) collective-permute-start(bf16[528,128]{1,0:T(8,128)(2,1)S(1)} %collective-permute-done.2.refs_0_.refs_1_), channel_id=1, source_target_pairs={{0,16},{16,0},{1,17},{17,1},{2,18},{18,2},{3,19},{19,3},{4,20},{20... | collective-permute-start | bytes 405512 | tf_op jit(solution)/shard_map/ppermute | solution.py:371
  12.8 10.3 %collective-permute-start.5 = (bf16[528,128]{1,0:T(8,128)(2,1)S(1)}, bf16[528,128]{1,0:T(8,128)(2,1)S(1)}, u32[]{:S(2)}, u32[]{:S(2)}) collective-permute-start(bf16[528,128]{1,0:T(8,128)(2,1)S(1)} %collective-permute-done.4.refs_0_.refs_3_), channel_id=1, source_target_pairs={{0,16},{16,0},{1,17},{17,1},{2,18},{18,2},{3,19},{19,3},{4,20},{20... | collective-permute-start | bytes 405512 | tf_op jit(solution)/shard_map/ppermute | solution.py:371
  18.2 6.0 %collective-permute-start.7 = (bf16[528,128]{1,0:T(8,128)(2,1)S(1)}, bf16[528,128]{1,0:T(8,128)(2,1)S(1)}, u32[]{:S(2)}, u32[]{:S(2)}) collective-permute-start(bf16[528,128]{1,0:T(8,128)(2,1)S(1)} %collective-permute-done.6.refs_0_.refs_2_), channel_id=1, source_target_pairs={{0,16},{16,0},{1,17},{17,1},{2,18},{18,2},{3,19},{19,3},{4,20},{20... | collective-permute-start | bytes 405512 | tf_op jit(solution)/shard_map/ppermute | solution.py:371
  19.7 2.2 %collective-permute-start.1 = (s32[1,1664]{1,0:T(1,128)S(1)}, s32[1,1664]{1,0:T(1,128)S(1)}, u32[]{:S(2)}, u32[]{:S(2)}) collective-permute-start(s32[1,1664]{1,0:T(1,128)S(1)} %get-tuple-element.18.mine), channel_id=1, source_target_pairs={{0,1},{1,0},{2,3},{3,2},{4,5},{5,4},{6,7},{7,6},{8,9},{9,8},{10,11... | collective-permute-start | bytes 19976 | tf_op jit(solution)/shard_map/ppermute | solution.py:371
  24.4 6.0 %collective-permute-start.9 = (bf16[128,128]{1,0:T(8,128)(2,1)S(1)}, bf16[128,128]{1,0:T(8,128)(2,1)S(1)}, u32[]{:S(2)}, u32[]{:S(2)}) collective-permute-start(bf16[128,128]{1,0:T(8,128)(2,1)S(1)} %shard_map.99.query), channel_id=1, source_target_pairs={{0,4},{4,8},{8,12},{12,0},{1,5},{5,9},{9,13},{13,1},{2,6},{6,10},{... | collective-permute-start | bytes 98312 | tf_op jit(solution)/shard_map/ppermute | solution.py:371
  24.5 4.1 %collective-permute-start.8 = (f32[16,256]{1,0:T(8,128)S(1)}, f32[16,256]{1,0:T(8,128)S(1)}, u32[]{:S(2)}, u32[]{:S(2)}) collective-permute-start(f32[16,256]{1,0:T(8,128)S(1)} %shard_map.101.tally), channel_id=1, source_target_pairs={{0,1},{1,0},{2,3},{3,2},{4,5},{5,4},{6,7},{7,6},{8,9},{9,8},{10,11... | collective-permute-start | bytes 49160 | tf_op jit(solution)/shard_map/ppermute | solution.py:371
  25.1 6.3 %collective-permute-start.11 = (bf16[128,128]{1,0:T(8,128)(2,1)S(1)}, bf16[128,128]{1,0:T(8,128)(2,1)S(1)}, u32[]{:S(2)}, u32[]{:S(2)}) collective-permute-start(bf16[128,128]{1,0:T(8,128)(2,1)S(1)} %shard_map.99.query), channel_id=1, source_target_pairs={{0,12},{4,0},{8,4},{12,8},{1,13},{5,1},{9,5},{13,9},{2,14},{6,2},{... | collective-permute-start | bytes 98312 | tf_op jit(solution)/shard_map/ppermute | solution.py:371
  29.2 5.0 %collective-permute-start.13 = (bf16[128,128]{1,0:T(8,128)(2,1)S(1)}, bf16[128,128]{1,0:T(8,128)(2,1)S(1)}, u32[]{:S(2)}, u32[]{:S(2)}) collective-permute-start(bf16[128,128]{1,0:T(8,128)(2,1)S(1)} %shard_map.99.query), channel_id=1, source_target_pairs={{0,8},{4,12},{8,0},{12,4},{1,9},{5,13},{9,1},{13,5},{2,10},{6,14},... | collective-permute-start | bytes 98312 | tf_op jit(solution)/shard_map/ppermute | solution.py:371
  31.1 6.4 %collective-permute-start.10 = (bf16[128,128]{1,0:T(8,128)(2,1)S(1)}, bf16[128,128]{1,0:T(8,128)(2,1)S(1)}, u32[]{:S(2)}, u32[]{:S(2)}) collective-permute-start(bf16[128,128]{1,0:T(8,128)(2,1)S(1)} %shard_map.104), channel_id=1, source_target_pairs={{0,12},{4,0},{8,4},{12,8},{1,13},{5,1},{9,5},{13,9},{2,14},{6,2},{... | collective-permute-start | bytes 98312 | tf_op jit(solution)/shard_map/ppermute | solution.py:371
  32.1 5.8 %collective-permute-start.12 = (bf16[128,128]{1,0:T(8,128)(2,1)S(1)}, bf16[128,128]{1,0:T(8,128)(2,1)S(1)}, u32[]{:S(2)}, u32[]{:S(2)}) collective-permute-start(bf16[128,128]{1,0:T(8,128)(2,1)S(1)} %shard_map.105), channel_id=1, source_target_pairs={{0,4},{4,8},{8,12},{12,0},{1,5},{5,9},{9,13},{13,1},{2,6},{6,10},{... | collective-permute-start | bytes 98312 | tf_op jit(solution)/shard_map/ppermute | solution.py:371
  34.9 5.2 %collective-permute-start.14 = (bf16[128,128]{1,0:T(8,128)(2,1)S(1)}, bf16[128,128]{1,0:T(8,128)(2,1)S(1)}, u32[]{:S(2)}, u32[]{:S(2)}) collective-permute-start(bf16[128,128]{1,0:T(8,128)(2,1)S(1)} %shard_map.106), channel_id=1, source_target_pairs={{0,8},{4,12},{8,0},{12,4},{1,9},{5,13},{9,1},{13,5},{2,10},{6,14},... | collective-permute-start | bytes 98312 | tf_op jit(solution)/shard_map/ppermute | solution.py:371
  40.1 1.2 %collective-permute-start.15 = (bf16[64,128]{1,0:T(8,128)(2,1)S(1)}, bf16[64,128]{1,0:T(8,128)(2,1)S(1)}, u32[]{:S(2)}, u32[]{:S(2)}) collective-permute-start(bf16[64,128]{1,0:T(8,128)(2,1)S(1)} %get-tuple-element.30), channel_id=1, source_target_pairs={{0,1},{1,0},{2,3},{3,2},{4,5},{5,4},{6,7},{7,6},{8,9},{9,8},{10,11... | collective-permute-start | bytes 49160 | tf_op jit(solution)/shard_map/ppermute | solution.py:371

commit v6 on v3

--- a/solution.py
+++ b/solution.py
@@ -307,20 +307,31 @@
     return pl.ds(pl.multiple_of((source * groups + group) * depth, depth), depth)
 
 
-def query_part_kernel(n, groups, k, step, mine, other, pick, total, part, feats):
+def query_part_kernel(n, groups, which, mine, other, pick, total, part, feats):
     items = mine.shape[0]
-    at = columns_of(n, groups, k, step, feats.shape[1])
+    depth = feats.shape[1] // len(which)
     part[...] = lax.dot(pick[...].astype(F32), total[...], precision=lax.Precision.HIGHEST)
-    feats[...] = (dot(pick[:, :items], mine[:, at]) + dot(pick[:, items:], other[:, at])).astype(BF16)
-
-
-def query_kernel(part, feats, block, query):
-    query[...] = (part[...] + dot(feats[...], block[: feats.shape[1]])).astype(BF16)
-
-
-def embed_last_kernel(n, groups, k, step, mine, other, total, block, rows, rows_t):
+    for slot, (k, step) in enumerate(which):
+        at = columns_of(n, groups, k, step, depth)
+        picked = dot(pick[:, :items], mine[:, at]) + dot(pick[:, items:], other[:, at])
+        feats[:, slot * depth : (slot + 1) * depth] = picked.astype(BF16)
+
+
+def query_kernel(part, feats, *refs):
+    blocks, query = refs[:-1], refs[-1]
+    depth = feats.shape[1] // len(blocks)
+    total = part[...]
+    for slot, block in enumerate(blocks):
+        total = total + dot(feats[:, slot * depth : (slot + 1) * depth], block[:depth])
+    query[...] = total.astype(BF16)
+
+
+def embed_last_kernel(n, groups, which, mine, other, total, *refs):
     items = mine.shape[0]
-    top, bottom = add_block(n, groups, k, step, mine, other, total[:items], total[items:], block)
+    blocks, (rows, rows_t) = refs[:-2], refs[-2:]
+    top, bottom = total[:items], total[items:]
+    for (k, step), block in zip(which, blocks):
+        top, bottom = add_block(n, groups, k, step, mine, other, top, bottom, block)
     rows[:items] = top.astype(BF16)
     rows[items:] = bottom.astype(BF16)
     rows_t[...] = jnp.transpose(rows[...])
@@ -451,10 +462,9 @@
         bytes_accessed=4 << 20,
     )
     across = {k: [along[k]] + [shift(along[k], "groups", g) for g in range(1, groups)] for k in order}
-    blocks = [((k, step), across[k][step]) for k in order for step in range(groups)]
-    chunks = [blocks[at : at + groups] for at in range(0, len(blocks) - groups, groups)]
-    chunks += [blocks[-groups:-1]]
-    for k, chunk in zip(order, chunks):
+    near = [((k, 0), across[k][0]) for k in order]
+    far = [((k, step), across[k][step]) for k in order for step in range(1, groups)]
+    for chunk in (near, far[:1]):
         which, arrived = zip(*chunk)
         total = call(
             functools.partial(embed_add_kernel, n, groups, which),
@@ -463,20 +473,20 @@
             flops=4 * items * depth * width,
             bytes_accessed=2 << 20,
         )
-    (k, step), arrived = blocks[-1]
+    which, arrived = zip(*far[1:])
     share = depth // groups
     part, feats = call(
-        functools.partial(query_part_kernel, n, groups, k, step),
-        (shape((cands, width), F32), shape((cands, share), BF16)),
+        functools.partial(query_part_kernel, n, groups, which),
+        (shape((cands, width), F32), shape((cands, share * len(which)), BF16)),
         (item_feats, feats_other, pick, total),
         flops=4 * cands * items * (share + 6 * width),
     )
-    query = call(query_kernel, shape((cands, width), BF16), (part, feats, arrived), flops=2 * cands * share * width)
+    query = call(query_kernel, shape((cands, width), BF16), (part, feats, *arrived), flops=4 * cands * share * width)
     rows, rows_t = call(
-        functools.partial(embed_last_kernel, n, groups, k, step),
+        functools.partial(embed_last_kernel, n, groups, which),
         (shape((2 * items, width), BF16), shape((width, 2 * items), BF16)),
-        (item_feats, feats_other, total, arrived),
-        flops=4 * items * share * width,
+        (item_feats, feats_other, total, *arrived),
+        flops=8 * items * share * width,
         bytes_accessed=2 << 20,
     )
     queries = {k: shift(query, "hist", k) for k in order}

time: 45.9 us -> 46.1 us (level)
    pallas_call x18 -> x17, Pallas kernels: 10.1 us -> 10.1 us  [call(): pl.pallas_call(kernel, out_shape=outs, in_specs=specs or [VM] * len(args)...]
  transfers between devices with their start and end apart: 16 -> 16, of which waited for: 7 -> 7; matrix products, arithmetic and copies ran while one was open for 0% -> 0% of each run, Pallas kernels for 20% -> 21%
where the time goes in v6:
time: 46.1 us; the launch traced here: 45.8 us
  starting transfers between devices  18.4 us (40%)
  waiting for transfers between devices  14.4 us (31%)
  Pallas kernels  10.1 us (22%)
  local copies, waits for them, and re-layouts  2.75 us (6%)
    ppermute x16, starting transfers between devices, shift(): lax.ppermute(value, axis, [(i, (i + k) % count) for i in range(count)])  18.4 us
    ppermute x16, waiting for transfers between devices, shift(): lax.ppermute(value, axis, [(i, (i + k) % count) for i in range(count)])  14.4 us
    pallas_call x17, Pallas kernels, call(): pl.pallas_call(kernel, out_shape=outs, in_specs=specs or [VM] * len(args)...  10.1 us
    unnamed x4, local copies, waits for them, and re-layouts  2.75 us
  transfers between devices with their start and end apart: 16, of which 7 were waited for; matrix products, arithmetic and copies ran while one was open for 0% of the time, Pallas kernels for 21%

profile of v6, /device:TPU:0, one launch (start us, length us, event | category | flops | bytes accessed | tf_op | source)
XLA Modules:
  0.0 45.8 jit_solution(8643057201159869059)
XLA Ops:
  0.0 0.5 %collective-permute-start = (bf16[256,4096]{1,0:T(8,128)(2,1)}, bf16[256,4096]{1,0:T(8,128)(2,1)S(1)}, u32[]{:S(2)}, u32[]{:S(2)}) collective-permute-start(bf16[256,4096]{1,0:T(8,128)(2,1)} %mine.9), channel_id=1, source_target_pairs={{0,1},{1,0},{2,3},{3,2},{4,5},{5,4},{6,7},{7,6},{8,9},{9,8},{10,11... | collective-permute-start | bytes 6291464 | tf_op jit(solution)/shard_map/ppermute | solution.py:383
  0.5 1.1 %shard_map.91 = (bf16[1024,128]{1,0:T(8,128)(2,1)S(1)}, bf16[528,128]{1,0:T(8,128)(2,1)S(1)}, s32[1,1664]{1,0:T(1,128)S(1)}) custom-call(bf16[1024,256]{1,0:T(8,128)(2,1)} %adapter.1, s32[1,256]{1,0:T(1,128)} %bitcast.5, s32[1,256]{1,0:T(1,128)} %bitcast.6, s32[1,64]{1,0:T(1,128)} %bitcast.7, s32[1,1024]{1,0:T(1,128)} %bitcast.4), custom_call_target="tpu_custom_call" | custom-call | bytes 262144 | tf_op jit(solution)/shard_map/pallas_call | solution.py:125
  1.6 2.6 %collective-permute-start.2 = (bf16[528,128]{1,0:T(8,128)(2,1)S(1)}, bf16[528,128]{1,0:T(8,128)(2,1)S(1)}, u32[]{:S(2)}, u32[]{:S(2)}) collective-permute-start(bf16[528,128]{1,0:T(8,128)(2,1)S(1)} %get-tuple-element.21.refs_0_), channel_id=1, source_target_pairs={{0,4},{4,8},{8,12},{12,0},{1,5},{5,9},{9,13},{13,1},{2,6},{6,10},{... | collective-permute-start | bytes 405512 | tf_op jit(solution)/shard_map/ppermute | solution.py:383
  4.3 2.1 %collective-permute-start.3 = (bf16[528,128]{1,0:T(8,128)(2,1)S(1)}, bf16[528,128]{1,0:T(8,128)(2,1)S(1)}, u32[]{:S(2)}, u32[]{:S(2)}) collective-permute-start(bf16[528,128]{1,0:T(8,128)(2,1)S(1)} %get-tuple-element.21.refs_0_), channel_id=1, source_target_pairs={{0,12},{4,0},{8,4},{12,8},{1,13},{5,1},{9,5},{13,9},{2,14},{6,2},{... | collective-permute-start | bytes 405512 | tf_op jit(solution)/shard_map/ppermute | solution.py:383
  6.3 4.4 %collective-permute-done.2.refs_0_.refs_1_ = bf16[528,128]{1,0:T(8,128)(2,1)S(1)} collective-permute-done((bf16[528,128]{1,0:T(8,128)(2,1)S(1)}, bf16[528,128]{1,0:T(8,128)(2,1)S(1)}, u32[]{:S(2)}, u32[]{:S(2)}) %collective-permute-start.2) | collective-permute-done | bytes 135200 | tf_op jit(solution)/shard_map/ppermute | solution.py:383
  10.8 0.0 collective-permute-start.4
  10.8 1.7 %collective-permute-start.5 = (bf16[528,128]{1,0:T(8,128)(2,1)S(1)}, bf16[528,128]{1,0:T(8,128)(2,1)S(1)}, u32[]{:S(2)}, u32[]{:S(2)}) collective-permute-start(bf16[528,128]{1,0:T(8,128)(2,1)S(1)} %collective-permute-done.2.refs_0_.refs_1_), channel_id=1, source_target_pairs={{0,16},{16,0},{1,17},{17,1},{2,18},{18,2},{3,19},{19,3},{4,20},{20... | collective-permute-start | bytes 405512 | tf_op jit(solution)/shard_map/ppermute | solution.py:383
  12.5 0.4 collective-permute-done.3.refs_1_.refs_3_
  12.9 1.5 %collective-permute-start.6 = (bf16[528,128]{1,0:T(8,128)(2,1)S(1)}, bf16[528,128]{1,0:T(8,128)(2,1)S(1)}, u32[]{:S(2)}, u32[]{:S(2)}) collective-permute-start(bf16[528,128]{1,0:T(8,128)(2,1)S(1)} %collective-permute-done.3.refs_1_.refs_3_), channel_id=1, source_target_pairs={{0,16},{16,0},{1,17},{17,1},{2,18},{18,2},{3,19},{19,3},{4,20},{20... | collective-permute-start | bytes 405512 | tf_op jit(solution)/shard_map/ppermute | solution.py:383
  14.4 3.9 %collective-permute-done.4.refs_2_ = bf16[528,128]{1,0:T(8,128)(2,1)S(1)} collective-permute-done((bf16[528,128]{1,0:T(8,128)(2,1)S(1)}, bf16[528,128]{1,0:T(8,128)(2,1)S(1)}, u32[]{:S(2)}, u32[]{:S(2)}) %collective-permute-start.4) | collective-permute-done | bytes 135200 | tf_op jit(solution)/shard_map/ppermute | solution.py:383
  18.3 1.5 %collective-permute-start.7 = (bf16[528,128]{1,0:T(8,128)(2,1)S(1)}, bf16[528,128]{1,0:T(8,128)(2,1)S(1)}, u32[]{:S(2)}, u32[]{:S(2)}) collective-permute-start(bf16[528,128]{1,0:T(8,128)(2,1)S(1)} %collective-permute-done.4.refs_2_), channel_id=1, source_target_pairs={{0,16},{16,0},{1,17},{17,1},{2,18},{18,2},{3,19},{19,3},{4,20},{20... | collective-permute-start | bytes 405512 | tf_op jit(solution)/shard_map/ppermute | solution.py:383
  19.8 0.0 collective-permute-start.1
  19.8 1.2 %collective-permute-done.1.other = s32[1,1664]{1,0:T(1,128)S(1)} collective-permute-done((s32[1,1664]{1,0:T(1,128)S(1)}, s32[1,1664]{1,0:T(1,128)S(1)}, u32[]{:S(2)}, u32[]{:S(2)}) %collective-permute-start.1) | collective-permute-done | bytes 6688 | tf_op jit(solution)/shard_map/ppermute | solution.py:383
  21.0 0.2 shard_map.92
  21.2 0.2 collective-permute-start.8
  21.5 0.0 collective-permute-done.other
  21.5 1.6 %copy-done = bf16[256,4096]{1,0:T(8,128)(2,1)S(1)} copy-done((bf16[256,4096]{1,0:T(8,128)(2,1)S(1)}, bf16[256,4096]{1,0:T(8,128)(2,1)}, u32[]{:S(2)}) %copy-start) | copy-done | bytes 2097176
  23.1 0.4 shard_map.93.total
  23.5 1.2 %copy-done.1 = bf16[256,4096]{1,0:T(8,128)(2,1)S(1)} copy-done((bf16[256,4096]{1,0:T(8,128)(2,1)S(1)}, bf16[256,4096]{1,0:T(8,128)(2,1)}, u32[]{:S(2)}) %copy-start.1) | copy-done | bytes 2097176
  24.7 0.6 %shard_map.94.total = f32[512,128]{1,0:T(8,128)S(1)} custom-call(bf16[256,4096]{1,0:T(8,128)(2,1)S(1)} %copy-done.1, bf16[256,4096]{1,0:T(8,128)(2,1)S(1)} %collective-permute-done.other, f32[512,128]{1,0:T(8,128)S(1)} %shard_map.93.total, bf16[528,128]{1,0:T(8,128)(2,1)S(1)} %collective-permute-done.2.refs_0_.refs_1_, ...), custom_call_target="tpu_custom_call" | custom-call | flops 134217728 | bytes 2097152 | tf_op jit(solution)/shard_map/pallas_call | solution.py:125
  25.2 0.0 collective-permute-done.5.refs_0_
  25.2 0.3 shard_map.95.total
  25.5 0.5 %shard_map.96 = (f32[128,128]{1,0:T(8,128)S(1)}, bf16[128,1024]{1,0:T(8,128)(2,1)S(1)}) custom-call(bf16[256,4096]{1,0:T(8,128)(2,1)S(1)} %copy-done.1, bf16[256,4096]{1,0:T(8,128)(2,1)S(1)} %collective-permute-done.other, bf16[128,512]{1,0:T(8,128)(2,1)S(1)} %get-tuple-element.19.pick, f32[512,128]{1,0:T(8,128)S(1)} %shard_map.95.total), custom_call_target="tpu_custom_call" | custom-call | flops 167772160 | bytes 262144 | tf_op jit(solution)/shard_map/pallas_call | solution.py:125
  26.1 0.0 collective-permute-done.6.refs_0_
  26.1 0.0 collective-permute-done.7.refs_1_
  26.1 0.2 shard_map.97.query
  26.3 0.1 collective-permute-start.9
  26.4 3.8 %collective-permute-start.11 = (bf16[128,128]{1,0:T(8,128)(2,1)S(1)}, bf16[128,128]{1,0:T(8,128)(2,1)S(1)}, u32[]{:S(2)}, u32[]{:S(2)}) collective-permute-start(bf16[128,128]{1,0:T(8,128)(2,1)S(1)} %shard_map.97.query), channel_id=1, source_target_pairs={{0,12},{4,0},{8,4},{12,8},{1,13},{5,1},{9,5},{13,9},{2,14},{6,2},{... | collective-permute-start | bytes 98312 | tf_op jit(solution)/shard_map/ppermute | solution.py:383
  30.2 2.1 %shard_map.98 = (bf16[128,1024]{1,0:T(8,128)(2,1)S(1)}, bf16[1024,128]{1,0:T(8,128)(2,1)S(1)}) custom-call(bf16[1024,512]{1,0:T(8,128)(2,1)} %hist_emb.1, bf16[512,256]{1,0:T(8,128)(2,1)} %key_weight.1, bf16[512,256]{1,0:T(8,128)(2,1)} %value_weight.1), custom_call_target="tpu_custom_call" | custom-call | flops 268435456 | bytes 4194304 | tf_op jit(solution)/shard_map/pallas_call | solution.py:125
  32.3 0.0 collective-permute-done.8.tally_other
  32.3 0.6 %shard_map.101.scale = f32[4,128,1536]{2,1,0:T(8,128)S(1)} custom-call(s32[1,1664]{1,0:T(1,128)S(1)} %get-tuple-element.18.mine, s32[1,1664]{1,0:T(1,128)S(1)} %collective-permute-done.1.other, bf16[256,1536]{1,0:T(8,128)(2,1)S(1)} %get-tuple-element.28.hot, f32[16,256]{1,0:T(8,128)S(1)} %shard_map.100.tally, f32[16,256]{1,0:T(8,128)S(1)} %collective-permute-done.8.tally_other), custom_call_target="tpu_custom_call" | custom-call | bytes 4194304 | tf_op jit(solution)/shard_map/pallas_call | solution.py:125
  32.9 0.1 collective-permute-start.13
  33.0 0.5 %shard_map.99 = (bf16[512,128]{1,0:T(8,128)(2,1)S(1)}, bf16[128,512]{1,0:T(8,128)(2,1)S(1)}) custom-call(bf16[256,4096]{1,0:T(8,128)(2,1)S(1)} %copy-done.1, bf16[256,4096]{1,0:T(8,128)(2,1)S(1)} %collective-permute-done.other, f32[512,128]{1,0:T(8,128)S(1)} %shard_map.95.total, bf16[528,128]{1,0:T(8,128)(2,1)S(1)} %collective-permute-done.6.refs_0_, ...), custom_call_target="tpu_custom_call" | custom-call | flops 134217728 | bytes 2097152 | tf_op jit(solution)/shard_map/pallas_call | solution.py:125
  33.5 0.0 collective-permute-done.9.query
  33.5 0.7 %shard_map.103 = bf16[128,128]{1,0:T(8,128)(2,1)S(1)} custom-call(bf16[128,128]{1,0:T(8,128)(2,1)S(1)} %collective-permute-done.9.query, bf16[128,1024]{1,0:T(8,128)(2,1)S(1)} %get-tuple-element.24.key_t, bf16[1024,128]{1,0:T(8,128)(2,1)S(1)} %get-tuple-element.25.value, bf16[128,512]{1,0:T(8,128)(2,1)S(1)} %get-tuple-element.26.rows_t, ...), custom_call_target="tpu_custom_call" | custom-call | flops 201326592 | bytes 1048576 | tf_op jit(solution)/shard_map/pallas_call | solution.py:125
  34.2 0.7 %collective-permute-start.10 = (bf16[128,128]{1,0:T(8,128)(2,1)S(1)}, bf16[128,128]{1,0:T(8,128)(2,1)S(1)}, u32[]{:S(2)}, u32[]{:S(2)}) collective-permute-start(bf16[128,128]{1,0:T(8,128)(2,1)S(1)} %shard_map.103), channel_id=1, source_target_pairs={{0,12},{4,0},{8,4},{12,8},{1,13},{5,1},{9,5},{13,9},{2,14},{6,2},{... | collective-permute-start | bytes 98312 | tf_op jit(solution)/shard_map/ppermute | solution.py:383
  34.9 0.0 collective-permute-done.11.query
  34.9 0.7 %shard_map.104 = bf16[128,128]{1,0:T(8,128)(2,1)S(1)} custom-call(bf16[128,128]{1,0:T(8,128)(2,1)S(1)} %collective-permute-done.11.query, bf16[128,1024]{1,0:T(8,128)(2,1)S(1)} %get-tuple-element.24.key_t, bf16[1024,128]{1,0:T(8,128)(2,1)S(1)} %get-tuple-element.25.value, bf16[128,512]{1,0:T(8,128)(2,1)S(1)} %get-tuple-element.26.rows_t, ...), custom_call_target="tpu_custom_call" | custom-call | flops 201326592 | bytes 1048576 | tf_op jit(solution)/shard_map/pallas_call | solution.py:125
  35.6 1.5 %collective-permute-start.12 = (bf16[128,128]{1,0:T(8,128)(2,1)S(1)}, bf16[128,128]{1,0:T(8,128)(2,1)S(1)}, u32[]{:S(2)}, u32[]{:S(2)}) collective-permute-start(bf16[128,128]{1,0:T(8,128)(2,1)S(1)} %shard_map.104), channel_id=1, source_target_pairs={{0,4},{4,8},{8,12},{12,0},{1,5},{5,9},{9,13},{13,1},{2,6},{6,10},{... | collective-permute-start | bytes 98312 | tf_op jit(solution)/shard_map/ppermute | solution.py:383
  37.1 0.9 %collective-permute-done.13.query = bf16[128,128]{1,0:T(8,128)(2,1)S(1)} collective-permute-done((bf16[128,128]{1,0:T(8,128)(2,1)S(1)}, bf16[128,128]{1,0:T(8,128)(2,1)S(1)}, u32[]{:S(2)}, u32[]{:S(2)}) %collective-permute-start.13) | collective-permute-done | bytes 32800 | tf_op jit(solution)/shard_map/ppermute | solution.py:383
  38.0 0.7 %shard_map.105 = bf16[128,128]{1,0:T(8,128)(2,1)S(1)} custom-call(bf16[128,128]{1,0:T(8,128)(2,1)S(1)} %collective-permute-done.13.query, bf16[128,1024]{1,0:T(8,128)(2,1)S(1)} %get-tuple-element.24.key_t, bf16[1024,128]{1,0:T(8,128)(2,1)S(1)} %get-tuple-element.25.value, bf16[128,512]{1,0:T(8,128)(2,1)S(1)} %get-tuple-element.26.rows_t, ...), custom_call_target="tpu_custom_call" | custom-call | flops 201326592 | bytes 1048576 | tf_op jit(solution)/shard_map/pallas_call | solution.py:125
  38.7 2.0 %collective-permute-start.14 = (bf16[128,128]{1,0:T(8,128)(2,1)S(1)}, bf16[128,128]{1,0:T(8,128)(2,1)S(1)}, u32[]{:S(2)}, u32[]{:S(2)}) collective-permute-start(bf16[128,128]{1,0:T(8,128)(2,1)S(1)} %shard_map.105), channel_id=1, source_target_pairs={{0,8},{4,12},{8,0},{12,4},{1,9},{5,13},{9,1},{13,5},{2,10},{6,14},... | collective-permute-start | bytes 98312 | tf_op jit(solution)/shard_map/ppermute | solution.py:383
  40.8 0.7 %shard_map.102.own = f32[128,128]{1,0:T(8,128)S(1)} custom-call(bf16[128,128]{1,0:T(8,128)(2,1)S(1)} %shard_map.97.query, bf16[128,1024]{1,0:T(8,128)(2,1)S(1)} %get-tuple-element.24.key_t, bf16[1024,128]{1,0:T(8,128)(2,1)S(1)} %get-tuple-element.25.value, bf16[128,512]{1,0:T(8,128)(2,1)S(1)} %get-tuple-element.26.rows_t, ...), custom_call_target="tpu_custom_call" | custom-call | flops 201326592 | bytes 1048576 | tf_op jit(solution)/shard_map/pallas_call | solution.py:125
  41.5 0.0 collective-permute-done.10.refs_0_
  41.5 2.5 %collective-permute-done.14.refs_2_ = bf16[128,128]{1,0:T(8,128)(2,1)S(1)} collective-permute-done((bf16[128,128]{1,0:T(8,128)(2,1)S(1)}, bf16[128,128]{1,0:T(8,128)(2,1)S(1)}, u32[]{:S(2)}, u32[]{:S(2)}) %collective-permute-start.14) | collective-permute-done | bytes 32800 | tf_op jit(solution)/shard_map/ppermute | solution.py:383
  44.0 0.1 collective-permute-start.15
  44.0 1.2 %collective-permute-done.15.got = bf16[64,128]{1,0:T(8,128)(2,1)S(1)} collective-permute-done((bf16[64,128]{1,0:T(8,128)(2,1)S(1)}, bf16[64,128]{1,0:T(8,128)(2,1)S(1)}, u32[]{:S(2)}, u32[]{:S(2)}) %collective-permute-start.15) | collective-permute-done | bytes 16416 | tf_op jit(solution)/shard_map/ppermute | solution.py:383
  45.2 0.6 %shard_map.107 = bf16[64,256]{1,0:T(8,128)(2,1)} custom-call(bf16[64,128]{1,0:T(8,128)(2,1)S(1)} %get-tuple-element.29.keep, bf16[64,128]{1,0:T(8,128)(2,1)S(1)} %collective-permute-done.15.got), custom_call_target="tpu_custom_call" | custom-call | bytes 262144 | tf_op jit(solution)/shard_map/pallas_call | solution.py:125
  (5 shorter events, 0.1 us)
Async XLA Ops:
  0.0 21.5 %collective-permute-start = (bf16[256,4096]{1,0:T(8,128)(2,1)}, bf16[256,4096]{1,0:T(8,128)(2,1)S(1)}, u32[]{:S(2)}, u32[]{:S(2)}) collective-permute-start(bf16[256,4096]{1,0:T(8,128)(2,1)} %mine.9), channel_id=1, source_target_pairs={{0,1},{1,0},{2,3},{3,2},{4,5},{5,4},{6,7},{7,6},{8,9},{9,8},{10,11... | collective-permute-start | bytes 6291464 | tf_op jit(solution)/shard_map/ppermute | solution.py:383
  1.6 9.1 %collective-permute-start.2 = (bf16[528,128]{1,0:T(8,128)(2,1)S(1)}, bf16[528,128]{1,0:T(8,128)(2,1)S(1)}, u32[]{:S(2)}, u32[]{:S(2)}) collective-permute-start(bf16[528,128]{1,0:T(8,128)(2,1)S(1)} %get-tuple-element.21.refs_0_), channel_id=1, source_target_pairs={{0,4},{4,8},{8,12},{12,0},{1,5},{5,9},{9,13},{13,1},{2,6},{6,10},{... | collective-permute-start | bytes 405512 | tf_op jit(solution)/shard_map/ppermute | solution.py:383
  4.3 8.6 %collective-permute-start.3 = (bf16[528,128]{1,0:T(8,128)(2,1)S(1)}, bf16[528,128]{1,0:T(8,128)(2,1)S(1)}, u32[]{:S(2)}, u32[]{:S(2)}) collective-permute-start(bf16[528,128]{1,0:T(8,128)(2,1)S(1)} %get-tuple-element.21.refs_0_), channel_id=1, source_target_pairs={{0,12},{4,0},{8,4},{12,8},{1,13},{5,1},{9,5},{13,9},{2,14},{6,2},{... | collective-permute-start | bytes 405512 | tf_op jit(solution)/shard_map/ppermute | solution.py:383
  10.8 7.5 %collective-permute-start.4 = (bf16[528,128]{1,0:T(8,128)(2,1)S(1)}, bf16[528,128]{1,0:T(8,128)(2,1)S(1)}, u32[]{:S(2)}, u32[]{:S(2)}) collective-permute-start(bf16[528,128]{1,0:T(8,128)(2,1)S(1)} %collective-permute-done.2.refs_0_.refs_1_), channel_id=1, source_target_pairs={{0,4},{4,8},{8,12},{12,0},{1,5},{5,9},{9,13},{13,1},{2,6},{6,10},{... | collective-permute-start | bytes 405512 | tf_op jit(solution)/shard_map/ppermute | solution.py:383
  10.8 14.5 %collective-permute-start.5 = (bf16[528,128]{1,0:T(8,128)(2,1)S(1)}, bf16[528,128]{1,0:T(8,128)(2,1)S(1)}, u32[]{:S(2)}, u32[]{:S(2)}) collective-permute-start(bf16[528,128]{1,0:T(8,128)(2,1)S(1)} %collective-permute-done.2.refs_0_.refs_1_), channel_id=1, source_target_pairs={{0,16},{16,0},{1,17},{17,1},{2,18},{18,2},{3,19},{19,3},{4,20},{20... | collective-permute-start | bytes 405512 | tf_op jit(solution)/shard_map/ppermute | solution.py:383
  12.9 13.2 %collective-permute-start.6 = (bf16[528,128]{1,0:T(8,128)(2,1)S(1)}, bf16[528,128]{1,0:T(8,128)(2,1)S(1)}, u32[]{:S(2)}, u32[]{:S(2)}) collective-permute-start(bf16[528,128]{1,0:T(8,128)(2,1)S(1)} %collective-permute-done.3.refs_1_.refs_3_), channel_id=1, source_target_pairs={{0,16},{16,0},{1,17},{17,1},{2,18},{18,2},{3,19},{19,3},{4,20},{20... | collective-permute-start | bytes 405512 | tf_op jit(solution)/shard_map/ppermute | solution.py:383
  18.3 7.8 %collective-permute-start.7 = (bf16[528,128]{1,0:T(8,128)(2,1)S(1)}, bf16[528,128]{1,0:T(8,128)(2,1)S(1)}, u32[]{:S(2)}, u32[]{:S(2)}) collective-permute-start(bf16[528,128]{1,0:T(8,128)(2,1)S(1)} %collective-permute-done.4.refs_2_), channel_id=1, source_target_pairs={{0,16},{16,0},{1,17},{17,1},{2,18},{18,2},{3,19},{19,3},{4,20},{20... | collective-permute-start | bytes 405512 | tf_op jit(solution)/shard_map/ppermute | solution.py:383
  19.8 1.2 %collective-permute-start.1 = (s32[1,1664]{1,0:T(1,128)S(1)}, s32[1,1664]{1,0:T(1,128)S(1)}, u32[]{:S(2)}, u32[]{:S(2)}) collective-permute-start(s32[1,1664]{1,0:T(1,128)S(1)} %get-tuple-element.18.mine), channel_id=1, source_target_pairs={{0,1},{1,0},{2,3},{3,2},{4,5},{5,4},{6,7},{7,6},{8,9},{9,8},{10,11... | collective-permute-start | bytes 19976 | tf_op jit(solution)/shard_map/ppermute | solution.py:383
  21.2 11.1 %collective-permute-start.8 = (f32[16,256]{1,0:T(8,128)S(1)}, f32[16,256]{1,0:T(8,128)S(1)}, u32[]{:S(2)}, u32[]{:S(2)}) collective-permute-start(f32[16,256]{1,0:T(8,128)S(1)} %shard_map.100.tally), channel_id=1, source_target_pairs={{0,1},{1,0},{2,3},{3,2},{4,5},{5,4},{6,7},{7,6},{8,9},{9,8},{10,11... | collective-permute-start | bytes 49160 | tf_op jit(solution)/shard_map/ppermute | solution.py:383
  21.5 1.6 %copy-start = (bf16[256,4096]{1,0:T(8,128)(2,1)S(1)}, bf16[256,4096]{1,0:T(8,128)(2,1)}, u32[]{:S(2)}) copy-start(bf16[256,4096]{1,0:T(8,128)(2,1)} %mine.9) | copy-start | bytes 6291460
  23.1 1.6 %copy-start.1 = (bf16[256,4096]{1,0:T(8,128)(2,1)S(1)}, bf16[256,4096]{1,0:T(8,128)(2,1)}, u32[]{:S(2)}) copy-start(bf16[256,4096]{1,0:T(8,128)(2,1)} %mine.9) | copy-start | bytes 6291460
  26.3 7.2 %collective-permute-start.9 = (bf16[128,128]{1,0:T(8,128)(2,1)S(1)}, bf16[128,128]{1,0:T(8,128)(2,1)S(1)}, u32[]{:S(2)}, u32[]{:S(2)}) collective-permute-start(bf16[128,128]{1,0:T(8,128)(2,1)S(1)} %shard_map.97.query), channel_id=1, source_target_pairs={{0,4},{4,8},{8,12},{12,0},{1,5},{5,9},{9,13},{13,1},{2,6},{6,10},{... | collective-permute-start | bytes 98312 | tf_op jit(solution)/shard_map/ppermute | solution.py:383
  26.4 8.5 %collective-permute-start.11 = (bf16[128,128]{1,0:T(8,128)(2,1)S(1)}, bf16[128,128]{1,0:T(8,128)(2,1)S(1)}, u32[]{:S(2)}, u32[]{:S(2)}) collective-permute-start(bf16[128,128]{1,0:T(8,128)(2,1)S(1)} %shard_map.97.query), channel_id=1, source_target_pairs={{0,12},{4,0},{8,4},{12,8},{1,13},{5,1},{9,5},{13,9},{2,14},{6,2},{... | collective-permute-start | bytes 98312 | tf_op jit(solution)/shard_map/ppermute | solution.py:383
  32.9 5.1 %collective-permute-start.13 = (bf16[128,128]{1,0:T(8,128)(2,1)S(1)}, bf16[128,128]{1,0:T(8,128)(2,1)S(1)}, u32[]{:S(2)}, u32[]{:S(2)}) collective-permute-start(bf16[128,128]{1,0:T(8,128)(2,1)S(1)} %shard_map.97.query), channel_id=1, source_target_pairs={{0,8},{4,12},{8,0},{12,4},{1,9},{5,13},{9,1},{13,5},{2,10},{6,14},... | collective-permute-start | bytes 98312 | tf_op jit(solution)/shard_map/ppermute | solution.py:383
  34.2 7.2 %collective-permute-start.10 = (bf16[128,128]{1,0:T(8,128)(2,1)S(1)}, bf16[128,128]{1,0:T(8,128)(2,1)S(1)}, u32[]{:S(2)}, u32[]{:S(2)}) collective-permute-start(bf16[128,128]{1,0:T(8,128)(2,1)S(1)} %shard_map.103), channel_id=1, source_target_pairs={{0,12},{4,0},{8,4},{12,8},{1,13},{5,1},{9,5},{13,9},{2,14},{6,2},{... | collective-permute-start | bytes 98312 | tf_op jit(solution)/shard_map/ppermute | solution.py:383
  35.6 5.9 %collective-permute-start.12 = (bf16[128,128]{1,0:T(8,128)(2,1)S(1)}, bf16[128,128]{1,0:T(8,128)(2,1)S(1)}, u32[]{:S(2)}, u32[]{:S(2)}) collective-permute-start(bf16[128,128]{1,0:T(8,128)(2,1)S(1)} %shard_map.104), channel_id=1, source_target_pairs={{0,4},{4,8},{8,12},{12,0},{1,5},{5,9},{9,13},{13,1},{2,6},{6,10},{... | collective-permute-start | bytes 98312 | tf_op jit(solution)/shard_map/ppermute | solution.py:383
  38.7 5.2 %collective-permute-start.14 = (bf16[128,128]{1,0:T(8,128)(2,1)S(1)}, bf16[128,128]{1,0:T(8,128)(2,1)S(1)}, u32[]{:S(2)}, u32[]{:S(2)}) collective-permute-start(bf16[128,128]{1,0:T(8,128)(2,1)S(1)} %shard_map.105), channel_id=1, source_target_pairs={{0,8},{4,12},{8,0},{12,4},{1,9},{5,13},{9,1},{13,5},{2,10},{6,14},... | collective-permute-start | bytes 98312 | tf_op jit(solution)/shard_map/ppermute | solution.py:383
  44.0 1.2 %collective-permute-start.15 = (bf16[64,128]{1,0:T(8,128)(2,1)S(1)}, bf16[64,128]{1,0:T(8,128)(2,1)S(1)}, u32[]{:S(2)}, u32[]{:S(2)}) collective-permute-start(bf16[64,128]{1,0:T(8,128)(2,1)S(1)} %get-tuple-element.30), channel_id=1, source_target_pairs={{0,1},{1,0},{2,3},{3,2},{4,5},{5,4},{6,7},{7,6},{8,9},{9,8},{10,11... | collective-permute-start | bytes 49160 | tf_op jit(solution)/shard_map/ppermute | solution.py:383

commit v7 on v6

--- a/solution.py
+++ b/solution.py
@@ -154,10 +154,9 @@
 
 
 def share_kernel(
-    adapter, item_user, routes, cand_index, hist_user, block, out, mine, user, owner, cand, event, events, sems
+    adapter, item_user, routes, cand_index, hist_user, out, mine, user, owner, cand, event, events, sems
 ):
-    _, cols = block.shape
-    rows = out.shape[0] - LISTED
+    rows, cols = out.shape[0] - LISTED, out.shape[1]
     row = pl.multiple_of(lax.axis_index("groups") * rows, rows)
     columns = pl.ds(col_start(cols), cols)
     part = event.shape[1]
@@ -167,8 +166,7 @@
         pltpu.make_async_copy(cand_index, cand, sems.at[2]),
         pltpu.make_async_copy(hist_user.at[:, pl.ds(col_start(part), part)], event, sems.at[3]),
         pltpu.make_async_copy(adapter.at[pl.ds(row, rows), columns], out.at[pl.ds(0, rows)], sems.at[4]),
-        pltpu.make_async_copy(adapter.at[:, columns], block, sems.at[5]),
-        pltpu.make_async_copy(hist_user, events, sems.at[6]),
+        pltpu.make_async_copy(hist_user, events, sems.at[5]),
     ]
     for copy in copies:
         copy.start()
@@ -262,13 +260,14 @@
         out[k] = jnp.where(column == user, inverse, 0.0)
 
 
-def project_kernel(hist_emb, key_weight, value_weight, key_t, value, emb, keys, values, sems):
+def project_kernel(adapter, hist_emb, key_weight, value_weight, key_t, value, block, emb, keys, values, sems):
     width = value.shape[1]
     columns = pl.ds(col_start(width), width)
     copies = [
         pltpu.make_async_copy(key_weight.at[:, columns], keys, sems.at[0]),
         pltpu.make_async_copy(value_weight.at[:, columns], values, sems.at[1]),
         pltpu.make_async_copy(hist_emb, emb, sems.at[2]),
+        pltpu.make_async_copy(adapter.at[:, columns], block, sems.at[3]),
     ]
     for copy in copies:
         copy.start()
@@ -398,10 +397,9 @@
     events, dim = hist_emb.shape
     order = shift_order(n)
 
-    block, own_share, mine = call(
+    own_share, mine = call(
         share_kernel,
         (
-            shape((depth, width), BF16),
             shape((depth // groups + LISTED, width), BF16),
             shape((1, 2 * items + cands + events), jnp.int32),
         ),
@@ -419,7 +417,7 @@
             pltpu.VMEM((1, cands // 2), jnp.int32),
             pltpu.VMEM((1, events // 2), jnp.int32),
             pltpu.VMEM((1, events), jnp.int32),
-            pltpu.SemaphoreType.DMA((7,)),
+            pltpu.SemaphoreType.DMA((6,)),
         ],
     )
     along = {}
@@ -433,18 +431,18 @@
     other = shift(mine, "rep", 1)
     keys = events + 2 * items
     hot, pick = call(users_kernel, (shape((USERS, keys), BF16), shape((cands, 2 * items), BF16)), (mine, other))
-    key_t, value = call(
+    key_t, value, block = call(
         project_kernel,
-        (shape((width, events), BF16), shape((events, width), BF16)),
-        (hist_emb, key_weight, value_weight),
+        (shape((width, events), BF16), shape((events, width), BF16), shape((depth, width), BF16)),
+        (adapter, hist_emb, key_weight, value_weight),
         flops=4 * events * dim * width,
         bytes_accessed=4 << 20,
-        specs=[HBM] * 3,
+        specs=[HBM] * 4,
         scratch=[
             pltpu.VMEM((events, dim), BF16),
             pltpu.VMEM((dim, width), BF16),
             pltpu.VMEM((dim, width), BF16),
-            pltpu.SemaphoreType.DMA((3,)),
+            pltpu.SemaphoreType.DMA((4,)),
         ],
     )
     total = call(

time: 46.1 us -> 41.9 us (0.909)
  local copies, waits for them, and re-layouts: 2.75 us -> 0.01 us
  waiting for transfers between devices: 14.4 us -> 12.7 us
    unnamed x4 -> x2, local copies, waits for them, and re-layouts: 2.75 us -> 0.01 us
    ppermute x16, waiting for transfers between devices: 14.4 us -> 12.7 us  [shift(): lax.ppermute(value, axis, [(i, (i + k) % count) for i in range(count)])]
  transfers between devices with their start and end apart: 16 -> 16, of which waited for: 7 -> 8; matrix products, arithmetic and copies ran while one was open for 0% -> 0% of each run, Pallas kernels for 21% -> 22%
where the time goes in v7:
time: 41.9 us; the launch traced here: 41.7 us
  starting transfers between devices  18.7 us (45%)
  waiting for transfers between devices  12.7 us (30%)
  Pallas kernels  10.2 us (24%)
    ppermute x16, starting transfers between devices, shift(): lax.ppermute(value, axis, [(i, (i + k) % count) for i in range(count)])  18.7 us
    ppermute x16, waiting for transfers between devices, shift(): lax.ppermute(value, axis, [(i, (i + k) % count) for i in range(count)])  12.7 us
    pallas_call x17, Pallas kernels, call(): pl.pallas_call(kernel, out_shape=outs, in_specs=specs or [VM] * len(args)...  10.2 us
  transfers between devices with their start and end apart: 16, of which 8 were waited for; matrix products, arithmetic and copies ran while one was open for 0% of the time, Pallas kernels for 22%

profile of v7, /device:TPU:0, one launch (start us, length us, event | category | flops | bytes accessed | tf_op | source)
XLA Modules:
  0.0 41.7 jit_solution(3504384895170623220)
XLA Ops:
  0.0 0.5 %collective-permute-start = (bf16[256,4096]{1,0:T(8,128)(2,1)}, bf16[256,4096]{1,0:T(8,128)(2,1)S(1)}, u32[]{:S(2)}, u32[]{:S(2)}) collective-permute-start(bf16[256,4096]{1,0:T(8,128)(2,1)} %mine.9), channel_id=1, source_target_pairs={{0,1},{1,0},{2,3},{3,2},{4,5},{5,4},{6,7},{7,6},{8,9},{9,8},{10,11... | collective-permute-start | bytes 6291464 | tf_op jit(solution)/shard_map/ppermute | solution.py:382
  0.5 1.2 %shard_map.91 = (bf16[528,128]{1,0:T(8,128)(2,1)S(1)}, s32[1,1664]{1,0:T(1,128)S(1)}) custom-call(bf16[1024,256]{1,0:T(8,128)(2,1)} %adapter.3, s32[1,256]{1,0:T(1,128)} %bitcast.5, s32[1,256]{1,0:T(1,128)} %bitcast.6, s32[1,64]{1,0:T(1,128)} %bitcast.7, s32[1,1024]{1,0:T(1,128)} %bitcast.4), custom_call_target="tpu_custom_call" | custom-call | bytes 262144 | tf_op jit(solution)/shard_map/pallas_call | solution.py:125
  1.7 2.6 %collective-permute-start.2 = (bf16[528,128]{1,0:T(8,128)(2,1)S(1)}, bf16[528,128]{1,0:T(8,128)(2,1)S(1)}, u32[]{:S(2)}, u32[]{:S(2)}) collective-permute-start(bf16[528,128]{1,0:T(8,128)(2,1)S(1)} %get-tuple-element.21.refs_0_), channel_id=1, source_target_pairs={{0,4},{4,8},{8,12},{12,0},{1,5},{5,9},{9,13},{13,1},{2,6},{6,10},{... | collective-permute-start | bytes 405512 | tf_op jit(solution)/shard_map/ppermute | solution.py:382
  4.3 2.1 %collective-permute-start.3 = (bf16[528,128]{1,0:T(8,128)(2,1)S(1)}, bf16[528,128]{1,0:T(8,128)(2,1)S(1)}, u32[]{:S(2)}, u32[]{:S(2)}) collective-permute-start(bf16[528,128]{1,0:T(8,128)(2,1)S(1)} %get-tuple-element.21.refs_0_), channel_id=1, source_target_pairs={{0,12},{4,0},{8,4},{12,8},{1,13},{5,1},{9,5},{13,9},{2,14},{6,2},{... | collective-permute-start | bytes 405512 | tf_op jit(solution)/shard_map/ppermute | solution.py:382
  6.4 4.4 %collective-permute-done.2.refs_0_.refs_1_ = bf16[528,128]{1,0:T(8,128)(2,1)S(1)} collective-permute-done((bf16[528,128]{1,0:T(8,128)(2,1)S(1)}, bf16[528,128]{1,0:T(8,128)(2,1)S(1)}, u32[]{:S(2)}, u32[]{:S(2)}) %collective-permute-start.2) | collective-permute-done | bytes 135200 | tf_op jit(solution)/shard_map/ppermute | solution.py:382
  10.8 0.0 collective-permute-start.4
  10.8 1.7 %collective-permute-start.5 = (bf16[528,128]{1,0:T(8,128)(2,1)S(1)}, bf16[528,128]{1,0:T(8,128)(2,1)S(1)}, u32[]{:S(2)}, u32[]{:S(2)}) collective-permute-start(bf16[528,128]{1,0:T(8,128)(2,1)S(1)} %collective-permute-done.2.refs_0_.refs_1_), channel_id=1, source_target_pairs={{0,16},{16,0},{1,17},{17,1},{2,18},{18,2},{3,19},{19,3},{4,20},{20... | collective-permute-start | bytes 405512 | tf_op jit(solution)/shard_map/ppermute | solution.py:382
  12.6 0.2 collective-permute-done.3.refs_1_.refs_3_
  12.8 1.5 %collective-permute-start.6 = (bf16[528,128]{1,0:T(8,128)(2,1)S(1)}, bf16[528,128]{1,0:T(8,128)(2,1)S(1)}, u32[]{:S(2)}, u32[]{:S(2)}) collective-permute-start(bf16[528,128]{1,0:T(8,128)(2,1)S(1)} %collective-permute-done.3.refs_1_.refs_3_), channel_id=1, source_target_pairs={{0,16},{16,0},{1,17},{17,1},{2,18},{18,2},{3,19},{19,3},{4,20},{20... | collective-permute-start | bytes 405512 | tf_op jit(solution)/shard_map/ppermute | solution.py:382
  14.3 3.9 %collective-permute-done.4.refs_2_ = bf16[528,128]{1,0:T(8,128)(2,1)S(1)} collective-permute-done((bf16[528,128]{1,0:T(8,128)(2,1)S(1)}, bf16[528,128]{1,0:T(8,128)(2,1)S(1)}, u32[]{:S(2)}, u32[]{:S(2)}) %collective-permute-start.4) | collective-permute-done | bytes 135200 | tf_op jit(solution)/shard_map/ppermute | solution.py:382
  18.2 1.5 %collective-permute-start.7 = (bf16[528,128]{1,0:T(8,128)(2,1)S(1)}, bf16[528,128]{1,0:T(8,128)(2,1)S(1)}, u32[]{:S(2)}, u32[]{:S(2)}) collective-permute-start(bf16[528,128]{1,0:T(8,128)(2,1)S(1)} %collective-permute-done.4.refs_2_), channel_id=1, source_target_pairs={{0,16},{16,0},{1,17},{17,1},{2,18},{18,2},{3,19},{19,3},{4,20},{20... | collective-permute-start | bytes 405512 | tf_op jit(solution)/shard_map/ppermute | solution.py:382
  19.7 0.0 collective-permute-start.1
  19.7 2.2 %shard_map.93 = (bf16[128,1024]{1,0:T(8,128)(2,1)S(1)}, bf16[1024,128]{1,0:T(8,128)(2,1)S(1)}, bf16[1024,128]{1,0:T(8,128)(2,1)S(1)}) custom-call(bf16[1024,256]{1,0:T(8,128)(2,1)} %adapter.3, bf16[1024,512]{1,0:T(8,128)(2,1)} %hist_emb.1, bf16[512,256]{1,0:T(8,128)(2,1)} %key_weight.1, bf16[512,256]{1,0:T(8,128)(2,1)} %value_weight.1), custom_call_target="tpu_custom_call" | custom-call | flops 268435456 | bytes 4194304 | tf_op jit(solution)/shard_map/pallas_call | solution.py:125
  21.9 0.0 collective-permute-done.1.other
  21.9 0.2 shard_map.92
  22.2 0.0 collective-permute-done.other
  22.2 0.0 copy-done
  22.2 0.4 %shard_map.94.total = f32[512,128]{1,0:T(8,128)S(1)} custom-call(bf16[256,4096]{1,0:T(8,128)(2,1)S(1)} %copy-done, bf16[256,4096]{1,0:T(8,128)(2,1)S(1)} %collective-permute-done.other, bf16[1024,128]{1,0:T(8,128)(2,1)S(1)} %get-tuple-element.20.block), custom_call_target="tpu_custom_call" | custom-call | flops 134217728 | bytes 4194304 | tf_op jit(solution)/shard_map/pallas_call | solution.py:125
  22.6 0.6 %shard_map.95.total = f32[512,128]{1,0:T(8,128)S(1)} custom-call(bf16[256,4096]{1,0:T(8,128)(2,1)S(1)} %copy-done, bf16[256,4096]{1,0:T(8,128)(2,1)S(1)} %collective-permute-done.other, f32[512,128]{1,0:T(8,128)S(1)} %shard_map.94.total, bf16[528,128]{1,0:T(8,128)(2,1)S(1)} %collective-permute-done.2.refs_0_.refs_1_, ...), custom_call_target="tpu_custom_call" | custom-call | flops 134217728 | bytes 2097152 | tf_op jit(solution)/shard_map/pallas_call | solution.py:125
  23.2 0.0 collective-permute-done.5.refs_0_
  23.2 0.3 shard_map.96.total
  23.5 0.5 %shard_map.97 = (f32[128,128]{1,0:T(8,128)S(1)}, bf16[128,1024]{1,0:T(8,128)(2,1)S(1)}) custom-call(bf16[256,4096]{1,0:T(8,128)(2,1)S(1)} %copy-done, bf16[256,4096]{1,0:T(8,128)(2,1)S(1)} %collective-permute-done.other, bf16[128,512]{1,0:T(8,128)(2,1)S(1)} %get-tuple-element.19.pick, f32[512,128]{1,0:T(8,128)S(1)} %shard_map.96.total), custom_call_target="tpu_custom_call" | custom-call | flops 167772160 | bytes 262144 | tf_op jit(solution)/shard_map/pallas_call | solution.py:125
  24.0 0.0 collective-permute-done.6.refs_0_
  24.0 0.0 collective-permute-done.7.refs_1_
  24.0 0.2 shard_map.98.query
  24.3 0.1 collective-permute-start.9
  24.4 0.6 %collective-permute-start.8 = (f32[16,256]{1,0:T(8,128)S(1)}, f32[16,256]{1,0:T(8,128)S(1)}, u32[]{:S(2)}, u32[]{:S(2)}) collective-permute-start(f32[16,256]{1,0:T(8,128)S(1)} %shard_map.100.tally), channel_id=1, source_target_pairs={{0,1},{1,0},{2,3},{3,2},{4,5},{5,4},{6,7},{7,6},{8,9},{9,8},{10,11... | collective-permute-start | bytes 49160 | tf_op jit(solution)/shard_map/ppermute | solution.py:382
  24.9 3.5 %collective-permute-start.11 = (bf16[128,128]{1,0:T(8,128)(2,1)S(1)}, bf16[128,128]{1,0:T(8,128)(2,1)S(1)}, u32[]{:S(2)}, u32[]{:S(2)}) collective-permute-start(bf16[128,128]{1,0:T(8,128)(2,1)S(1)} %shard_map.98.query), channel_id=1, source_target_pairs={{0,12},{4,0},{8,4},{12,8},{1,13},{5,1},{9,5},{13,9},{2,14},{6,2},{... | collective-permute-start | bytes 98312 | tf_op jit(solution)/shard_map/ppermute | solution.py:382
  28.5 0.0 collective-permute-done.8.tally_other
  28.5 0.6 %shard_map.101.scale = f32[4,128,1536]{2,1,0:T(8,128)S(1)} custom-call(s32[1,1664]{1,0:T(1,128)S(1)} %get-tuple-element.18.mine, s32[1,1664]{1,0:T(1,128)S(1)} %collective-permute-done.1.other, bf16[256,1536]{1,0:T(8,128)(2,1)S(1)} %get-tuple-element.28.hot, f32[16,256]{1,0:T(8,128)S(1)} %shard_map.100.tally, f32[16,256]{1,0:T(8,128)S(1)} %collective-permute-done.8.tally_other), custom_call_target="tpu_custom_call" | custom-call | bytes 4194304 | tf_op jit(solution)/shard_map/pallas_call | solution.py:125
  29.0 0.1 collective-permute-start.13
  29.1 0.5 %shard_map.99 = (bf16[512,128]{1,0:T(8,128)(2,1)S(1)}, bf16[128,512]{1,0:T(8,128)(2,1)S(1)}) custom-call(bf16[256,4096]{1,0:T(8,128)(2,1)S(1)} %copy-done, bf16[256,4096]{1,0:T(8,128)(2,1)S(1)} %collective-permute-done.other, f32[512,128]{1,0:T(8,128)S(1)} %shard_map.96.total, bf16[528,128]{1,0:T(8,128)(2,1)S(1)} %collective-permute-done.6.refs_0_, ...), custom_call_target="tpu_custom_call" | custom-call | flops 134217728 | bytes 2097152 | tf_op jit(solution)/shard_map/pallas_call | solution.py:125
  29.6 0.7 %collective-permute-done.9.query = bf16[128,128]{1,0:T(8,128)(2,1)S(1)} collective-permute-done((bf16[128,128]{1,0:T(8,128)(2,1)S(1)}, bf16[128,128]{1,0:T(8,128)(2,1)S(1)}, u32[]{:S(2)}, u32[]{:S(2)}) %collective-permute-start.9) | collective-permute-done | bytes 32800 | tf_op jit(solution)/shard_map/ppermute | solution.py:382
  30.3 0.7 %shard_map.103 = bf16[128,128]{1,0:T(8,128)(2,1)S(1)} custom-call(bf16[128,128]{1,0:T(8,128)(2,1)S(1)} %collective-permute-done.9.query, bf16[128,1024]{1,0:T(8,128)(2,1)S(1)} %get-tuple-element.24.key_t, bf16[1024,128]{1,0:T(8,128)(2,1)S(1)} %get-tuple-element.25.value, bf16[128,512]{1,0:T(8,128)(2,1)S(1)} %get-tuple-element.26.rows_t, ...), custom_call_target="tpu_custom_call" | custom-call | flops 201326592 | bytes 1048576 | tf_op jit(solution)/shard_map/pallas_call | solution.py:125
  31.0 0.4 collective-permute-start.10
  31.4 0.0 collective-permute-done.11.query
  31.4 0.7 %shard_map.104 = bf16[128,128]{1,0:T(8,128)(2,1)S(1)} custom-call(bf16[128,128]{1,0:T(8,128)(2,1)S(1)} %collective-permute-done.11.query, bf16[128,1024]{1,0:T(8,128)(2,1)S(1)} %get-tuple-element.24.key_t, bf16[1024,128]{1,0:T(8,128)(2,1)S(1)} %get-tuple-element.25.value, bf16[128,512]{1,0:T(8,128)(2,1)S(1)} %get-tuple-element.26.rows_t, ...), custom_call_target="tpu_custom_call" | custom-call | flops 201326592 | bytes 1048576 | tf_op jit(solution)/shard_map/pallas_call | solution.py:125
  32.1 1.8 %collective-permute-start.12 = (bf16[128,128]{1,0:T(8,128)(2,1)S(1)}, bf16[128,128]{1,0:T(8,128)(2,1)S(1)}, u32[]{:S(2)}, u32[]{:S(2)}) collective-permute-start(bf16[128,128]{1,0:T(8,128)(2,1)S(1)} %shard_map.104), channel_id=1, source_target_pairs={{0,4},{4,8},{8,12},{12,0},{1,5},{5,9},{9,13},{13,1},{2,6},{6,10},{... | collective-permute-start | bytes 98312 | tf_op jit(solution)/shard_map/ppermute | solution.py:382
  33.8 0.1 collective-permute-done.13.query
  33.9 0.7 %shard_map.105 = bf16[128,128]{1,0:T(8,128)(2,1)S(1)} custom-call(bf16[128,128]{1,0:T(8,128)(2,1)S(1)} %collective-permute-done.13.query, bf16[128,1024]{1,0:T(8,128)(2,1)S(1)} %get-tuple-element.24.key_t, bf16[1024,128]{1,0:T(8,128)(2,1)S(1)} %get-tuple-element.25.value, bf16[128,512]{1,0:T(8,128)(2,1)S(1)} %get-tuple-element.26.rows_t, ...), custom_call_target="tpu_custom_call" | custom-call | flops 201326592 | bytes 1048576 | tf_op jit(solution)/shard_map/pallas_call | solution.py:125
  34.6 2.3 %collective-permute-start.14 = (bf16[128,128]{1,0:T(8,128)(2,1)S(1)}, bf16[128,128]{1,0:T(8,128)(2,1)S(1)}, u32[]{:S(2)}, u32[]{:S(2)}) collective-permute-start(bf16[128,128]{1,0:T(8,128)(2,1)S(1)} %shard_map.105), channel_id=1, source_target_pairs={{0,8},{4,12},{8,0},{12,4},{1,9},{5,13},{9,1},{13,5},{2,10},{6,14},... | collective-permute-start | bytes 98312 | tf_op jit(solution)/shard_map/ppermute | solution.py:382
  36.9 0.7 %shard_map.102.own = f32[128,128]{1,0:T(8,128)S(1)} custom-call(bf16[128,128]{1,0:T(8,128)(2,1)S(1)} %shard_map.98.query, bf16[128,1024]{1,0:T(8,128)(2,1)S(1)} %get-tuple-element.24.key_t, bf16[1024,128]{1,0:T(8,128)(2,1)S(1)} %get-tuple-element.25.value, bf16[128,512]{1,0:T(8,128)(2,1)S(1)} %get-tuple-element.26.rows_t, ...), custom_call_target="tpu_custom_call" | custom-call | flops 201326592 | bytes 1048576 | tf_op jit(solution)/shard_map/pallas_call | solution.py:125
  37.6 0.0 collective-permute-done.10.refs_0_
  37.6 0.3 collective-permute-done.12.refs_1_
  37.9 2.0 %collective-permute-done.14.refs_2_ = bf16[128,128]{1,0:T(8,128)(2,1)S(1)} collective-permute-done((bf16[128,128]{1,0:T(8,128)(2,1)S(1)}, bf16[128,128]{1,0:T(8,128)(2,1)S(1)}, u32[]{:S(2)}, u32[]{:S(2)}) %collective-permute-start.14) | collective-permute-done | bytes 32800 | tf_op jit(solution)/shard_map/ppermute | solution.py:382
  39.9 0.1 collective-permute-start.15
  40.0 1.2 %collective-permute-done.15.got = bf16[64,128]{1,0:T(8,128)(2,1)S(1)} collective-permute-done((bf16[64,128]{1,0:T(8,128)(2,1)S(1)}, bf16[64,128]{1,0:T(8,128)(2,1)S(1)}, u32[]{:S(2)}, u32[]{:S(2)}) %collective-permute-start.15) | collective-permute-done | bytes 16416 | tf_op jit(solution)/shard_map/ppermute | solution.py:382
  41.1 0.6 %shard_map.107 = bf16[64,256]{1,0:T(8,128)(2,1)} custom-call(bf16[64,128]{1,0:T(8,128)(2,1)S(1)} %get-tuple-element.29.keep, bf16[64,128]{1,0:T(8,128)(2,1)S(1)} %collective-permute-done.15.got), custom_call_target="tpu_custom_call" | custom-call | bytes 262144 | tf_op jit(solution)/shard_map/pallas_call | solution.py:125
  (3 shorter events, 0.1 us)
Async XLA Ops:
  0.0 22.2 %copy-start = (bf16[256,4096]{1,0:T(8,128)(2,1)S(1)}, bf16[256,4096]{1,0:T(8,128)(2,1)}, u32[]{:S(2)}) copy-start(bf16[256,4096]{1,0:T(8,128)(2,1)} %mine.9) | copy-start | bytes 6291460
  0.0 22.2 %collective-permute-start = (bf16[256,4096]{1,0:T(8,128)(2,1)}, bf16[256,4096]{1,0:T(8,128)(2,1)S(1)}, u32[]{:S(2)}, u32[]{:S(2)}) collective-permute-start(bf16[256,4096]{1,0:T(8,128)(2,1)} %mine.9), channel_id=1, source_target_pairs={{0,1},{1,0},{2,3},{3,2},{4,5},{5,4},{6,7},{7,6},{8,9},{9,8},{10,11... | collective-permute-start | bytes 6291464 | tf_op jit(solution)/shard_map/ppermute | solution.py:382
  1.7 9.1 %collective-permute-start.2 = (bf16[528,128]{1,0:T(8,128)(2,1)S(1)}, bf16[528,128]{1,0:T(8,128)(2,1)S(1)}, u32[]{:S(2)}, u32[]{:S(2)}) collective-permute-start(bf16[528,128]{1,0:T(8,128)(2,1)S(1)} %get-tuple-element.21.refs_0_), channel_id=1, source_target_pairs={{0,4},{4,8},{8,12},{12,0},{1,5},{5,9},{9,13},{13,1},{2,6},{6,10},{... | collective-permute-start | bytes 405512 | tf_op jit(solution)/shard_map/ppermute | solution.py:382
  4.3 8.5 %collective-permute-start.3 = (bf16[528,128]{1,0:T(8,128)(2,1)S(1)}, bf16[528,128]{1,0:T(8,128)(2,1)S(1)}, u32[]{:S(2)}, u32[]{:S(2)}) collective-permute-start(bf16[528,128]{1,0:T(8,128)(2,1)S(1)} %get-tuple-element.21.refs_0_), channel_id=1, source_target_pairs={{0,12},{4,0},{8,4},{12,8},{1,13},{5,1},{9,5},{13,9},{2,14},{6,2},{... | collective-permute-start | bytes 405512 | tf_op jit(solution)/shard_map/ppermute | solution.py:382
  10.8 7.4 %collective-permute-start.4 = (bf16[528,128]{1,0:T(8,128)(2,1)S(1)}, bf16[528,128]{1,0:T(8,128)(2,1)S(1)}, u32[]{:S(2)}, u32[]{:S(2)}) collective-permute-start(bf16[528,128]{1,0:T(8,128)(2,1)S(1)} %collective-permute-done.2.refs_0_.refs_1_), channel_id=1, source_target_pairs={{0,4},{4,8},{8,12},{12,0},{1,5},{5,9},{9,13},{13,1},{2,6},{6,10},{... | collective-permute-start | bytes 405512 | tf_op jit(solution)/shard_map/ppermute | solution.py:382
  10.8 12.4 %collective-permute-start.5 = (bf16[528,128]{1,0:T(8,128)(2,1)S(1)}, bf16[528,128]{1,0:T(8,128)(2,1)S(1)}, u32[]{:S(2)}, u32[]{:S(2)}) collective-permute-start(bf16[528,128]{1,0:T(8,128)(2,1)S(1)} %collective-permute-done.2.refs_0_.refs_1_), channel_id=1, source_target_pairs={{0,16},{16,0},{1,17},{17,1},{2,18},{18,2},{3,19},{19,3},{4,20},{20... | collective-permute-start | bytes 405512 | tf_op jit(solution)/shard_map/ppermute | solution.py:382
  12.8 11.2 %collective-permute-start.6 = (bf16[528,128]{1,0:T(8,128)(2,1)S(1)}, bf16[528,128]{1,0:T(8,128)(2,1)S(1)}, u32[]{:S(2)}, u32[]{:S(2)}) collective-permute-start(bf16[528,128]{1,0:T(8,128)(2,1)S(1)} %collective-permute-done.3.refs_1_.refs_3_), channel_id=1, source_target_pairs={{0,16},{16,0},{1,17},{17,1},{2,18},{18,2},{3,19},{19,3},{4,20},{20... | collective-permute-start | bytes 405512 | tf_op jit(solution)/shard_map/ppermute | solution.py:382
  18.2 5.8 %collective-permute-start.7 = (bf16[528,128]{1,0:T(8,128)(2,1)S(1)}, bf16[528,128]{1,0:T(8,128)(2,1)S(1)}, u32[]{:S(2)}, u32[]{:S(2)}) collective-permute-start(bf16[528,128]{1,0:T(8,128)(2,1)S(1)} %collective-permute-done.4.refs_2_), channel_id=1, source_target_pairs={{0,16},{16,0},{1,17},{17,1},{2,18},{18,2},{3,19},{19,3},{4,20},{20... | collective-permute-start | bytes 405512 | tf_op jit(solution)/shard_map/ppermute | solution.py:382
  19.7 2.2 %collective-permute-start.1 = (s32[1,1664]{1,0:T(1,128)S(1)}, s32[1,1664]{1,0:T(1,128)S(1)}, u32[]{:S(2)}, u32[]{:S(2)}) collective-permute-start(s32[1,1664]{1,0:T(1,128)S(1)} %get-tuple-element.18.mine), channel_id=1, source_target_pairs={{0,1},{1,0},{2,3},{3,2},{4,5},{5,4},{6,7},{7,6},{8,9},{9,8},{10,11... | collective-permute-start | bytes 19976 | tf_op jit(solution)/shard_map/ppermute | solution.py:382
  24.3 6.0 %collective-permute-start.9 = (bf16[128,128]{1,0:T(8,128)(2,1)S(1)}, bf16[128,128]{1,0:T(8,128)(2,1)S(1)}, u32[]{:S(2)}, u32[]{:S(2)}) collective-permute-start(bf16[128,128]{1,0:T(8,128)(2,1)S(1)} %shard_map.98.query), channel_id=1, source_target_pairs={{0,4},{4,8},{8,12},{12,0},{1,5},{5,9},{9,13},{13,1},{2,6},{6,10},{... | collective-permute-start | bytes 98312 | tf_op jit(solution)/shard_map/ppermute | solution.py:382
  24.4 4.1 %collective-permute-start.8 = (f32[16,256]{1,0:T(8,128)S(1)}, f32[16,256]{1,0:T(8,128)S(1)}, u32[]{:S(2)}, u32[]{:S(2)}) collective-permute-start(f32[16,256]{1,0:T(8,128)S(1)} %shard_map.100.tally), channel_id=1, source_target_pairs={{0,1},{1,0},{2,3},{3,2},{4,5},{5,4},{6,7},{7,6},{8,9},{9,8},{10,11... | collective-permute-start | bytes 49160 | tf_op jit(solution)/shard_map/ppermute | solution.py:382
  24.9 6.4 %collective-permute-start.11 = (bf16[128,128]{1,0:T(8,128)(2,1)S(1)}, bf16[128,128]{1,0:T(8,128)(2,1)S(1)}, u32[]{:S(2)}, u32[]{:S(2)}) collective-permute-start(bf16[128,128]{1,0:T(8,128)(2,1)S(1)} %shard_map.98.query), channel_id=1, source_target_pairs={{0,12},{4,0},{8,4},{12,8},{1,13},{5,1},{9,5},{13,9},{2,14},{6,2},{... | collective-permute-start | bytes 98312 | tf_op jit(solution)/shard_map/ppermute | solution.py:382
  29.0 4.9 %collective-permute-start.13 = (bf16[128,128]{1,0:T(8,128)(2,1)S(1)}, bf16[128,128]{1,0:T(8,128)(2,1)S(1)}, u32[]{:S(2)}, u32[]{:S(2)}) collective-permute-start(bf16[128,128]{1,0:T(8,128)(2,1)S(1)} %shard_map.98.query), channel_id=1, source_target_pairs={{0,8},{4,12},{8,0},{12,4},{1,9},{5,13},{9,1},{13,5},{2,10},{6,14},... | collective-permute-start | bytes 98312 | tf_op jit(solution)/shard_map/ppermute | solution.py:382
  31.0 6.6 %collective-permute-start.10 = (bf16[128,128]{1,0:T(8,128)(2,1)S(1)}, bf16[128,128]{1,0:T(8,128)(2,1)S(1)}, u32[]{:S(2)}, u32[]{:S(2)}) collective-permute-start(bf16[128,128]{1,0:T(8,128)(2,1)S(1)} %shard_map.103), channel_id=1, source_target_pairs={{0,12},{4,0},{8,4},{12,8},{1,13},{5,1},{9,5},{13,9},{2,14},{6,2},{... | collective-permute-start | bytes 98312 | tf_op jit(solution)/shard_map/ppermute | solution.py:382
  32.1 5.8 %collective-permute-start.12 = (bf16[128,128]{1,0:T(8,128)(2,1)S(1)}, bf16[128,128]{1,0:T(8,128)(2,1)S(1)}, u32[]{:S(2)}, u32[]{:S(2)}) collective-permute-start(bf16[128,128]{1,0:T(8,128)(2,1)S(1)} %shard_map.104), channel_id=1, source_target_pairs={{0,4},{4,8},{8,12},{12,0},{1,5},{5,9},{9,13},{13,1},{2,6},{6,10},{... | collective-permute-start | bytes 98312 | tf_op jit(solution)/shard_map/ppermute | solution.py:382
  34.6 5.2 %collective-permute-start.14 = (bf16[128,128]{1,0:T(8,128)(2,1)S(1)}, bf16[128,128]{1,0:T(8,128)(2,1)S(1)}, u32[]{:S(2)}, u32[]{:S(2)}) collective-permute-start(bf16[128,128]{1,0:T(8,128)(2,1)S(1)} %shard_map.105), channel_id=1, source_target_pairs={{0,8},{4,12},{8,0},{12,4},{1,9},{5,13},{9,1},{13,5},{2,10},{6,14},... | collective-permute-start | bytes 98312 | tf_op jit(solution)/shard_map/ppermute | solution.py:382
  39.9 1.2 %collective-permute-start.15 = (bf16[64,128]{1,0:T(8,128)(2,1)S(1)}, bf16[64,128]{1,0:T(8,128)(2,1)S(1)}, u32[]{:S(2)}, u32[]{:S(2)}) collective-permute-start(bf16[64,128]{1,0:T(8,128)(2,1)S(1)} %get-tuple-element.30), channel_id=1, source_target_pairs={{0,1},{1,0},{2,3},{3,2},{4,5},{5,4},{6,7},{7,6},{8,9},{9,8},{10,11... | collective-permute-start | bytes 49160 | tf_op jit(solution)/shard_map/ppermute | solution.py:382
